TPU v7x, 512 devices: a whole 4x8x8 slice. The times are simulated.
512 devices in a mesh: tok: 64 (over y, z_lo, x), feat: 8 (over z_hi, core).
Axes of the slice: x: 4, y: 8, z: 8 (z_hi: 4, z_lo: 2; z = z_hi * 2 + z_lo), core: 2. Of those that a mesh axis runs over, the one named last changes fastest.
Arguments:
- hidden_states: bfloat16 [110592, 8192], P('tok', 'feat'), may hold values from -60 to 60
- current_block: float32 [8192, 64], P('feat'), may hold values from -0.0625 to 0.0625
- directions: float32 [8192, 64], P('feat'), may hold values from -0.0625 to 0.0625
Outputs:
- block_image: float32 [8192, 192], P('feat')
- gram_image: float32 [192, 192], replicated
- gram_search: float32 [192, 192], replicated
All inputs are finite; a program needn't handle non-finite values.
Results may differ from a plain program's by a relative error of at most 0.005.
Values may be sent and summed in bfloat16 or wider, within the bound.
No kernel may reach another device: no remote copies, remote signals or barrier semaphores. Data moves between devices by JAX's collectives and lax.ppermute only.
A program may use at most 64 MiB of HBM per device.

v0:
```python
import math

import jax
import jax.numpy as jnp
from jax import lax
from jax.sharding import PartitionSpec as P

LAG = 256


def extended(value, sides, width):
    for axis, dim in sides:
        count, length = (lax.axis_size(axis), value.shape[dim])
        up = [(i, (i + 1) % count) for i in range(count - 1)]
        down = [(j, i) for i, j in up]
        last = lax.slice_in_dim(value, length - width, length, axis=dim)
        initial = lax.slice_in_dim(value, 0, width, axis=dim)
        before = lax.ppermute(last, axis, up)
        after = lax.ppermute(initial, axis, down)
        value = jnp.concatenate([before, value, after], axis=dim)
    return value


def local(hidden_states, current_block, directions):
    highest = lax.Precision.HIGHEST
    tok_count = hidden_states.shape[0]
    block_cols = current_block.shape[1]
    tokens_all = tok_count * lax.axis_size("tok")
    factor = 0.5 / math.sqrt(tokens_all - LAG)

    def project(vectors):
        partial_value = jnp.dot(hidden_states, vectors, preferred_element_type=jnp.float32)
        projected = lax.psum(partial_value, "feat")
        padded = extended(projected, (("tok", 0),), LAG)
        lagged = (padded[2 * LAG : 2 * LAG + tok_count] + padded[:tok_count]).astype(jnp.bfloat16)
        backward = lax.dot_general(
            hidden_states, lagged, (((0,), (0,)), ((), ())), preferred_element_type=jnp.float32
        )
        return lax.psum(backward, "tok") * factor

    def totals(values):
        return lax.psum(values, "feat")

    image_x = project(current_block.astype(jnp.bfloat16))
    rayleigh = totals(jnp.dot(current_block.T, image_x, precision=highest))
    residual = image_x - jnp.dot(current_block, rayleigh, precision=highest)
    lengths = totals(jnp.sum(residual * residual, axis=0, keepdims=True))
    unit_residual = residual * lax.rsqrt(lengths + 1e-06)
    residual_half = unit_residual.astype(jnp.bfloat16)
    trailing = project(jnp.concatenate([residual_half, directions.astype(jnp.bfloat16)], axis=1))
    image_r = trailing[:, :block_cols]
    image_p = trailing[:, block_cols:]
    image_local = jnp.concatenate([image_x, image_r, image_p], axis=1)
    search = jnp.concatenate([current_block, unit_residual, directions], axis=1)
    gram_image, gram_search = totals(
        (
            jnp.dot(search.T, image_local, precision=highest),
            jnp.dot(search.T, search, precision=highest),
        )
    )
    return (image_local, gram_image, gram_search)


def solution(mesh):
    return jax.shard_map(
        local,
        mesh=mesh,
        in_specs=(P("tok", "feat"), P("feat", None), P("feat", None)),
        out_specs=(P("feat", None), P(), P()),
        check_vma=False,
    )
```

profile of v0, /device:TPU:6, one launch (start us, length us, event | category | flops | bytes accessed | tf_op | source)
XLA Modules:
  0.0 1517.4 jit_solution(5912813304142426680)
XLA Ops:
  7.2 0.0 copy-start
  7.2 0.0 all-reduce.7.cloned.1.call-start
  7.2 1.9 copy-done
  9.2 2.9 fusion.12
  12.1 0.0 all-reduce.7.cloned.1.call-update
  12.1 0.0 all-reduce.9.cloned.1.call-start
  12.1 84.4 %all-reduce.7.cloned.1.call-done = f32[1728,64]{0,1:T(8,128)} async-done(((f32[1728,64]{0,1:T(8,128)}), f32[1728,64]{0,1:T(8,128)}) %all-reduce.7.cloned.1.call-update) | async-done | bytes 442384 | tf_op jit(solution)/shard_map/psum | solution.py:33
  96.6 1.0 fusion.21
  97.6 2.8 collective-permute-start
  100.3 5.2 collective-permute-start.1
  105.5 0.3 collective-permute-done
  105.8 1.6 collective-permute-done.1
  107.4 2.6 convolution_bitcast_fusion.3
  110.0 0.0 all-reduce.9.cloned.1.call-update
  110.0 0.0 all-reduce.11.cloned.1.call-start
  110.0 1.6 convert_element_type.18
  111.7 554.6 %all-reduce.9.cloned.1.call-done = f32[1024,64]{0,1:T(8,128)} async-done(((f32[1024,64]{0,1:T(8,128)}), f32[1024,64]{0,1:T(8,128)}) %all-reduce.9.cloned.1.call-update) | async-done | bytes 262160 | tf_op jit(solution)/shard_map/psum | solution.py:39
  666.3 2.0 convolution_bitcast_fusion.4
  668.3 28.3 %psum.58 = f32[64,64]{0,1:T(8,128)} all-reduce(f32[64,64]{0,1:T(8,128)} %convolution_bitcast_fusion.4), channel_id=1, replica_groups=mesh['tok'=64,'feat'=8] {'feat'}, use_global_device_ids=true, to_apply=%region_2.0 | all-reduce | flops 4096 | bytes 32768 | tf_op jit(solution)/shard_map/psum | solution.py:42
  696.7 2.2 multiply_reduce_fusion
  698.9 14.2 psum.59
  713.1 1.8 fusion.19
  714.9 3.0 convolution_bitcast_fusion
  717.8 0.0 all-reduce.11.cloned.1.call-update
  717.8 0.0 all-reduce.13.cloned.1.call-start
  717.9 82.9 %all-reduce.11.cloned.1.call-done = f32[1728,128]{1,0:T(8,128)} async-done(((f32[1728,128]{1,0:T(8,128)}), f32[1728,128]{1,0:T(8,128)}) %all-reduce.11.cloned.1.call-update) | async-done | bytes 884752 | tf_op jit(solution)/shard_map/psum | solution.py:33
  800.8 1.0 fusion.20
  801.8 2.8 collective-permute-start.2
  804.5 5.2 collective-permute-start.3
  809.7 1.0 collective-permute-done.2
  810.7 1.5 collective-permute-done.3
  812.2 2.8 convolution_bitcast_fusion.1
  815.1 0.0 all-reduce.13.cloned.1.call-update
  815.1 0.0 all-reduce.15.cloned.1.call-start
  815.1 2.9 fusion.3
  818.0 1.7 broadcast_multiply_fusion.2
  819.7 599.8 %all-reduce.13.cloned.1.call-done = f32[1024,128]{0,1:T(8,128)} async-done(((f32[1024,128]{0,1:T(8,128)}), f32[1024,128]{0,1:T(8,128)}) %all-reduce.13.cloned.1.call-update) | async-done | bytes 524304 | tf_op jit(solution)/shard_map/psum | solution.py:39
  1419.5 1.1 broadcast_multiply_fusion
  1420.6 1.0 pad_maximum_fusion.2
  1421.7 0.0 copy-start.1
  1421.7 0.9 copy-done.1
  1422.5 2.6 fusion.4
  1425.1 0.0 all-reduce.15.cloned.1.call-update
  1425.2 82.5 %all-reduce.15.cloned.1.call-done = (f32[192,192]{1,0:T(8,128)}, f32[192,192]{1,0:T(8,128)}) async-done(((f32[192,192]{1,0:T(8,128)}, f32[192,192]{1,0:T(8,128)}), (f32[192,192]{1,0:T(8,128)}, f32[192,192]{1,0:T(8,128)})) %all-reduce.15.cloned.1.call-update) | async-done | bytes 294928 | tf_op jit(solution)/shard_map/psum | solution.py:42
  1507.6 1.6 copy.12
  1509.2 1.6 copy.13
  (1 shorter events, 0.0 us)
Async XLA Ops:
  7.2 2.0 copy-start
  7.2 89.4 %all-reduce.7.cloned.1.call-start = ((), (), s32[]{:S(2)}) async-start(), calls=%async_computation | async-start | bytes 917504 | tf_op jit(solution)/shard_map/psum | solution.py:33
  12.1 654.2 %all-reduce.9.cloned.1.call-start = ((), (), s32[]{:S(2)}) async-start(), calls=%async_computation.1 | async-start | bytes 524288 | tf_op jit(solution)/shard_map/psum | solution.py:39
  97.6 8.3 collective-permute-start
  100.3 7.1 collective-permute-start.1
  110.0 690.8 %all-reduce.11.cloned.1.call-start = ((), (), s32[]{:S(2)}) async-start(), calls=%async_computation.2 | async-start | bytes 1769472 | tf_op jit(solution)/shard_map/psum | solution.py:33
  717.8 701.7 %all-reduce.13.cloned.1.call-start = ((), (), s32[]{:S(2)}) async-start(), calls=%async_computation.3 | async-start | bytes 1048576 | tf_op jit(solution)/shard_map/psum | solution.py:39
  801.8 9.0 collective-permute-start.2
  804.5 7.7 collective-permute-start.3
  815.1 692.5 %all-reduce.15.cloned.1.call-start = ((), (), s32[]{:S(2)}) async-start(), calls=%async_computation.4 | async-start | bytes 786432 | tf_op jit(solution)/shard_map/psum | solution.py:42
  1421.7 0.9 copy-start.1
Sparse Core Ops, SparseCore 0:
  12.2 84.2 all-reduce.6
  110.1 556.1 all-reduce.8
  718.0 82.7 all-reduce.10
  815.2 604.2 all-reduce.12
  1425.3 82.2 all-reduce.14
where the time goes:
time: 1520 us
  waiting for transfers between devices  1410 us (93%)
  blocking collectives  42.6 us (3%)
  matrix products  20.9 us (1%)
  starting transfers between devices  16.1 us (1%)
    psum x2, waiting for transfers between devices, project(): return lax.psum(backward, 'tok') * factor  1150 us
    psum x2, waiting for transfers between devices, project(): projected = lax.psum(partial_value, 'feat')  167 us
    psum x1, waiting for transfers between devices, totals(): return lax.psum(values, 'feat')  82.5 us
    psum x2, blocking collectives, totals(): return lax.psum(values, 'feat')  42.6 us
  transfers between devices with their start and end apart: 9, of which 9 were waited for; matrix products, arithmetic and copies ran while one was open for 0% of the time, Pallas kernels for 0%

commit v1 on v0

v1 whole, which is shorter than its diff:
```python
import math

import jax
import jax.numpy as jnp
from jax import lax
from jax.sharding import PartitionSpec as P

LAG = 256
SMALL = 2.0**-20
HIGHEST = lax.Precision.HIGHEST


def exchange(value, axis):
    return lax.all_to_all(value, axis, 0, 0, tiled=True)


def scattered_sum(value, axis):
    return jnp.sum(exchange(value, axis).astype(jnp.float32), axis=0)


def gathered(value, axis):
    return exchange(jnp.broadcast_to(value, (lax.axis_size(axis),) + value.shape), axis)


def rows_dot(a, b, **kwargs):
    return lax.dot_general(a, b, (((1,), (1,)), ((), ())), preferred_element_type=jnp.float32, **kwargs)


def local(hidden_states, current_block, directions):
    tokens, features = hidden_states.shape
    cols = current_block.shape[1]
    feat, tok = lax.axis_size("feat"), lax.axis_size("tok")
    factor = 0.5 / math.sqrt(tokens * tok - LAG)
    half = jnp.bfloat16

    up = [(i, i + 1) for i in range(tok - 1)]
    down = [(i + 1, i) for i in range(tok - 1)]
    behind = lax.ppermute(hidden_states[tokens - LAG :], "tok", up)
    ahead = lax.ppermute(hidden_states[:LAG], "tok", down)
    x, p = current_block.T, directions.T

    def project(vectors):
        pieces = [rows_dot(vectors, part) for part in (behind, hidden_states, ahead)]
        return jnp.concatenate(pieces, axis=1)

    def lagged(projected):
        return projected[:, 2 * LAG :] + projected[:, : tokens]

    def backward(lagged_rows):
        return lax.dot_general(
            lagged_rows, hidden_states, (((1,), (0,)), ((), ())), preferred_element_type=jnp.float32
        )

    side = lax.psum(
        jnp.concatenate(
            [
                project(p.astype(half)),
                rows_dot(p, jnp.concatenate([x, p]), precision=HIGHEST),
                rows_dot(x, x, precision=HIGHEST),
            ],
            axis=1,
        ),
        "feat",
    )

    part = lagged(project(x.astype(half)))
    own = scattered_sum(part.reshape(feat, cols // feat, tokens), "feat").astype(half)
    lag_x = gathered(own, "feat").reshape(cols, tokens)
    own = scattered_sum(backward(lag_x).reshape(tok, cols // tok, features), "tok") * factor
    image_x = gathered(own, "tok").reshape(cols, features)

    both = rows_dot(image_x, jnp.concatenate([x, p]), precision=HIGHEST)
    both = jnp.sum(gathered(both, "feat"), axis=0)
    rayleigh_t, image_x_p = both[:, :cols], both[:, cols:]
    residual = (image_x - jnp.dot(rayleigh_t, x, precision=HIGHEST)) * SMALL

    width = tokens + 2 * LAG
    part = jnp.concatenate(
        [
            project(residual.astype(half)),
            rows_dot(residual, jnp.concatenate([x, residual, p]), precision=HIGHEST),
        ],
        axis=1,
    )
    own = scattered_sum(part.reshape(feat, cols // feat, part.shape[1]), "feat")
    high = own.astype(half)
    low = (own[:, width:] - high[:, width:].astype(jnp.float32)).astype(half)
    everything = gathered(jnp.concatenate([high, low], axis=1), "feat").reshape(cols, -1)
    proj_r = everything[:, :width]
    inner = everything[:, width:].astype(jnp.float32)
    inner = inner[:, : 3 * cols] + inner[:, 3 * cols :]
    r_x, r_r, r_p = (inner[:, i * cols : (i + 1) * cols] for i in range(3))

    proj_p = side[:, :width]
    lag_r = lagged(proj_r.astype(jnp.float32)).astype(half)
    lag_p = lagged(proj_p).astype(half)
    mid_r = proj_r[:, LAG : LAG + tokens]
    mid_p = proj_p[:, LAG : LAG + tokens].astype(half)
    image = backward(jnp.concatenate([lag_r, lag_p]))
    cross = rows_dot(jnp.concatenate([mid_r, mid_p]), jnp.concatenate([lag_r, lag_p]))
    part = jnp.concatenate(
        [
            image[:cols].reshape(tok, -1),
            image[cols:].reshape(tok, -1),
            cross[:cols, :cols].reshape(tok, -1),
            cross[cols:, :cols].reshape(tok, -1),
            cross[cols:, cols:].reshape(tok, -1),
        ],
        axis=1,
    )
    own = scattered_sum(part[:, None, :], "tok") * factor
    total = gathered(own, "tok")[:, 0, :]
    sizes = [cols * features // tok] * 2 + [cols * cols // tok] * 3
    ends = [sum(sizes[: i + 1]) for i in range(5)]
    image_r, image_p = (total[:, e - s : e].reshape(cols, features) for e, s in zip(ends[:2], sizes[:2]))
    c_rr, c_pr, c_pp = (total[:, e - s : e].reshape(cols, cols) for e, s in zip(ends[2:], sizes[2:]))

    lengths = jnp.sum(r_r * jnp.eye(cols, dtype=jnp.float32), axis=1, keepdims=True)
    scale = lax.rsqrt(lengths * (1.0 / SMALL**2) + 1e-06) * (1.0 / SMALL)
    across = scale.T

    block_image = jnp.concatenate([image_x, image_r * scale, image_p])
    u_x, u_p = r_x * scale, r_p * scale
    u_u = r_r * scale * across
    u_image_x = (r_r * (1.0 / SMALL) + jnp.dot(r_x, rayleigh_t.T, precision=HIGHEST)) * scale
    p_image_u = c_pr * across
    gram_image = jnp.concatenate(
        [
            jnp.concatenate([rayleigh_t.T, u_image_x.T, image_x_p], axis=1),
            jnp.concatenate([u_image_x, c_rr * scale * across, p_image_u.T], axis=1),
            jnp.concatenate([image_x_p.T, p_image_u, c_pp], axis=1),
        ]
    )
    p_x, p_p, x_x = (side[:, width + i * cols : width + (i + 1) * cols] for i in range(3))
    gram_search = jnp.concatenate(
        [
            jnp.concatenate([x_x, u_x.T, p_x.T], axis=1),
            jnp.concatenate([u_x, u_u, u_p], axis=1),
            jnp.concatenate([p_x, u_p.T, p_p], axis=1),
        ]
    )
    return (block_image.T, gram_image, gram_search)


def solution(mesh):
    return jax.shard_map(
        local,
        mesh=mesh,
        in_specs=(P("tok", "feat"), P("feat", None), P("feat", None)),
        out_specs=(P("feat", None), P(), P()),
        check_vma=False,
    )
```

time: 1520 us -> 325 us (0.21)
  waiting for transfers between devices: 1410 us -> 106 us
  blocking collectives: 42.6 us -> 122 us
    psum x5 -> x1, waiting for transfers between devices: 1400 us -> 66.1 us  [local(): lax.psum(jnp.concatenate([project(p.astype(half)), rows_dot(p, jnp.concat...]
    all_to_all x0 -> x6, blocking collectives: none -> 122 us  [exchange(): return lax.all_to_all(value, axis, 0, 0, tiled=True)]
    psum x2 -> x0, blocking collectives: 42.6 us -> none  [totals(): return lax.psum(values, 'feat')]
    all_to_all x0 -> x3, waiting for transfers between devices: none -> 27.7 us  [exchange(): return lax.all_to_all(value, axis, 0, 0, tiled=True)]
  transfers between devices with their start and end apart: 9 -> 6, of which waited for: 9 -> 5; matrix products, arithmetic and copies ran while one was open for 0% -> 7% of each run, Pallas kernels for 0% -> 0%
where the time goes in v1:
time: 325 us; the launch traced here: 323 us
  blocking collectives  122 us (38%)
  waiting for transfers between devices  106 us (33%)
  matrix products  24.1 us (7%)
  starting transfers between devices  21.1 us (6%)
  local copies, waits for them, and re-layouts  20.5 us (6%)
  other arithmetic  15.5 us (5%)
  between operations  14.4 us (4%)
    all_to_all x6, blocking collectives, exchange(): return lax.all_to_all(value, axis, 0, 0, tiled=True)  122 us
    psum x1, waiting for transfers between devices, local(): lax.psum(jnp.concatenate([project(p.astype(half)), rows_dot(p, jnp.concat...  66.1 us
    all_to_all x3, waiting for transfers between devices, exchange(): return lax.all_to_all(value, axis, 0, 0, tiled=True)  27.7 us
    dot_general x14, matrix products, rows_dot(): lax.dot_general(a, b, (((1,), (1,)), ((), ())), preferred_element_type=jn...  19.6 us
    all_to_all x3, starting transfers between devices, exchange(): return lax.all_to_all(value, axis, 0, 0, tiled=True)  14.9 us
    unnamed x47, local copies, waits for them, and re-layouts  6.63 us
  transfers between devices with their start and end apart: 6, of which 5 were waited for; matrix products, arithmetic and copies ran while one was open for 7% of the time, Pallas kernels for 0%

profile of v1, /device:TPU:6, one launch (start us, length us, event | category | flops | bytes accessed | tf_op | source)
XLA Modules:
  0.0 323.3 jit_solution(342067930068575905)
XLA Ops:
  7.2 1.3 fusion.44
  8.5 4.2 %collective-permute-start.1 = (bf16[256,1024]{1,0:T(8,128)(2,1)S(1)}, bf16[256,1024]{1,0:T(8,128)(2,1)S(1)}, u32[]{:S(2)}, u32[]{:S(2)}) collective-permute-start(bf16[256,1024]{1,0:T(8,128)(2,1)S(1)} %get-tuple-element.16), channel_id=1, source_target_pairs={{0,8},{8,16},{16,24},{24,32},{32,40},{40,48},{48,56},{56,64},{64,7... | collective-permute-start | bytes 1572872 | tf_op jit(solution)/shard_map/ppermute | solution.py:38
  12.7 1.9 collective-permute-start
  14.6 3.2 fusion.49
  17.8 6.2 %collective-permute-done.1 = bf16[256,1024]{1,0:T(8,128)(2,1)S(1)} collective-permute-done((bf16[256,1024]{1,0:T(8,128)(2,1)S(1)}, bf16[256,1024]{1,0:T(8,128)(2,1)S(1)}, u32[]{:S(2)}, u32[]{:S(2)}) %collective-permute-start.1) | collective-permute-done | bytes 524320 | tf_op jit(solution)/shard_map/ppermute | solution.py:38
  24.3 5.7 %collective-permute-done = bf16[256,1024]{1,0:T(8,128)(2,1)S(1)} collective-permute-done((bf16[256,1024]{1,0:T(8,128)(2,1)S(1)}, bf16[256,1024]{1,0:T(8,128)(2,1)S(1)}, u32[]{:S(2)}, u32[]{:S(2)}) %collective-permute-start) | collective-permute-done | bytes 524320 | tf_op jit(solution)/shard_map/ppermute | solution.py:39
  31.0 26.4 %all_to_all.45 = f32[8,8,1728]{2,1,0:T(8,128)} all-to-all(f32[8,8,1728]{2,1,0:T(8,128)S(1)} %fusion.12), channel_id=1, replica_groups=mesh['tok'=64,'feat'=8] {'feat'}, dimensions={0} | all-to-all | bytes 884736 | tf_op jit(solution)/shard_map/all_to_all | solution.py:14
  57.4 1.7 reduce_sum.54
  59.8 14.0 %all_to_all.46 = bf16[8,8,1728]{2,1,0:T(8,128)(2,1)S(1)} all-to-all(bf16[8,8,1728]{2,1,0:T(8,128)(2,1)S(1)} %broadcast_in_dim.19), channel_id=1, replica_groups=mesh['tok'=64,'feat'=8] {'feat'}, dimensions={0} | all-to-all | bytes 442368 | tf_op jit(solution)/shard_map/all_to_all | solution.py:14
  74.9 21.6 %all_to_all.47 = f32[64,1,1024]{2,1,0:T(1,128)} all-to-all(f32[64,1,1024]{2,1,0:T(1,128)S(1)} %copy.65), channel_id=1, replica_groups=mesh['tok'=64,'feat'=8] {'tok'}, dimensions={0} | all-to-all | bytes 524288 | tf_op jit(solution)/shard_map/all_to_all | solution.py:14
  96.5 1.1 reduce_sum.55
  97.8 16.3 %all_to_all.48 = f32[64,1,1024]{2,1,0:T(1,128)S(1)} all-to-all(f32[64,1,1024]{2,1,0:T(1,128)S(1)} %broadcast_in_dim.20), channel_id=1, replica_groups=mesh['tok'=64,'feat'=8] {'tok'}, dimensions={0} | all-to-all | bytes 524288 | tf_op jit(solution)/shard_map/all_to_all | solution.py:14
  114.8 1.7 fusion.17
  116.5 15.2 %all_to_all.49 = f32[8,64,128]{2,1,0:T(8,128)} all-to-all(f32[8,64,128]{2,1,0:T(8,128)S(1)} %broadcast_in_dim.21), channel_id=1, replica_groups=mesh['tok'=64,'feat'=8] {'feat'}, dimensions={0} | all-to-all | bytes 524288 | tf_op jit(solution)/shard_map/all_to_all | solution.py:14
  131.7 1.6 reduce_sum.56
  133.3 1.4 fusion
  134.7 2.0 fusion.32
  136.7 1.5 fusion.5
  138.2 0.9 fusion.34
  139.1 0.9 fusion.30
  140.1 2.0 concatenate.65
  142.0 4.2 %all-to-all-start.5 = ((f32[8,8,2432]{2,1,0:T(8,128)}), f32[8,8,2432]{2,1,0:T(8,128)}, u32[]{:S(2)}, u32[]{:S(2)}) async-start(f32[8,8,2432]{2,1,0:T(8,128)} %bitcast.123), calls=%async_computation.5 | async-start | bytes 1245184 | tf_op jit(solution)/shard_map/all_to_all | solution.py:14
  146.3 2.1 convolution_dynamic-update-slice_fusion.2
  148.3 3.0 convolution_dynamic-update-slice_fusion
  151.4 0.9 convolution_dynamic-update-slice_fusion.1
  152.3 1.2 fusion.1
  153.5 1.0 convolution_dynamic-update-slice_fusion.3
  154.5 12.1 %all-to-all-done.5 = f32[8,8,2432]{2,1,0:T(8,128)} async-done(((f32[8,8,2432]{2,1,0:T(8,128)}), f32[8,8,2432]{2,1,0:T(8,128)}, u32[]{:S(2)}, u32[]{:S(2)}) %all-to-all-start.5) | async-done | bytes 622624 | tf_op jit(solution)/shard_map/all_to_all | solution.py:14
  166.6 1.7 reduce_sum.57
  168.3 0.9 convert_element_type.38
  170.8 4.3 %all-to-all-start.6 = ((bf16[8,8,2624]{2,1,0:T(8,128)(2,1)}), bf16[8,8,2624]{2,1,0:T(8,128)(2,1)}, u32[]{:S(2)}, u32[]{:S(2)}) async-start(bf16[8,8,2624]{2,1,0:T(8,128)(2,1)} %broadcast_in_dim.22), calls=%async_computation.6 | async-start | bytes 688128 | tf_op jit(solution)/shard_map/all_to_all | solution.py:14
  175.0 66.1 %all-reduce.2.cloned.1.call-done = f32[64,2432]{0,1:T(8,128)} async-done(((f32[64,2432]{0,1:T(8,128)}), f32[64,2432]{0,1:T(8,128)}) %all-reduce.2.cloned.1.call-update) | async-done | bytes 622608 | tf_op jit(solution)/shard_map/psum | solution.py:54
  241.1 2.0 slice.200
  243.1 2.3 fusion.3
  245.4 1.7 slice.145
  247.1 1.7 slice.152
  248.7 2.0 copy.96
  250.7 1.1 convert_element_type.41
  251.9 0.8 fusion.4
  252.7 1.9 copy.97
  254.7 2.2 fusion.19
  258.4 28.3 %all_to_all.50 = f32[64,1,2240]{2,1,0:T(1,128)S(1)} all-to-all(f32[64,1,2240]{2,1,0:T(1,128)S(1)} %copy.74), channel_id=1, replica_groups=mesh['tok'=64,'feat'=8] {'tok'}, dimensions={0} | all-to-all | bytes 1146880 | tf_op jit(solution)/shard_map/all_to_all | solution.py:14
  287.1 1.1 broadcast_in_dim.24
  288.2 6.5 %all-to-all-start.8 = ((f32[64,1,2240]{2,1,0:T(1,128)}), f32[64,1,2240]{2,1,0:T(1,128)S(1)}, u32[]{:S(2)}, u32[]{:S(2)}) async-start(f32[64,1,2240]{2,1,0:T(1,128)} %broadcast_in_dim.24), calls=%async_computation.8 | async-start | bytes 1179648 | tf_op jit(solution)/shard_map/all_to_all | solution.py:14
  295.0 0.9 slice.157
  296.4 15.6 %all-to-all-done.8 = f32[64,1,2240]{2,1,0:T(1,128)S(1)} async-done(((f32[64,1,2240]{2,1,0:T(1,128)}), f32[64,1,2240]{2,1,0:T(1,128)S(1)}, u32[]{:S(2)}, u32[]{:S(2)}) %all-to-all-start.8) | async-done | bytes 573472 | tf_op jit(solution)/shard_map/all_to_all | solution.py:14
  312.4 0.9 slice_multiply_fusion.2
  314.7 0.9 maximum_bitcast_fusion
  (84 shorter events, 10.6 us)
Async XLA Ops:
  7.2 7.5 %copy-start.1 = (f32[1024,64]{0,1:T(8,128)S(1)}, f32[1024,64]{0,1:T(8,128)}, u32[]{:S(2)}) copy-start(f32[1024,64]{0,1:T(8,128)} %param.4) | copy-start | bytes 786436
  8.5 15.6 %collective-permute-start.1 = (bf16[256,1024]{1,0:T(8,128)(2,1)S(1)}, bf16[256,1024]{1,0:T(8,128)(2,1)S(1)}, u32[]{:S(2)}, u32[]{:S(2)}) collective-permute-start(bf16[256,1024]{1,0:T(8,128)(2,1)S(1)} %get-tuple-element.16), channel_id=1, source_target_pairs={{0,8},{8,16},{16,24},{24,32},{32,40},{40,48},{48,56},{56,64},{64,7... | collective-permute-start | bytes 1572872 | tf_op jit(solution)/shard_map/ppermute | solution.py:38
  12.7 17.4 %collective-permute-start = (bf16[256,1024]{1,0:T(8,128)(2,1)S(1)}, bf16[256,1024]{1,0:T(8,128)(2,1)S(1)}, u32[]{:S(2)}, u32[]{:S(2)}) collective-permute-start(bf16[256,1024]{1,0:T(8,128)(2,1)S(1)} %get-tuple-element.15), channel_id=1, source_target_pairs={{8,0},{16,8},{24,16},{32,24},{40,32},{48,40},{56,48},{64,56},{72,6... | collective-permute-start | bytes 1572872 | tf_op jit(solution)/shard_map/ppermute | solution.py:39
  24.0 6.9 %copy-start.6 = (bf16[256,1024]{1,0:T(8,128)(2,1)}, bf16[256,1024]{1,0:T(8,128)(2,1)S(1)}, u32[]{:S(2)}) copy-start(bf16[256,1024]{1,0:T(8,128)(2,1)S(1)} %collective-permute-done.1) | copy-start | bytes 1572868
  30.1 0.8 copy-start.8
  30.1 43.8 %copy-start = (bf16[1728,1024]{1,0:T(8,128)(2,1)S(1)}, bf16[1728,1024]{1,0:T(8,128)(2,1)}, u32[]{:S(2)}) copy-start(bf16[1728,1024]{1,0:T(8,128)(2,1)} %param.3) | copy-start | bytes 10616836
  114.1 0.7 copy-start.11
  134.7 2.0 copy-start.2
  134.7 2.0 copy-start.4
  136.7 1.5 copy-start.7
  136.7 2.4 copy-start.9
  142.0 24.6 %all-to-all-start.5 = ((f32[8,8,2432]{2,1,0:T(8,128)}), f32[8,8,2432]{2,1,0:T(8,128)}, u32[]{:S(2)}, u32[]{:S(2)}) async-start(f32[8,8,2432]{2,1,0:T(8,128)} %bitcast.123), calls=%async_computation.5 | async-start | bytes 1245184 | tf_op jit(solution)/shard_map/all_to_all | solution.py:14
  146.2 94.9 %all-reduce.2.cloned.1.call-start = ((), (), s32[]{:S(2)}) async-start(), calls=%async_computation.9 | async-start | bytes 2490368 | tf_op jit(solution)/shard_map/psum | solution.py:54
  148.3 3.0 copy-start.5
  148.3 3.0 copy-start.10
  148.3 4.0 %copy-start.3 = (f32[1024,64]{0,1:T(8,128)S(1)}, f32[1024,64]{0,1:T(8,128)}, u32[]{:S(2)}) copy-start(f32[1024,64]{0,1:T(8,128)} %param.4) | copy-start | bytes 786436
  170.8 74.6 %all-to-all-start.6 = ((bf16[8,8,2624]{2,1,0:T(8,128)(2,1)}), bf16[8,8,2624]{2,1,0:T(8,128)(2,1)}, u32[]{:S(2)}, u32[]{:S(2)}) async-start(bf16[8,8,2624]{2,1,0:T(8,128)(2,1)} %broadcast_in_dim.22), calls=%async_computation.6 | async-start | bytes 688128 | tf_op jit(solution)/shard_map/all_to_all | solution.py:14
  254.7 2.3 copy-start.13
  254.7 2.3 copy-start.14
  254.7 2.3 copy-start.15
  254.7 2.3 copy-start.16
  286.7 8.0 %copy-start.12 = (f32[64,1,1024]{2,1,0:T(1,128)S(1)}, f32[64,1,1024]{2,1,0:T(1,128)}, u32[]{:S(2)}) copy-start(f32[64,1,1024]{2,1,0:T(1,128)} %copy-done.11) | copy-start | bytes 786436
  287.0 7.7 %copy-start.17 = (f32[64,128]{1,0:T(8,128)S(1)}, f32[64,128]{1,0:T(8,128)}, u32[]{:S(2)}) copy-start(f32[64,128]{1,0:T(8,128)} %reduce_sum.56) | copy-start | bytes 98308
  288.2 23.8 %all-to-all-start.8 = ((f32[64,1,2240]{2,1,0:T(1,128)}), f32[64,1,2240]{2,1,0:T(1,128)S(1)}, u32[]{:S(2)}, u32[]{:S(2)}) async-start(f32[64,1,2240]{2,1,0:T(1,128)} %broadcast_in_dim.24), calls=%async_computation.8 | async-start | bytes 1179648 | tf_op jit(solution)/shard_map/all_to_all | solution.py:14
Sparse Core Ops, SparseCore 0:
  154.6 86.4 all-reduce.1

commit v2 on v1

v2 whole, which is shorter than its diff:
```python
import math

import jax
import jax.numpy as jnp
from jax import lax
from jax.sharding import PartitionSpec as P

LAG = 256
SMALL = 2.0**-20
HIGHEST = lax.Precision.HIGHEST


def exchange(value, axis):
    return lax.all_to_all(value, axis, 0, 0, tiled=True)


def scattered_sum(value, axis):
    return jnp.sum(exchange(value, axis).astype(jnp.float32), axis=0)


def gathered(value, axis):
    return exchange(jnp.broadcast_to(value, (lax.axis_size(axis),) + value.shape), axis)


def rows_dot(a, b, **kwargs):
    return lax.dot_general(a, b, (((1,), (1,)), ((), ())), preferred_element_type=jnp.float32, **kwargs)


def pair(value):
    high = value.astype(jnp.bfloat16)
    return jnp.concatenate([high, (value - high.astype(jnp.float32)).astype(jnp.bfloat16)], axis=1)


def joined(value):
    value = value.astype(jnp.float32)
    middle = value.shape[1] // 2
    return value[:, :middle] + value[:, middle:]


def local(hidden_states, current_block, directions):
    tokens, features = hidden_states.shape
    cols = current_block.shape[1]
    feat, tok = lax.axis_size("feat"), lax.axis_size("tok")
    factor = 0.5 / math.sqrt(tokens * tok - LAG)
    half = jnp.bfloat16

    up = [(i, i + 1) for i in range(tok - 1)]
    down = [(i + 1, i) for i in range(tok - 1)]
    behind = lax.ppermute(hidden_states[tokens - LAG :], "tok", up)
    ahead = lax.ppermute(hidden_states[:LAG], "tok", down)
    x, p = current_block.T, directions.T
    width = tokens + 2 * LAG

    def project(vectors):
        pieces = [rows_dot(vectors, part).astype(half) for part in (behind, hidden_states, ahead)]
        return jnp.concatenate(pieces, axis=1)

    def lagged(projected):
        projected = projected.astype(jnp.float32)
        return (projected[:, 2 * LAG :] + projected[:, :tokens]).astype(half)

    def middle(projected):
        return projected[:, LAG : LAG + tokens]

    def backward(lagged_rows):
        return lax.dot_general(
            lagged_rows, hidden_states, (((1,), (0,)), ((), ())), preferred_element_type=jnp.float32
        )

    def inner(a, b):
        return rows_dot(a, b, precision=HIGHEST)

    def times(a, b):
        return jnp.dot(a, b, precision=HIGHEST)

    part = project(jnp.concatenate([x.astype(half), p.astype(half)]))
    zero = jnp.zeros((cols, cols), jnp.float32)
    products = jnp.concatenate(
        [jnp.concatenate([inner(x, x), inner(p, x)]), jnp.concatenate([zero, inner(p, p)])], axis=1
    )
    part = jnp.concatenate([part, pair(products)], axis=1)
    own = scattered_sum(part.reshape(feat, 2 * cols // feat, part.shape[1]), "feat")
    own = jnp.concatenate([own[:, :width].astype(half), pair(joined(own[:, width:]))], axis=1)
    known = gathered(own, "feat").reshape(2 * cols, -1)
    proj_x, proj_p = known[:cols, :width], known[cols:, :width]
    lag_x, lag_p = lagged(proj_x), lagged(proj_p)

    part = jnp.concatenate(
        [backward(lag_x).reshape(tok, -1), rows_dot(lag_x, middle(proj_x)).reshape(tok, -1)], axis=1
    )
    own = scattered_sum(part[:, None, :], "tok") * factor
    total = gathered(own, "tok")[:, 0, :]
    split = cols * features // tok
    image_x = total[:, :split].reshape(cols, features)
    estimate = total[:, split:].reshape(cols, cols)
    residual = (image_x - times(estimate, x)) * SMALL

    part = project(residual.astype(half))
    products = jnp.concatenate(
        [inner(residual, x), inner(residual, p), inner(residual, residual), inner(image_x, x), inner(image_x, p)],
        axis=1,
    )
    part = jnp.concatenate([part, pair(products)], axis=1)
    own = scattered_sum(part.reshape(feat, cols // feat, part.shape[1]), "feat")
    products = joined(own[:, width:])
    first = lax.axis_index("feat") * (cols // feat)
    lacks = (products[:, 3 * cols : 4 * cols] - lax.dynamic_slice_in_dim(estimate, first, cols // feat)) * SMALL
    proj_r = own[:, :width] - jnp.dot(lacks.astype(half), proj_x, preferred_element_type=jnp.float32)
    own = jnp.concatenate([proj_r.astype(half), pair(products)], axis=1)
    found = gathered(own, "feat").reshape(cols, -1)
    proj_r = found[:, :width]
    lag_r = lagged(proj_r)

    part = jnp.concatenate(
        [
            backward(lag_r).astype(half).reshape(tok, -1),
            backward(lag_p).astype(half).reshape(tok, -1),
            pair(rows_dot(middle(proj_r), lag_r).reshape(tok, -1)),
            pair(rows_dot(middle(proj_p), lag_r).reshape(tok, -1)),
            pair(rows_dot(middle(proj_p), lag_p).reshape(tok, -1)),
        ],
        axis=1,
    )
    own = scattered_sum(part[:, None, :], "tok") * factor
    images, own = own[:, : 2 * split].astype(half), own[:, 2 * split :]
    each = cols * cols // tok
    own = [images] + [pair(joined(own[:, 2 * i * each : 2 * (i + 1) * each])) for i in range(3)]
    total = gathered(jnp.concatenate(own, axis=1), "tok")[:, 0, :]
    image_r, image_p = (
        total[:, i * split : (i + 1) * split].reshape(cols, features).astype(jnp.float32) for i in range(2)
    )
    c_rr, c_pr, c_pp = (
        joined(total[:, 2 * (split + i * each) : 2 * (split + (i + 1) * each)]).reshape(cols, cols) for i in range(3)
    )

    products = joined(found[:, width:])
    r_x, r_p, r_r, rayleigh_t, image_x_p = (products[:, i * cols : (i + 1) * cols] for i in range(5))
    products = joined(known[:, width:])
    x_x, p_x, p_p = products[:cols, :cols], products[cols:, :cols], products[cols:, cols:]
    lacks = (rayleigh_t - estimate) * SMALL
    shift = times(lacks, r_x.T)
    r_r = r_r - shift - shift.T + times(times(lacks, x_x), lacks.T)
    r_x = r_x - times(lacks, x_x)
    r_p = r_p - times(lacks, p_x.T)

    lengths = jnp.sum(r_r * jnp.eye(cols, dtype=jnp.float32), axis=1, keepdims=True)
    scale = lax.rsqrt(lengths * (1.0 / SMALL**2) + 1e-06) * (1.0 / SMALL)
    across = scale.T

    block_image = jnp.concatenate([image_x, image_r * scale, image_p])
    u_x, u_p = r_x * scale, r_p * scale
    u_u = r_r * scale * across
    u_image_x = (r_r * (1.0 / SMALL) + times(r_x, rayleigh_t.T)) * scale
    p_image_u = c_pr * across
    gram_image = jnp.concatenate(
        [
            jnp.concatenate([rayleigh_t.T, u_image_x.T, image_x_p], axis=1),
            jnp.concatenate([u_image_x, c_rr * scale * across, p_image_u.T], axis=1),
            jnp.concatenate([image_x_p.T, p_image_u, c_pp], axis=1),
        ]
    )
    gram_search = jnp.concatenate(
        [
            jnp.concatenate([x_x, u_x.T, p_x.T], axis=1),
            jnp.concatenate([u_x, u_u, u_p], axis=1),
            jnp.concatenate([p_x, u_p.T, p_p], axis=1),
        ]
    )
    return (block_image.T, gram_image, gram_search)


def solution(mesh):
    return jax.shard_map(
        local,
        mesh=mesh,
        in_specs=(P("tok", "feat"), P("feat", None), P("feat", None)),
        out_specs=(P("feat", None), P(), P()),
        check_vma=False,
    )
```

time: 325 us -> 260 us (0.80)
  waiting for transfers between devices: 106 us -> 52.1 us
  blocking collectives: 122 us -> 77.5 us
  matrix products: 24.1 us -> 40.7 us
  between operations: 14.4 us -> 1.16 us
  starting transfers between devices: 21.1 us -> 32.6 us
  local copies, waits for them, and re-layouts: 20.5 us -> 31.7 us
  other arithmetic: 15.5 us -> 21.9 us
    psum x1 -> x0, waiting for transfers between devices: 66.1 us -> none  [local(): lax.psum(jnp.concatenate([project(p.astype(half)), rows_dot(p, jnp.concat...]
    all_to_all x6 -> x3, blocking collectives: 122 us -> 77.5 us  [exchange(): return lax.all_to_all(value, axis, 0, 0, tiled=True)]
    all_to_all x3 -> x5, waiting for transfers between devices: 27.7 us -> 49.8 us  [exchange(): return lax.all_to_all(value, axis, 0, 0, tiled=True)]
    dot_general x14 -> x18, matrix products: 19.6 us -> 31.2 us  [rows_dot(): lax.dot_general(a, b, (((1,), (1,)), ((), ())), preferred_element_type=jn...]
    all_to_all x3 -> x5, starting transfers between devices: 14.9 us -> 26.5 us  [exchange(): return lax.all_to_all(value, axis, 0, 0, tiled=True)]
    concatenate x2 -> x8, local copies, waits for them, and re-layouts: 2.04 us -> 9.92 us  [the longest x2 4 us: local(): part = jnp.concatenate([part, pair(products)], axis=1)]
    ppermute x1, waiting for transfers between devices: 5.75 us -> 0.01 us  [local(): ahead = lax.ppermute(hidden_states[:LAG], 'tok', down)]
    ppermute x1, waiting for transfers between devices: 6.22 us -> 2.29 us  [local(): behind = lax.ppermute(hidden_states[tokens - LAG:], 'tok', up)]
  transfers between devices with their start and end apart: 6 -> 7, of which waited for: 5 -> 6; matrix products, arithmetic and copies ran while one was open for 7% -> 12% of each run, Pallas kernels for 0% -> 0%
where the time goes in v2:
time: 260 us; the launch traced here: 258 us
  blocking collectives  77.5 us (30%)
  waiting for transfers between devices  52.1 us (20%)
  matrix products  40.7 us (16%)
  starting transfers between devices  32.6 us (13%)
  local copies, waits for them, and re-layouts  31.7 us (12%)
  other arithmetic  21.9 us (8%)
    all_to_all x3, blocking collectives, exchange(): return lax.all_to_all(value, axis, 0, 0, tiled=True)  77.5 us
    all_to_all x5, waiting for transfers between devices, exchange(): return lax.all_to_all(value, axis, 0, 0, tiled=True)  49.8 us
    dot_general x18, matrix products, rows_dot(): lax.dot_general(a, b, (((1,), (1,)), ((), ())), preferred_element_type=jn...  31.2 us
    all_to_all x5, starting transfers between devices, exchange(): return lax.all_to_all(value, axis, 0, 0, tiled=True)  26.5 us
    unnamed x52, local copies, waits for them, and re-layouts  10.4 us
  transfers between devices with their start and end apart: 7, of which 6 were waited for; matrix products, arithmetic and copies ran while one was open for 12% of the time, Pallas kernels for 0%

profile of v2, /device:TPU:6, one launch (start us, length us, event | category | flops | bytes accessed | tf_op | source)
XLA Modules:
  0.0 257.6 jit_solution(10704994359818292441)
XLA Ops:
  0.6 2.2 fusion.53
  2.9 4.2 %collective-permute-start = (bf16[256,1024]{1,0:T(8,128)(2,1)S(1)}, bf16[256,1024]{1,0:T(8,128)(2,1)S(1)}, u32[]{:S(2)}, u32[]{:S(2)}) collective-permute-start(bf16[256,1024]{1,0:T(8,128)(2,1)S(1)} %get-tuple-element.29), channel_id=1, source_target_pairs={{0,8},{8,16},{16,24},{24,32},{32,40},{40,48},{48,56},{56,64},{64,7... | collective-permute-start | bytes 1572872 | tf_op jit(solution)/shard_map/ppermute | solution.py:49
  7.0 1.9 collective-permute-start.1
  9.0 2.0 fusion.55
  11.0 2.0 fusion.56
  13.0 2.0 fusion.57
  16.1 2.3 collective-permute-done
  20.1 1.6 copy.73
  21.7 1.5 constant_dynamic-update-slice_fusion
  23.3 2.8 %fusion.1 = bf16[128,2496]{0,1:T(8,128)(2,1)} fusion(bf16[128,2496]{0,1:T(8,128)(2,1)} %constant_dynamic-update-slice_fusion, bf16[1728,1024]{1,0:T(8,128)(2,1)S(1)} %copy-done, bf16[64,1024]{1,0:T(8,128)(2,1)} %copy-done.9, bf16[64,1024]{1,0:T(8,128)(2,1)} %copy-done.11), kind=kOutput, calls=%fused_computation.3 | convolution fusion | flops 453730304 | bytes 4243456 | tf_op jit(solution)/shard_map/dot_general | solution.py:26
  26.1 2.0 fusion.3
  29.5 2.2 copy.74
  31.6 31.5 %all_to_all.40 = bf16[8,16,2496]{2,1,0:T(8,128)(2,1)S(1)} all-to-all(bf16[8,16,2496]{2,1,0:T(8,128)(2,1)} %bitcast.81), channel_id=1, replica_groups=mesh['tok'=64,'feat'=8] {'feat'}, dimensions={0} | all-to-all | bytes 1277952 | tf_op jit(solution)/shard_map/all_to_all | solution.py:14
  63.9 1.6 concatenate.70
  66.5 22.9 %all_to_all.41 = bf16[8,16,2496]{2,1,0:T(8,128)(2,1)S(1)} all-to-all(bf16[8,16,2496]{2,1,0:T(8,128)(2,1)S(1)} %broadcast_in_dim.20), channel_id=1, replica_groups=mesh['tok'=64,'feat'=8] {'feat'}, dimensions={0} | all-to-all | bytes 1277952 | tf_op jit(solution)/shard_map/all_to_all | solution.py:14
  91.7 23.0 %all_to_all.42 = f32[64,1,1088]{2,1,0:T(1,128)} all-to-all(f32[64,1,1088]{2,1,0:T(1,128)S(1)} %copy.75), channel_id=1, replica_groups=mesh['tok'=64,'feat'=8] {'tok'}, dimensions={0} | all-to-all | bytes 557056 | tf_op jit(solution)/shard_map/all_to_all | solution.py:14
  116.8 6.2 %all-to-all-start.3 = ((f32[64,1,1088]{2,1,0:T(1,128)}), f32[64,1,1088]{2,1,0:T(1,128)}, u32[]{:S(2)}, u32[]{:S(2)}) async-start(f32[64,1,1088]{2,1,0:T(1,128)} %broadcast_in_dim.22), calls=%async_computation.3 | async-start | bytes 589824 | tf_op jit(solution)/shard_map/all_to_all | solution.py:14
  123.0 1.6 slice_convert_fusion.6
  124.7 9.5 %all-to-all-done.3 = f32[64,1,1088]{2,1,0:T(1,128)} async-done(((f32[64,1,1088]{2,1,0:T(1,128)}), f32[64,1,1088]{2,1,0:T(1,128)}, u32[]{:S(2)}, u32[]{:S(2)}) %all-to-all-start.3) | async-done | bytes 278560 | tf_op jit(solution)/shard_map/all_to_all | solution.py:14
  136.7 2.0 fusion.59
  138.7 1.9 fusion.60
  141.6 1.9 fusion.48
  144.5 1.9 convolution_convert_fusion.1
  146.4 1.5 concatenate.72
  147.9 1.6 subtract_convert_fusion
  149.5 2.0 convolution_convert_fusion.6
  151.5 2.0 convolution_convert_fusion.7
  153.6 1.8 concatenate.73
  155.4 4.1 %all-to-all-start.4 = ((bf16[8,8,2880]{2,1,0:T(8,128)(2,1)}), bf16[8,8,2880]{2,1,0:T(8,128)(2,1)}, u32[]{:S(2)}, u32[]{:S(2)}) async-start(bf16[8,8,2880]{2,1,0:T(8,128)(2,1)} %bitcast.82), calls=%async_computation.4 | async-start | bytes 753664 | tf_op jit(solution)/shard_map/all_to_all | solution.py:14
  159.5 1.5 slice_add_fusion.4
  161.0 1.9 fusion.6
  164.3 9.5 %all-to-all-done.4 = bf16[8,8,2880]{2,1,0:T(8,128)(2,1)} async-done(((bf16[8,8,2880]{2,1,0:T(8,128)(2,1)}), bf16[8,8,2880]{2,1,0:T(8,128)(2,1)}, u32[]{:S(2)}, u32[]{:S(2)}) %all-to-all-start.4) | async-done | bytes 368672 | tf_op jit(solution)/shard_map/all_to_all | solution.py:14
  174.9 1.8 fusion
  176.8 1.5 concatenate.74
  178.2 1.6 broadcast_in_dim.23
  179.8 4.3 %all-to-all-start.5 = ((bf16[8,8,2880]{2,1,0:T(8,128)(2,1)}), bf16[8,8,2880]{2,1,0:T(8,128)(2,1)}, u32[]{:S(2)}, u32[]{:S(2)}) async-start(bf16[8,8,2880]{2,1,0:T(8,128)(2,1)} %broadcast_in_dim.23), calls=%async_computation.5 | async-start | bytes 753664 | tf_op jit(solution)/shard_map/all_to_all | solution.py:14
  184.1 1.5 fusion.54
  185.6 1.5 copy.90
  187.0 1.9 subtract_convert_fusion.2
  188.9 2.3 convolution_convert_fusion.2
  192.0 7.0 %all-to-all-done.5 = bf16[8,8,2880]{2,1,0:T(8,128)(2,1)} async-done(((bf16[8,8,2880]{2,1,0:T(8,128)(2,1)}), bf16[8,8,2880]{2,1,0:T(8,128)(2,1)}, u32[]{:S(2)}, u32[]{:S(2)}) %all-to-all-start.5) | async-done | bytes 368672 | tf_op jit(solution)/shard_map/all_to_all | solution.py:14
  201.0 1.8 subtract_convert_fusion.3
  202.7 1.8 subtract_convert_fusion.4
  210.3 6.2 %all-to-all-start.6 = ((bf16[64,2,1216]{2,1,0:T(2,128)(2,1)}), bf16[64,2,1216]{2,1,0:T(2,128)(2,1)S(1)}, u32[]{:S(2)}, u32[]{:S(2)}) async-start(bf16[64,2,1216]{2,1,0:T(2,128)(2,1)} %reshape.57), calls=%async_computation.6 | async-start | bytes 655360 | tf_op jit(solution)/shard_map/all_to_all | solution.py:14
  218.0 11.6 %all-to-all-done.6 = bf16[64,2,1216]{2,1,0:T(2,128)(2,1)S(1)} async-done(((bf16[64,2,1216]{2,1,0:T(2,128)(2,1)}), bf16[64,2,1216]{2,1,0:T(2,128)(2,1)S(1)}, u32[]{:S(2)}, u32[]{:S(2)}) %all-to-all-start.6) | async-done | bytes 311328 | tf_op jit(solution)/shard_map/all_to_all | solution.py:14
  231.3 2.5 reduce.4
  234.8 5.8 %all-to-all-start.7 = ((bf16[64,2,1216]{2,1,0:T(2,128)(2,1)}), bf16[64,2,1216]{2,1,0:T(2,128)(2,1)S(1)}, u32[]{:S(2)}, u32[]{:S(2)}) async-start(bf16[64,2,1216]{2,1,0:T(2,128)(2,1)} %reshape.59), calls=%async_computation.7 | async-start | bytes 655360 | tf_op jit(solution)/shard_map/all_to_all | solution.py:14
  241.2 12.2 %all-to-all-done.7 = bf16[64,2,1216]{2,1,0:T(2,128)(2,1)S(1)} async-done(((bf16[64,2,1216]{2,1,0:T(2,128)(2,1)}), bf16[64,2,1216]{2,1,0:T(2,128)(2,1)S(1)}, u32[]{:S(2)}, u32[]{:S(2)}) %all-to-all-start.7) | async-done | bytes 311328 | tf_op jit(solution)/shard_map/all_to_all | solution.py:14
  (116 shorter events, 34.5 us)
Async XLA Ops:
  0.6 22.6 %copy-start = (bf16[1728,1024]{1,0:T(8,128)(2,1)S(1)}, bf16[1728,1024]{1,0:T(8,128)(2,1)}, u32[]{:S(2)}) copy-start(bf16[1728,1024]{1,0:T(8,128)(2,1)} %param.3) | copy-start | bytes 10616836
  2.9 15.5 %collective-permute-start = (bf16[256,1024]{1,0:T(8,128)(2,1)S(1)}, bf16[256,1024]{1,0:T(8,128)(2,1)S(1)}, u32[]{:S(2)}, u32[]{:S(2)}) collective-permute-start(bf16[256,1024]{1,0:T(8,128)(2,1)S(1)} %get-tuple-element.29), channel_id=1, source_target_pairs={{0,8},{8,16},{16,24},{24,32},{32,40},{40,48},{48,56},{56,64},{64,7... | collective-permute-start | bytes 1572872 | tf_op jit(solution)/shard_map/ppermute | solution.py:49
  7.0 19.0 %collective-permute-start.1 = (bf16[256,1024]{1,0:T(8,128)(2,1)}, bf16[256,1024]{1,0:T(8,128)(2,1)}, u32[]{:S(2)}, u32[]{:S(2)}) collective-permute-start(bf16[256,1024]{1,0:T(8,128)(2,1)} %get-tuple-element.28), channel_id=1, source_target_pairs={{8,0},{16,8},{24,16},{32,24},{40,32},{48,40},{56,48},{64,56},{72,6... | collective-permute-start | bytes 1572872 | tf_op jit(solution)/shard_map/ppermute | solution.py:50
  16.1 2.3 copy-start.9
  16.1 2.3 copy-start.11
  18.4 0.8 copy-start.8
  21.7 4.4 %copy-start.10 = (bf16[64,1024]{1,0:T(8,128)(2,1)S(1)}, bf16[64,1024]{1,0:T(8,128)(2,1)}, u32[]{:S(2)}) copy-start(bf16[64,1024]{1,0:T(8,128)(2,1)} %copy-done.9) | copy-start | bytes 393220
  21.7 4.4 %copy-start.12 = (bf16[64,1024]{1,0:T(8,128)(2,1)S(1)}, bf16[64,1024]{1,0:T(8,128)(2,1)}, u32[]{:S(2)}) copy-start(bf16[64,1024]{1,0:T(8,128)(2,1)} %copy-done.11) | copy-start | bytes 393220
  21.7 6.3 %copy-start.13 = (f32[64,64]{0,1:T(8,128)S(1)}, f32[64,64]{0,1:T(8,128)}, u32[]{:S(2)}) copy-start(f32[64,64]{0,1:T(8,128)} %fusion.55) | copy-start | bytes 49156
  21.7 6.3 %copy-start.14 = (f32[64,64]{0,1:T(8,128)S(1)}, f32[64,64]{0,1:T(8,128)}, u32[]{:S(2)}) copy-start(f32[64,64]{0,1:T(8,128)} %fusion.56) | copy-start | bytes 49156
  21.7 6.3 %copy-start.15 = (f32[64,64]{0,1:T(8,128)S(1)}, f32[64,64]{0,1:T(8,128)}, u32[]{:S(2)}) copy-start(f32[64,64]{0,1:T(8,128)} %fusion.57) | copy-start | bytes 49156
  89.4 1.0 copy-start.3
  116.8 17.3 %all-to-all-start.3 = ((f32[64,1,1088]{2,1,0:T(1,128)}), f32[64,1,1088]{2,1,0:T(1,128)}, u32[]{:S(2)}, u32[]{:S(2)}) async-start(f32[64,1,1088]{2,1,0:T(1,128)} %broadcast_in_dim.22), calls=%async_computation.3 | async-start | bytes 589824 | tf_op jit(solution)/shard_map/all_to_all | solution.py:14
  134.2 9.3 %copy-start.2 = (f32[1024,64]{0,1:T(8,128)S(1)}, f32[1024,64]{0,1:T(8,128)}, u32[]{:S(2)}) copy-start(f32[1024,64]{0,1:T(8,128)} %param.4) | copy-start | bytes 786436
  135.2 8.3 %copy-start.4 = (f32[64,1,1088]{2,0,1:T(8,128)}, f32[64,1,1088]{2,0,1:T(8,128)S(1)}, u32[]{:S(2)}) copy-start(f32[64,1,1088]{2,0,1:T(8,128)S(1)} %copy.97) | copy-start | bytes 835588
  136.6 7.8 %copy-start.1 = (f32[64,1024]{1,0:T(8,128)}, f32[64,1024]{1,0:T(8,128)S(1)}, u32[]{:S(2)}) copy-start(f32[64,1024]{1,0:T(8,128)S(1)} %fusion.2) | copy-start | bytes 786436
  155.4 18.4 %all-to-all-start.4 = ((bf16[8,8,2880]{2,1,0:T(8,128)(2,1)}), bf16[8,8,2880]{2,1,0:T(8,128)(2,1)}, u32[]{:S(2)}, u32[]{:S(2)}) async-start(bf16[8,8,2880]{2,1,0:T(8,128)(2,1)} %bitcast.82), calls=%async_computation.4 | async-start | bytes 753664 | tf_op jit(solution)/shard_map/all_to_all | solution.py:14
  179.8 19.2 %all-to-all-start.5 = ((bf16[8,8,2880]{2,1,0:T(8,128)(2,1)}), bf16[8,8,2880]{2,1,0:T(8,128)(2,1)}, u32[]{:S(2)}, u32[]{:S(2)}) async-start(bf16[8,8,2880]{2,1,0:T(8,128)(2,1)} %broadcast_in_dim.23), calls=%async_computation.5 | async-start | bytes 753664 | tf_op jit(solution)/shard_map/all_to_all | solution.py:14
  187.0 4.2 %copy-start.5 = (f32[64,1,1088]{2,0,1:T(8,128)S(1)}, f32[64,1,1088]{2,0,1:T(8,128)}, u32[]{:S(2)}) copy-start(f32[64,1,1088]{2,0,1:T(8,128)} %copy-done.4) | copy-start | bytes 835588
  207.9 32.7 %copy-start.7 = (f32[128,128]{1,0:T(8,128)S(1)}, f32[128,128]{1,0:T(8,128)}, u32[]{:S(2)}) copy-start(f32[128,128]{1,0:T(8,128)} %slice_add_fusion.4) | copy-start | bytes 196612
  210.3 19.3 %all-to-all-start.6 = ((bf16[64,2,1216]{2,1,0:T(2,128)(2,1)}), bf16[64,2,1216]{2,1,0:T(2,128)(2,1)S(1)}, u32[]{:S(2)}, u32[]{:S(2)}) async-start(bf16[64,2,1216]{2,1,0:T(2,128)(2,1)} %reshape.57), calls=%async_computation.6 | async-start | bytes 655360 | tf_op jit(solution)/shard_map/all_to_all | solution.py:14
  230.6 23.7 %copy-start.18 = (f32[64,64]{0,1:T(8,128)S(1)}, f32[64,64]{0,1:T(8,128)}, u32[]{:S(2)}) copy-start(f32[64,64]{0,1:T(8,128)} %get-tuple-element.40) | copy-start | bytes 49156
  230.7 23.8 %copy-start.19 = (f32[64,64]{0,1:T(8,128)S(1)}, f32[64,64]{0,1:T(8,128)}, u32[]{:S(2)}) copy-start(f32[64,64]{0,1:T(8,128)} %copy.90) | copy-start | bytes 49156
  233.8 22.1 %copy-start.6 = (f32[64,1024]{1,0:T(8,128)S(1)}, f32[64,1024]{1,0:T(8,128)}, u32[]{:S(2)}) copy-start(f32[64,1024]{1,0:T(8,128)} %slice.252) | copy-start | bytes 786436
  234.8 18.6 %all-to-all-start.7 = ((bf16[64,2,1216]{2,1,0:T(2,128)(2,1)}), bf16[64,2,1216]{2,1,0:T(2,128)(2,1)S(1)}, u32[]{:S(2)}, u32[]{:S(2)}) async-start(bf16[64,2,1216]{2,1,0:T(2,128)(2,1)} %reshape.59), calls=%async_computation.7 | async-start | bytes 655360 | tf_op jit(solution)/shard_map/all_to_all | solution.py:14
  241.2 15.7 %copy-start.16 = (f32[64,64]{1,0:T(8,128)S(1)}, f32[64,64]{1,0:T(8,128)}, u32[]{:S(2)}) copy-start(f32[64,64]{1,0:T(8,128)} %get-tuple-element.41) | copy-start | bytes 49156
  241.2 15.7 %copy-start.17 = (f32[64,64]{1,0:T(8,128)S(1)}, f32[64,64]{1,0:T(8,128)}, u32[]{:S(2)}) copy-start(f32[64,64]{1,0:T(8,128)} %get-tuple-element.42) | copy-start | bytes 49156

commit v3 on v0

v3 whole, which is shorter than its diff:
```python
import functools
import math

import jax
import jax.numpy as jnp
from jax import lax
from jax.experimental import pallas as pl
from jax.experimental.pallas import tpu as pltpu
from jax.sharding import PartitionSpec as P

LAG = 256
SMALL = 2.0**-20
LANES = 128
HIGHEST = lax.Precision.HIGHEST
HALF = jnp.bfloat16
FLOAT = jnp.float32


def padded(size):
    return -(-size // LANES) * LANES


def exchange(value, axis):
    return lax.all_to_all(value, axis, 0, 0, tiled=True)


def kernel_call(body, outputs, *operands):
    many = isinstance(outputs, list)
    spec = pl.BlockSpec(memory_space=pltpu.VMEM)
    return pl.pallas_call(
        body,
        out_shape=outputs,
        in_specs=[spec] * len(operands),
        out_specs=[spec] * len(outputs) if many else spec,
        compiler_params=pltpu.CompilerParams(vmem_limit_bytes=48 * 2**20),
    )(*operands)


def shape(dims, dtype):
    return jax.ShapeDtypeStruct(dims, dtype)


def rows_dot(a, b, precision=None):
    return lax.dot_general(a, b, (((1,), (1,)), ((), ())), preferred_element_type=FLOAT, precision=precision)


def exact(a, b):
    return rows_dot(a, b, HIGHEST)


def times(a, b):
    return jnp.dot(a, b, precision=HIGHEST, preferred_element_type=FLOAT)


def high_low(value):
    high = value.astype(HALF)
    return high, (value - high.astype(FLOAT)).astype(HALF)


def joined(value):
    value = value.astype(FLOAT)
    middle = value.shape[1] // 2
    return value[:, :middle] + value[:, middle:]


def project_own(vectors, hidden, out):
    whole = hidden.shape[0] // LANES * LANES
    out[:, LAG : LAG + whole] = rows_dot(vectors, hidden[:whole]).astype(HALF)


def project_edges(vectors, hidden_tail, behind, ahead, out, tokens):
    whole = tokens // LANES * LANES
    width = tokens + 2 * LAG
    rest = tokens - whole
    fill = (LANES - rest) % LANES
    rows = vectors.shape[0]
    out[:, :LAG] = rows_dot(vectors, behind[...]).astype(HALF)
    if rest:
        tile = jnp.concatenate([hidden_tail, ahead[:fill]])
        out[:, LAG + whole : LAG + whole + LANES] = rows_dot(vectors, tile).astype(HALF)
    last = rows_dot(vectors, ahead[fill:]).astype(HALF)
    spare = padded(width) - width
    if spare:
        last = jnp.concatenate([last, jnp.zeros((rows, spare), HALF)], axis=1)
    out[:, LAG + whole + rest + fill : padded(width)] = last


def start_kernel(x, p, hidden, out):
    cols, wide = x.shape[0], out.shape[1] - 4 * x.shape[0]
    both = jnp.concatenate([x[...], p[...]])
    project_own(both.astype(HALF), hidden, out)
    high, low = high_low(exact(both, both))
    out[:, wide : wide + 2 * cols] = high
    out[:, wide + 2 * cols :] = low


def edge_kernel(tokens, x, p, tail, behind, ahead, start, out):
    out[...] = start[...]
    both = jnp.concatenate([x[...], p[...]]).astype(HALF)
    project_edges(both, tail[...], behind, ahead, out, tokens)


def known_kernel(wide, received, out):
    total = jnp.sum(received[...].astype(FLOAT), axis=0)
    high, low = high_low(joined(total[:, wide:]))
    total = jnp.concatenate([total[:, :wide].astype(HALF), high, low], axis=1)
    out[...] = jnp.broadcast_to(total, out.shape)


def shifted(projected, tokens):
    return [projected[:, 2 * LAG : 2 * LAG + tokens], projected[:, :tokens]]


def first_kernel(known, hidden, out):
    tokens, features = hidden.shape
    cols = out.shape[0]
    projected = known[:cols]
    halves = jnp.concatenate(shifted(projected, tokens))
    image = jnp.dot(halves, hidden[...], preferred_element_type=FLOAT)
    out[:, :features] = image[:cols] + image[cols:]
    cross = rows_dot(halves, projected[:, LAG : LAG + tokens])
    out[:, features:] = cross[:cols] + cross[cols:]


def residual_kernel(total, x, p, hidden, behind, ahead, out):
    tokens, features = hidden.shape
    cols = x.shape[0]
    image = total[:, :features]
    residual = (image - times(total[:, features:], x[...])) * SMALL
    rounded = residual.astype(HALF)
    project_own(rounded, hidden, out)
    project_edges(rounded, hidden[tokens // LANES * LANES :], behind, ahead, out, tokens)
    both = jnp.concatenate([x[...], p[...]])
    products = exact(jnp.concatenate([residual, image]), both)
    own = exact(jnp.concatenate([residual, residual]), residual)[:cols]
    own = jnp.concatenate([own, jnp.zeros_like(own)], axis=1)
    at = padded(tokens + 2 * LAG)
    for value in (products[:cols], products[cols:], own):
        high, low = high_low(value)
        out[:, at : at + 2 * cols] = high
        out[:, at + 6 * cols : at + 8 * cols] = low
        at += 2 * cols


def found_kernel(wide, where, received, estimate, known, out):
    rows = received.shape[1]
    cols = estimate.shape[0]
    total = jnp.sum(received[...].astype(FLOAT), axis=0)
    products = joined(total[:, wide:])
    first = pl.multiple_of(where[0] * rows, rows)
    lacks = (products[:, 2 * cols : 3 * cols] - estimate[pl.ds(first, rows), :]) * SMALL
    lacks = jnp.concatenate([lacks, jnp.zeros_like(lacks)]).astype(HALF)
    shift = jnp.dot(lacks, known[:cols, :wide], preferred_element_type=FLOAT)[:rows]
    high, low = high_low(products)
    total = jnp.concatenate([(total[:, :wide] - shift).astype(HALF), high, low], axis=1)
    out[...] = jnp.broadcast_to(total, out.shape)


def image_kernel(blocks, found, known, hidden, out):
    tokens, features = hidden.shape
    cols = found.shape[0]
    span = features // blocks
    proj_r, proj_p = found[:, : tokens + 2 * LAG], known[cols:, : tokens + 2 * LAG]
    halves = jnp.concatenate(shifted(proj_r, tokens) + shifted(proj_p, tokens))
    middles = jnp.concatenate([proj_r[:, LAG : LAG + tokens], proj_p[:, LAG : LAG + tokens]])
    image = jnp.dot(halves, hidden[...], preferred_element_type=FLOAT)
    cross = rows_dot(halves, middles)

    def summed(value):
        return jnp.concatenate(
            [value[:cols] + value[cols : 2 * cols], value[2 * cols : 3 * cols] + value[3 * cols :]]
        )

    image, cross = summed(image), summed(cross)
    high = cross.astype(HALF).astype(FLOAT)
    low = cross - high
    left = lax.broadcasted_iota(jnp.int32, cross.shape, 1) < cols
    pieces = [
        jnp.where(left, high, pltpu.roll(low, cols, 1)),
        jnp.where(left, pltpu.roll(high, cols, 1), low),
    ]
    groups = 2 * cols // 8
    for g in range(groups):
        for b in range(blocks):
            out[g * blocks + b, :, :span] = image[8 * g : 8 * g + 8, b * span : (b + 1) * span].astype(HALF)
    for k in range(out.shape[0]):
        if k < 2 * groups:
            g = k % groups
            out[k, :, span:] = pieces[k // groups][8 * g : 8 * g + 8].astype(HALF)
        else:
            out[k, :, span:] = jnp.zeros((8, 2 * cols), HALF)


def total_kernel(factor, cols, received, out):
    span = received.shape[2] - 2 * cols
    total = jnp.sum(received[...].astype(FLOAT), axis=0) * factor
    cross = total[:, span:]
    cross = cross + pltpu.roll(cross, cols, 1)
    high = cross.astype(HALF).astype(FLOAT)
    left = lax.broadcasted_iota(jnp.int32, cross.shape, 1) < cols
    cross = jnp.where(left, high, cross - high)
    total = jnp.concatenate([total[:, :span], cross], axis=1).astype(HALF)
    out[...] = jnp.broadcast_to(total, out.shape)


def last_kernel(blocks, gathered, first_total, scale, across, top, u_image_x, p_image_x, images, gram):
    cols = scale.shape[0]
    features = images.shape[1]
    span = features // blocks
    groups = cols // 8
    images[:cols] = first_total[:, :features]
    for g in range(groups):
        for b in range(blocks):
            at = slice(b * span, (b + 1) * span)
            rows = slice(cols + 8 * g, cols + 8 * g + 8)
            images[rows, at] = gathered[g * blocks + b, :, :span].astype(FLOAT) * scale[8 * g : 8 * g + 8]
            rows = slice(2 * cols + 8 * g, 2 * cols + 8 * g + 8)
            images[rows, at] = gathered[(groups + g) * blocks + b, :, :span].astype(FLOAT)

    def piece(first):
        value = jnp.concatenate([gathered[k, :, span:].astype(FLOAT) for k in range(first, first + groups)])
        return (value + pltpu.roll(value, cols, 1))[:, :cols]

    rr, pr, rp, pp = (piece(i * groups) for i in range(4))
    gram[:cols] = top[...]
    gram[cols : 2 * cols, :cols] = u_image_x[...]
    gram[cols : 2 * cols, cols : 2 * cols] = rr * scale[...] * across[...]
    gram[cols : 2 * cols, 2 * cols :] = rp * scale[...]
    gram[2 * cols :, :cols] = p_image_x[...]
    gram[2 * cols :, cols : 2 * cols] = pr * across[...]
    gram[2 * cols :, 2 * cols :] = pp


def local(hidden_states, current_block, directions):
    tokens, features = hidden_states.shape
    cols = current_block.shape[1]
    feat, tok = lax.axis_size("feat"), lax.axis_size("tok")
    factor = 0.5 / math.sqrt(tokens * tok - LAG)
    wide = padded(tokens + 2 * LAG)
    blocks = tok * 8 // (2 * cols)

    up = [(i, i + 1) for i in range(tok - 1)]
    down = [(i + 1, i) for i in range(tok - 1)]
    behind = lax.ppermute(hidden_states[tokens - LAG :], "tok", up)
    ahead = lax.ppermute(hidden_states[:LAG], "tok", down)
    x, p = current_block.T, directions.T

    total = wide + 4 * cols
    part = kernel_call(start_kernel, shape((2 * cols, total), HALF), x, p, hidden_states)
    tail = hidden_states[tokens // LANES * LANES :]
    part = kernel_call(
        functools.partial(edge_kernel, tokens), shape((2 * cols, total), HALF), x, p, tail, behind, ahead, part
    )
    blocked = shape((feat, 2 * cols // feat, total), HALF)
    part = exchange(part.reshape(blocked.shape), "feat")
    part = kernel_call(functools.partial(known_kernel, wide), blocked, part)
    known = exchange(part, "feat").reshape(2 * cols, total)

    part = kernel_call(first_kernel, shape((cols, features + cols), FLOAT), known, hidden_states)
    part = exchange(part.reshape(tok, 1, -1), "tok")
    part = jnp.sum(part, axis=0) * factor
    part = exchange(jnp.broadcast_to(part, (tok,) + part.shape), "tok")
    first_total = part.reshape(cols, features + cols)
    estimate = first_total[:, features:]

    total = wide + 12 * cols
    part = kernel_call(
        residual_kernel, shape((cols, total), HALF), first_total, x, p, hidden_states, behind, ahead
    )
    blocked = shape((feat, cols // feat, total), HALF)
    part = exchange(part.reshape(blocked.shape), "feat")
    where = lax.axis_index("feat").astype(jnp.int32).reshape(1)
    vmem = pl.BlockSpec(memory_space=pltpu.VMEM)
    part = pl.pallas_call(
        functools.partial(found_kernel, wide),
        out_shape=blocked,
        in_specs=[pl.BlockSpec(memory_space=pltpu.SMEM), vmem, vmem, vmem],
        out_specs=vmem,
        compiler_params=pltpu.CompilerParams(vmem_limit_bytes=48 * 2**20),
    )(where, part, estimate, known)
    found = exchange(part, "feat").reshape(cols, total)

    blocked = shape((tok, 8, features // blocks + 2 * cols), HALF)
    part = kernel_call(functools.partial(image_kernel, blocks), blocked, found, known, hidden_states)
    part = exchange(part, "tok")
    part = kernel_call(functools.partial(total_kernel, factor, cols), blocked, part)
    gathered = exchange(part, "tok")

    products = joined(found[:, wide:])
    r_x, r_p, rayleigh_t, image_x_p, r_r = (products[:, i * cols : (i + 1) * cols] for i in range(5))
    products = joined(known[:, wide:])
    x_x, p_x, p_p = products[:cols, :cols], products[cols:, :cols], products[cols:, cols:]
    lacks = (rayleigh_t - estimate) * SMALL
    shift = times(lacks, r_x.T)
    r_r = r_r - shift - shift.T + times(times(lacks, x_x), lacks.T)
    r_x = r_x - times(lacks, x_x)
    r_p = r_p - times(lacks, p_x.T)

    lengths = jnp.sum(r_r * jnp.eye(cols, dtype=FLOAT), axis=1, keepdims=True)
    scale = lax.rsqrt(lengths * (1.0 / SMALL**2) + 1e-06) * (1.0 / SMALL)
    across = scale.T
    u_x, u_p = r_x * scale, r_p * scale
    u_u = r_r * scale * across
    u_image_x = (r_r * (1.0 / SMALL) + times(r_x, rayleigh_t.T)) * scale
    top = jnp.concatenate([rayleigh_t.T, u_image_x.T, image_x_p], axis=1)
    gram_search = jnp.concatenate(
        [
            jnp.concatenate([x_x, u_x.T, p_x.T], axis=1),
            jnp.concatenate([u_x, u_u, u_p], axis=1),
            jnp.concatenate([p_x, u_p.T, p_p], axis=1),
        ]
    )
    images, gram_image = kernel_call(
        functools.partial(last_kernel, blocks),
        [shape((3 * cols, features), FLOAT), shape((3 * cols, 3 * cols), FLOAT)],
        gathered,
        first_total,
        scale,
        across,
        top,
        u_image_x,
        image_x_p.T,
    )
    return (images.T, gram_image, gram_search)


def solution(mesh):
    return jax.shard_map(
        local,
        mesh=mesh,
        in_specs=(P("tok", "feat"), P("feat", None), P("feat", None)),
        out_specs=(P("feat", None), P(), P()),
        check_vma=False,
    )
```

time: 1520 us -> 230 us (0.15)
  waiting for transfers between devices: 1410 us -> 51 us
  blocking collectives: 42.6 us -> 92.4 us
  local copies, waits for them, and re-layouts: 8.05 us -> 34.9 us
  matrix products: 20.9 us -> 5.62 us
    psum x5 -> x0, waiting for transfers between devices: 1400 us -> none  [the longest x2 1150 us: project(): return lax.psum(backward, 'tok') * factor]
    all_to_all x0 -> x4, blocking collectives: none -> 92.4 us  [exchange(): return lax.all_to_all(value, axis, 0, 0, tiled=True)]
    psum x2 -> x0, blocking collectives: 42.6 us -> none  [totals(): return lax.psum(values, 'feat')]
    all_to_all x0 -> x4, waiting for transfers between devices: none -> 41.9 us  [exchange(): return lax.all_to_all(value, axis, 0, 0, tiled=True)]
    all_to_all x0 -> x4, starting transfers between devices: none -> 20.6 us  [exchange(): return lax.all_to_all(value, axis, 0, 0, tiled=True)]
    dot_general x8 -> x5, matrix products: 20.9 us -> 5.62 us  [times(): return jnp.dot(a, b, precision=HIGHEST, preferred_element_type=FLOAT)]
  transfers between devices with their start and end apart: 9 -> 6, of which waited for: 9 -> 6; matrix products, arithmetic and copies ran while one was open for 0% -> 7% of each run, Pallas kernels for 0% -> 1%
where the time goes in v3:
time: 230 us; the launch traced here: 228 us
  blocking collectives  92.4 us (40%)
  waiting for transfers between devices  51 us (22%)
  local copies, waits for them, and re-layouts  34.9 us (15%)
  starting transfers between devices  26.7 us (12%)
  Pallas kernels  11.1 us (5%)
  matrix products  5.62 us (2%)
  other arithmetic  4.99 us (2%)
    all_to_all x4, blocking collectives, exchange(): return lax.all_to_all(value, axis, 0, 0, tiled=True)  92.4 us
    all_to_all x4, waiting for transfers between devices, exchange(): return lax.all_to_all(value, axis, 0, 0, tiled=True)  41.9 us
    all_to_all x4, starting transfers between devices, exchange(): return lax.all_to_all(value, axis, 0, 0, tiled=True)  20.6 us
    unnamed x57, local copies, waits for them, and re-layouts  20 us
    pallas_call x8, Pallas kernels, kernel_call(): pl.pallas_call(body, out_shape=outputs, in_specs=[spec] * len(operands),...  9.92 us
    ppermute x1, waiting for transfers between devices, local(): ahead = lax.ppermute(hidden_states[:LAG], 'tok', down)  6.03 us
    dot_general x5, matrix products, times(): return jnp.dot(a, b, precision=HIGHEST, preferred_element_type=FLOAT)  5.62 us
  transfers between devices with their start and end apart: 6, of which 6 were waited for; matrix products, arithmetic and copies ran while one was open for 7% of the time, Pallas kernels for 1%

profile of v3, /device:TPU:6, one launch (start us, length us, event | category | flops | bytes accessed | tf_op | source)
XLA Modules:
  0.0 227.6 jit_solution(14143978871238702210)
XLA Ops:
  0.6 1.3 fusion.7
  1.9 4.2 %collective-permute-start = (bf16[256,1024]{1,0:T(8,128)(2,1)S(1)}, bf16[256,1024]{1,0:T(8,128)(2,1)S(1)}, u32[]{:S(2)}, u32[]{:S(2)}) collective-permute-start(bf16[256,1024]{1,0:T(8,128)(2,1)S(1)} %get-tuple-element.17), channel_id=1, source_target_pairs={{0,8},{8,16},{16,24},{24,32},{32,40},{40,48},{48,56},{56,64},{64,7... | collective-permute-start | bytes 1572872 | tf_op jit(solution)/shard_map/ppermute | solution.py:244
  6.1 1.9 collective-permute-start.1
  8.0 0.9 slice.54.tail
  9.0 2.0 copy-done
  11.0 0.9 copy-done.7
  11.9 0.9 copy-done.9
  12.9 1.6 shard_map.58.start
  14.5 3.0 %collective-permute-done.behind = bf16[256,1024]{1,0:T(8,128)(2,1)S(1)} collective-permute-done((bf16[256,1024]{1,0:T(8,128)(2,1)S(1)}, bf16[256,1024]{1,0:T(8,128)(2,1)S(1)}, u32[]{:S(2)}, u32[]{:S(2)}) %collective-permute-start) | collective-permute-done | bytes 524320 | tf_op jit(solution)/shard_map/ppermute | solution.py:244
  17.5 6.0 %collective-permute-done.1.ahead = bf16[256,1024]{1,0:T(8,128)(2,1)S(1)} collective-permute-done((bf16[256,1024]{1,0:T(8,128)(2,1)S(1)}, bf16[256,1024]{1,0:T(8,128)(2,1)S(1)}, u32[]{:S(2)}, u32[]{:S(2)}) %collective-permute-start.1) | collective-permute-done | bytes 524320 | tf_op jit(solution)/shard_map/ppermute | solution.py:245
  24.0 30.4 %all_to_all.40.received = bf16[8,16,2560]{2,1,0:T(8,128)(2,1)S(1)} all-to-all(bf16[8,16,2560]{2,1,0:T(8,128)(2,1)S(1)} %bitcast.40), channel_id=1, replica_groups=mesh['tok'=64,'feat'=8] {'feat'}, dimensions={0} | all-to-all | bytes 1310720 | tf_op jit(solution)/shard_map/all_to_all | solution.py:24
  54.5 23.5 %all_to_all.41 = bf16[8,16,2560]{2,1,0:T(8,128)(2,1)S(1)} all-to-all(bf16[8,16,2560]{2,1,0:T(8,128)(2,1)S(1)} %shard_map.60), channel_id=1, replica_groups=mesh['tok'=64,'feat'=8] {'feat'}, dimensions={0} | all-to-all | bytes 1310720 | tf_op jit(solution)/shard_map/all_to_all | solution.py:24
  79.9 21.9 %all_to_all.42 = f32[64,1,1088]{2,1,0:T(1,128)} all-to-all(f32[64,1,1088]{2,1,0:T(1,128)S(1)} %copy.48), channel_id=1, replica_groups=mesh['tok'=64,'feat'=8] {'tok'}, dimensions={0} | all-to-all | bytes 557056 | tf_op jit(solution)/shard_map/all_to_all | solution.py:24
  101.8 1.2 reduce_sum.18
  103.1 16.6 %all_to_all.43 = f32[64,1,1088]{2,1,0:T(1,128)S(1)} all-to-all(f32[64,1,1088]{2,1,0:T(1,128)S(1)} %broadcast_in_dim.4), channel_id=1, replica_groups=mesh['tok'=64,'feat'=8] {'tok'}, dimensions={0} | all-to-all | bytes 557056 | tf_op jit(solution)/shard_map/all_to_all | solution.py:24
  120.5 0.9 copy-done.8
  121.4 0.9 copy-done.10
  122.4 1.0 copy-done.12
  123.4 1.0 copy-done.14
  124.4 2.6 %shard_map.62 = bf16[64,3072]{1,0:T(8,128)(2,1)S(1)} custom-call(f32[64,1088]{1,0:T(8,128)S(1)} %bitcast.38, f32[64,1024]{1,0:T(8,128)S(1)} %bitcast.43, f32[64,1024]{1,0:T(8,128)S(1)} %bitcast.46, bf16[1728,1024]{1,0:T(8,128)(2,1)S(1)} %copy-done.1, bf16[256,1024]{1,0:T(8,128)(2,1)S(1)} %copy-done.12, bf16[256,1024]{1,0:T(8,128)(2,1)S(1)} %copy-done.14), custom_call_target="tpu_custom_call" | custom-call | tf_op jit(solution)/shard_map/pallas_call | solution.py:30
  128.5 4.3 %all-to-all-start.4 = ((bf16[8,8,3072]{2,1,0:T(8,128)(2,1)}), bf16[8,8,3072]{2,1,0:T(8,128)(2,1)}, u32[]{:S(2)}, u32[]{:S(2)}) async-start(bf16[8,8,3072]{2,1,0:T(8,128)(2,1)} %bitcast.47), calls=%async_computation.4 | async-start | bytes 786432 | tf_op jit(solution)/shard_map/all_to_all | solution.py:24
  132.8 2.0 copy.49
  134.8 1.4 slice.72
  136.2 1.5 copy.51.estimate
  137.6 9.9 %all-to-all-done.4.received = bf16[8,8,3072]{2,1,0:T(8,128)(2,1)} async-done(((bf16[8,8,3072]{2,1,0:T(8,128)(2,1)}), bf16[8,8,3072]{2,1,0:T(8,128)(2,1)}, u32[]{:S(2)}, u32[]{:S(2)}) %all-to-all-start.4) | async-done | bytes 393248 | tf_op jit(solution)/shard_map/all_to_all | solution.py:24
  147.6 1.1 copy-done.3
  149.4 1.2 shard_map.63
  151.3 4.1 %all-to-all-start.5 = ((bf16[8,8,3072]{2,1,0:T(8,128)(2,1)}), bf16[8,8,3072]{2,1,0:T(8,128)(2,1)}, u32[]{:S(2)}, u32[]{:S(2)}) async-start(bf16[8,8,3072]{2,1,0:T(8,128)(2,1)} %copy-done.17), calls=%async_computation.5 | async-start | bytes 786432 | tf_op jit(solution)/shard_map/all_to_all | solution.py:24
  155.4 1.5 slice.79
  156.9 1.6 copy.73
  160.7 1.4 copy.62
  162.1 8.8 %all-to-all-done.5 = bf16[8,8,3072]{2,1,0:T(8,128)(2,1)} async-done(((bf16[8,8,3072]{2,1,0:T(8,128)(2,1)}), bf16[8,8,3072]{2,1,0:T(8,128)(2,1)}, u32[]{:S(2)}, u32[]{:S(2)}) %all-to-all-start.5) | async-done | bytes 393248 | tf_op jit(solution)/shard_map/all_to_all | solution.py:24
  170.9 1.5 slice.73
  172.4 1.7 copy.72
  174.1 1.0 convert_element_type.7
  176.8 1.6 fusion.4
  178.4 1.1 copy-done.4
  179.4 2.4 %shard_map.64 = bf16[64,8,384]{2,1,0:T(8,128)(2,1)S(1)} custom-call(bf16[64,3072]{1,0:T(8,128)(2,1)} %bitcast.9.found, bf16[128,2560]{1,0:T(8,128)(2,1)S(1)} %bitcast.37, bf16[1728,1024]{1,0:T(8,128)(2,1)S(1)} %copy-done.1), custom_call_target="tpu_custom_call" | custom-call | tf_op jit(solution)/shard_map/pallas_call | solution.py:30
  184.4 1.1 select_reduce_fusion
  185.5 6.2 %all-to-all-start.6 = ((bf16[64,8,384]{2,1,0:T(8,128)(2,1)}), bf16[64,8,384]{2,1,0:T(8,128)(2,1)S(1)}, u32[]{:S(2)}, u32[]{:S(2)}) async-start(bf16[64,8,384]{2,1,0:T(8,128)(2,1)} %copy-done.15), calls=%async_computation.6 | async-start | bytes 786432 | tf_op jit(solution)/shard_map/all_to_all | solution.py:24
  191.6 1.0 convolution_add_fusion
  192.7 1.1 convolution_subtract_fusion
  194.0 0.9 broadcast_multiply_fusion
  194.9 10.9 %all-to-all-done.6.received = bf16[64,8,384]{2,1,0:T(8,128)(2,1)S(1)} async-done(((bf16[64,8,384]{2,1,0:T(8,128)(2,1)}), bf16[64,8,384]{2,1,0:T(8,128)(2,1)S(1)}, u32[]{:S(2)}, u32[]{:S(2)}) %all-to-all-start.6) | async-done | bytes 393248 | tf_op jit(solution)/shard_map/all_to_all | solution.py:24
  205.8 0.9 shard_map.65
  206.7 5.9 %all-to-all-start.7 = ((bf16[64,8,384]{2,1,0:T(8,128)(2,1)}), bf16[64,8,384]{2,1,0:T(8,128)(2,1)S(1)}, u32[]{:S(2)}, u32[]{:S(2)}) async-start(bf16[64,8,384]{2,1,0:T(8,128)(2,1)} %shard_map.65), calls=%async_computation.7 | async-start | bytes 786432 | tf_op jit(solution)/shard_map/all_to_all | solution.py:24
  214.2 12.4 %all-to-all-done.7.gathered = bf16[64,8,384]{2,1,0:T(8,128)(2,1)S(1)} async-done(((bf16[64,8,384]{2,1,0:T(8,128)(2,1)}), bf16[64,8,384]{2,1,0:T(8,128)(2,1)S(1)}, u32[]{:S(2)}, u32[]{:S(2)}) %all-to-all-start.7) | async-done | bytes 393248 | tf_op jit(solution)/shard_map/all_to_all | solution.py:24
  226.5 1.1 shard_map.66
  (75 shorter events, 14.3 us)
Async XLA Ops:
  1.9 15.6 %collective-permute-start = (bf16[256,1024]{1,0:T(8,128)(2,1)S(1)}, bf16[256,1024]{1,0:T(8,128)(2,1)S(1)}, u32[]{:S(2)}, u32[]{:S(2)}) collective-permute-start(bf16[256,1024]{1,0:T(8,128)(2,1)S(1)} %get-tuple-element.17), channel_id=1, source_target_pairs={{0,8},{8,16},{16,24},{24,32},{32,40},{40,48},{48,56},{56,64},{64,7... | collective-permute-start | bytes 1572872 | tf_op jit(solution)/shard_map/ppermute | solution.py:244
  6.1 17.4 %collective-permute-start.1 = (bf16[256,1024]{1,0:T(8,128)(2,1)S(1)}, bf16[256,1024]{1,0:T(8,128)(2,1)S(1)}, u32[]{:S(2)}, u32[]{:S(2)}) collective-permute-start(bf16[256,1024]{1,0:T(8,128)(2,1)S(1)} %get-tuple-element.16), channel_id=1, source_target_pairs={{8,0},{16,8},{24,16},{32,24},{40,32},{48,40},{56,48},{64,56},{72,6... | collective-permute-start | bytes 1572872 | tf_op jit(solution)/shard_map/ppermute | solution.py:245
  9.0 2.0 copy-start
  11.0 0.9 copy-start.7
  11.9 0.9 copy-start.9
  14.4 63.5 %copy-start.1 = (bf16[1728,1024]{1,0:T(8,128)(2,1)S(1)}, bf16[1728,1024]{1,0:T(8,128)(2,1)}, u32[]{:S(2)}) copy-start(bf16[1728,1024]{1,0:T(8,128)(2,1)} %hidden.7) | copy-start | bytes 10616836
  17.5 61.3 %copy-start.11 = (bf16[256,1024]{1,0:T(8,128)(2,1)}, bf16[256,1024]{1,0:T(8,128)(2,1)S(1)}, u32[]{:S(2)}) copy-start(bf16[256,1024]{1,0:T(8,128)(2,1)S(1)} %collective-permute-done.behind) | copy-start | bytes 1572868
  23.5 55.3 %copy-start.13 = (bf16[256,1024]{1,0:T(8,128)(2,1)}, bf16[256,1024]{1,0:T(8,128)(2,1)S(1)}, u32[]{:S(2)}) copy-start(bf16[256,1024]{1,0:T(8,128)(2,1)S(1)} %collective-permute-done.1.ahead) | copy-start | bytes 1572868
  78.8 0.8 copy-start.2
  119.8 0.7 copy-start.19
  120.5 0.9 copy-start.8
  121.4 0.9 copy-start.10
  122.4 1.0 copy-start.12
  123.4 1.0 copy-start.14
  127.0 0.7 copy-start.5
  127.7 0.7 copy-start.16
  128.5 19.1 %all-to-all-start.4 = ((bf16[8,8,3072]{2,1,0:T(8,128)(2,1)}), bf16[8,8,3072]{2,1,0:T(8,128)(2,1)}, u32[]{:S(2)}, u32[]{:S(2)}) async-start(bf16[8,8,3072]{2,1,0:T(8,128)(2,1)} %bitcast.47), calls=%async_computation.4 | async-start | bytes 786432 | tf_op jit(solution)/shard_map/all_to_all | solution.py:24
  147.6 1.1 copy-start.3
  148.6 0.8 copy-start.18
  150.6 0.7 copy-start.17
  151.3 19.6 %all-to-all-start.5 = ((bf16[8,8,3072]{2,1,0:T(8,128)(2,1)}), bf16[8,8,3072]{2,1,0:T(8,128)(2,1)}, u32[]{:S(2)}, u32[]{:S(2)}) async-start(bf16[8,8,3072]{2,1,0:T(8,128)(2,1)} %copy-done.17), calls=%async_computation.5 | async-start | bytes 786432 | tf_op jit(solution)/shard_map/all_to_all | solution.py:24
  159.3 0.6 copy-start.22
  175.1 1.6 copy-start.20
  175.9 0.8 copy-start.21
  178.4 1.1 copy-start.4
  181.9 0.7 copy-start.15
  182.6 30.0 %copy-start.23 = (f32[64,64]{1,0:T(8,128)S(1)}, f32[64,64]{1,0:T(8,128)}, u32[]{:S(2)}) copy-start(f32[64,64]{1,0:T(8,128)} %get-tuple-element.23) | copy-start | bytes 49156
  182.6 30.0 %copy-start.24 = (f32[64,64]{1,0:T(8,128)S(1)}, f32[64,64]{1,0:T(8,128)}, u32[]{:S(2)}) copy-start(f32[64,64]{1,0:T(8,128)} %copy.62) | copy-start | bytes 49156
  182.6 30.3 %copy-start.25 = (f32[64,64]{0,1:T(8,128)S(1)}, f32[64,64]{0,1:T(8,128)}, u32[]{:S(2)}) copy-start(f32[64,64]{0,1:T(8,128)} %get-tuple-element.24) | copy-start | bytes 49156
  182.7 30.3 %copy-start.26 = (f32[64,64]{0,1:T(8,128)S(1)}, f32[64,64]{0,1:T(8,128)}, u32[]{:S(2)}) copy-start(f32[64,64]{0,1:T(8,128)} %get-tuple-element.25) | copy-start | bytes 49156
  182.7 43.9 %copy-start.6 = (f32[64,1,1088]{2,0,1:T(8,128)S(1)}, f32[64,1,1088]{2,0,1:T(8,128)}, u32[]{:S(2)}) copy-start(f32[64,1,1088]{2,0,1:T(8,128)} %copy-done.5) | copy-start | bytes 835588
  185.5 20.3 %all-to-all-start.6 = ((bf16[64,8,384]{2,1,0:T(8,128)(2,1)}), bf16[64,8,384]{2,1,0:T(8,128)(2,1)S(1)}, u32[]{:S(2)}, u32[]{:S(2)}) async-start(bf16[64,8,384]{2,1,0:T(8,128)(2,1)} %copy-done.15), calls=%async_computation.6 | async-start | bytes 786432 | tf_op jit(solution)/shard_map/all_to_all | solution.py:24
  206.7 19.8 %all-to-all-start.7 = ((bf16[64,8,384]{2,1,0:T(8,128)(2,1)}), bf16[64,8,384]{2,1,0:T(8,128)(2,1)S(1)}, u32[]{:S(2)}, u32[]{:S(2)}) async-start(bf16[64,8,384]{2,1,0:T(8,128)(2,1)} %shard_map.65), calls=%async_computation.7 | async-start | bytes 786432 | tf_op jit(solution)/shard_map/all_to_all | solution.py:24

commit v4 on v3

v4 whole, which is shorter than its diff:
```python
import functools
import math

import jax
import jax.numpy as jnp
from jax import lax
from jax.experimental import pallas as pl
from jax.experimental.pallas import tpu as pltpu
from jax.sharding import PartitionSpec as P

LAG = 256
SMALL = 2.0**-20
LANES = 128
HIGHEST = lax.Precision.HIGHEST
HALF = jnp.bfloat16
FLOAT = jnp.float32


def padded(size):
    return -(-size // LANES) * LANES


def exchange(value, axis):
    return lax.all_to_all(value, axis, 0, 0, tiled=True)


def kernel_call(body, outputs, *operands):
    many = isinstance(outputs, list)
    spec = pl.BlockSpec(memory_space=pltpu.VMEM)
    return pl.pallas_call(
        body,
        out_shape=outputs,
        in_specs=[spec] * len(operands),
        out_specs=[spec] * len(outputs) if many else spec,
        compiler_params=pltpu.CompilerParams(vmem_limit_bytes=16 * 2**20),
    )(*operands)


def shape(dims, dtype):
    return jax.ShapeDtypeStruct(dims, dtype)


def rows_dot(a, b, precision=None):
    return lax.dot_general(a, b, (((1,), (1,)), ((), ())), preferred_element_type=FLOAT, precision=precision)


def exact(a, b):
    return rows_dot(a, b, HIGHEST)


def times(a, b):
    return jnp.dot(a, b, precision=HIGHEST, preferred_element_type=FLOAT)


def high_low(value):
    high = value.astype(HALF)
    return high, (value - high.astype(FLOAT)).astype(HALF)


def joined(value):
    value = value.astype(FLOAT)
    middle = value.shape[1] // 2
    return value[:, :middle] + value[:, middle:]


def project_own(vectors, hidden, out):
    whole = hidden.shape[0] // LANES * LANES
    out[:, :whole] = rows_dot(vectors, hidden[:whole]).astype(HALF)


def project_edge(vectors, tail, ahead):
    rows, rest = vectors.shape[0], tail.shape[0]
    value = rows_dot(vectors, jnp.concatenate([tail, ahead[...]])).astype(HALF)
    spare = padded(rest + LAG) - rest - LAG
    if spare:
        value = jnp.concatenate([value, jnp.zeros((rows, spare), HALF)], axis=1)
    return value


def start_kernel(x, p, hidden, out):
    cols = x.shape[0]
    wide = out.shape[1] - 4 * cols
    both = jnp.concatenate([x[...], p[...]])
    project_own(both.astype(HALF), hidden, out)
    high, low = high_low(exact(both, both))
    out[:, wide : wide + 2 * cols] = high
    out[:, wide + 2 * cols :] = low


def edge_kernel(whole, x, p, tail, ahead, start, out):
    wide = out.shape[1] - 4 * x.shape[0]
    out[:, :whole] = start[:, :whole]
    out[:, wide:] = start[:, wide:]
    both = jnp.concatenate([x[...], p[...]]).astype(HALF)
    out[:, whole:wide] = project_edge(both, tail[...], ahead)


def known_kernel(wide, received, out):
    total = jnp.sum(received[...].astype(FLOAT), axis=0)
    high, low = high_low(joined(total[:, wide:]))
    total = jnp.concatenate([total[:, :wide].astype(HALF), high, low], axis=1)
    out[...] = jnp.broadcast_to(total, out.shape)


def lag_image(projected, hidden, ahead):
    tokens = hidden.shape[0]
    cut = tokens // LANES * LANES - LAG
    here, later = projected[:, :tokens], projected[:, LAG : LAG + tokens]
    edge = jnp.concatenate([hidden[cut + LAG :], ahead[...]])
    image = jnp.dot(later, hidden[...], preferred_element_type=FLOAT)
    image += jnp.dot(here[:, :cut], hidden[LAG : LAG + cut], preferred_element_type=FLOAT)
    image += jnp.dot(here[:, cut:], edge, preferred_element_type=FLOAT)
    return image, rows_dot(later, here) + rows_dot(here, later)


def first_kernel(known, hidden, ahead, out):
    features = hidden.shape[1]
    image, cross = lag_image(known[: out.shape[0]], hidden, ahead)
    out[:, :features] = image
    out[:, features:] = cross


def residual_kernel(feat, total, x, p, hidden, ahead, out):
    tokens, features = hidden.shape
    cols = x.shape[0]
    whole, at = tokens // LANES * LANES, padded(tokens + LAG)
    image = total[:, :features]
    residual = (image - times(total[:, features:], x[...])) * SMALL
    rounded = residual.astype(HALF)
    project_own(rounded, hidden, out)
    out[:, whole:at] = project_edge(rounded, hidden[whole:], ahead)
    both = jnp.concatenate([x[...], p[...]])
    products = exact(jnp.concatenate([residual, image]), both)
    share = total[:, features:] * (1.0 / feat)
    lacks = products[cols:] - jnp.concatenate([share, jnp.zeros_like(share)], axis=1)
    own = exact(jnp.concatenate([residual, residual]), residual)[:cols]
    own = jnp.concatenate([own, jnp.zeros_like(own)], axis=1)
    for value in (products[:cols], lacks, own):
        high, low = high_low(value)
        out[:, at : at + 2 * cols] = high
        out[:, at + 6 * cols : at + 8 * cols] = low
        at += 2 * cols


def found_kernel(wide, received, known, out):
    rows = received.shape[1]
    cols = known.shape[0] // 2
    total = jnp.sum(received[...].astype(FLOAT), axis=0)
    products = joined(total[:, wide:])
    lacks = products[:, 2 * cols : 3 * cols] * SMALL
    lacks = jnp.concatenate([lacks, jnp.zeros_like(lacks)]).astype(HALF)
    shift = jnp.dot(lacks, known[:cols, :wide], preferred_element_type=FLOAT)[:rows]
    high, low = high_low(products)
    total = jnp.concatenate([(total[:, :wide] - shift).astype(HALF), high, low], axis=1)
    out[...] = jnp.broadcast_to(total, out.shape)


def side_by_side(first, second):
    cols = first.shape[1] // 2
    left = lax.broadcasted_iota(jnp.int32, first.shape, 1) < cols
    return jnp.where(left, first, pltpu.roll(second, cols, 1))


def image_kernel(blocks, found, known, hidden, ahead, out):
    tokens, features = hidden.shape
    cols = found.shape[0]
    span = features // blocks
    wide = padded(tokens + LAG)
    image, cross = lag_image(jnp.concatenate([found[:, :wide], known[cols:, :wide]]), hidden, ahead)
    high = cross.astype(HALF).astype(FLOAT)
    low = cross - high
    pieces = [side_by_side(high, low), side_by_side(pltpu.roll(high, cols, 1), pltpu.roll(low, cols, 1))]
    groups = 2 * cols // 8
    for g in range(groups):
        for b in range(blocks):
            out[g * blocks + b, :, :span] = image[8 * g : 8 * g + 8, b * span : (b + 1) * span].astype(HALF)
    for k in range(out.shape[0]):
        if k < 2 * groups:
            g = k % groups
            out[k, :, span:] = pieces[k // groups][8 * g : 8 * g + 8].astype(HALF)
        else:
            out[k, :, span:] = jnp.zeros((8, 2 * cols), HALF)


def total_kernel(factor, cols, received, out):
    span = received.shape[2] - 2 * cols
    total = jnp.sum(received[...].astype(FLOAT), axis=0) * factor
    cross = total[:, span:]
    cross = cross + pltpu.roll(cross, cols, 1)
    high = cross.astype(HALF).astype(FLOAT)
    left = lax.broadcasted_iota(jnp.int32, cross.shape, 1) < cols
    cross = jnp.where(left, high, cross - high)
    total = jnp.concatenate([total[:, :span], cross], axis=1).astype(HALF)
    out[...] = jnp.broadcast_to(total, out.shape)


def inner_products(wide, first_total, found, known, search):
    cols = found.shape[0]
    products = joined(found[:, wide:])
    r_x, r_p, lacks, image_x_p, r_r = (products[:, i * cols : (i + 1) * cols] for i in range(5))
    products = joined(known[:, wide:])
    x_x, p_x, p_p = products[:cols, :cols], products[cols:, :cols], products[cols:, cols:]
    rayleigh_t = first_total[:, first_total.shape[1] - cols :] + lacks
    lacks = lacks * SMALL
    lacks_xx = times(lacks, x_x)
    r_r = r_r - exact(lacks, r_x) - exact(r_x, lacks) + exact(lacks_xx, lacks)
    r_x = r_x - lacks_xx
    r_p = r_p - exact(lacks, p_x)
    square = (cols, cols)
    eye = lax.broadcasted_iota(jnp.int32, square, 0) == lax.broadcasted_iota(jnp.int32, square, 1)
    lengths = jnp.where(eye, r_r, 0.0)

    def scaling(lengths):
        return lax.rsqrt(lengths * (1.0 / SMALL**2) + 1e-06) * (1.0 / SMALL)

    scale = scaling(jnp.sum(lengths, axis=1, keepdims=True))
    across = scaling(jnp.sum(lengths, axis=0, keepdims=True))
    u_image_x = (r_r * (1.0 / SMALL) + exact(r_x, rayleigh_t)) * scale
    u_x, u_p = r_x * scale, r_p * scale
    turned = exact(eye.astype(FLOAT), jnp.concatenate([rayleigh_t, u_image_x, image_x_p, u_x, p_x, u_p]))
    turned = [turned[:, i * cols : (i + 1) * cols] for i in range(6)]
    rows = [[x_x, turned[3], turned[4]], [u_x, r_r * scale * across, u_p], [p_x, turned[5], p_p]]
    for i, row in enumerate(rows):
        search[i * cols : (i + 1) * cols] = jnp.concatenate(row, axis=1)
    return scale, across, turned[:3], u_image_x, image_x_p


def last_kernel(blocks, wide, gathered, first_total, found, known, images, gram, search):
    cols = found.shape[0]
    scale, across, turned, u_image_x, image_x_p = inner_products(wide, first_total, found, known, search)
    features = images.shape[1]
    span = features // blocks
    groups = cols // 8
    images[:cols] = first_total[:, :features]
    for g in range(groups):
        for b in range(blocks):
            at = slice(b * span, (b + 1) * span)
            rows = slice(cols + 8 * g, cols + 8 * g + 8)
            images[rows, at] = gathered[g * blocks + b, :, :span].astype(FLOAT) * scale[8 * g : 8 * g + 8]
            rows = slice(2 * cols + 8 * g, 2 * cols + 8 * g + 8)
            images[rows, at] = gathered[(groups + g) * blocks + b, :, :span].astype(FLOAT)

    def piece(first):
        value = jnp.concatenate([gathered[k, :, span:].astype(FLOAT) for k in range(first, first + groups)])
        return (value + pltpu.roll(value, cols, 1))[:, :cols]

    rr, pr, rp, pp = (piece(i * groups) for i in range(4))
    rows = [
        [turned[0], turned[1], image_x_p],
        [u_image_x, rr * scale * across, rp * scale],
        [turned[2], pr * across, pp],
    ]
    for i, row in enumerate(rows):
        gram[i * cols : (i + 1) * cols] = jnp.concatenate(row, axis=1)


def local(hidden_states, current_block, directions):
    tokens, features = hidden_states.shape
    cols = current_block.shape[1]
    feat, tok = lax.axis_size("feat"), lax.axis_size("tok")
    factor = 0.5 / math.sqrt(tokens * tok - LAG)
    whole, wide = tokens // LANES * LANES, padded(tokens + LAG)
    blocks = tok * 8 // (2 * cols)

    ahead = lax.ppermute(hidden_states[:LAG], "tok", [(i + 1, i) for i in range(tok - 1)])
    x, p = current_block.T, directions.T

    total = wide + 4 * cols
    flat = shape((2 * cols, total), HALF)
    part = kernel_call(start_kernel, flat, x, p, hidden_states)
    part = kernel_call(functools.partial(edge_kernel, whole), flat, x, p, hidden_states[whole:], ahead, part)
    blocked = shape((feat, 2 * cols // feat, total), HALF)
    part = exchange(part.reshape(blocked.shape), "feat")
    part = kernel_call(functools.partial(known_kernel, wide), blocked, part)
    known = exchange(part, "feat").reshape(2 * cols, total)

    part = kernel_call(first_kernel, shape((cols, features + cols), FLOAT), known, hidden_states, ahead)
    part = exchange(part.reshape(tok, 1, -1), "tok")
    part = jnp.sum(part, axis=0) * factor
    part = exchange(jnp.broadcast_to(part, (tok,) + part.shape), "tok")
    first_total = part.reshape(cols, features + cols)

    total = wide + 12 * cols
    part = kernel_call(
        functools.partial(residual_kernel, feat), shape((cols, total), HALF), first_total, x, p, hidden_states, ahead
    )
    blocked = shape((feat, cols // feat, total), HALF)
    part = exchange(part.reshape(blocked.shape), "feat")
    part = kernel_call(functools.partial(found_kernel, wide), blocked, part, known)
    found = exchange(part, "feat").reshape(cols, total)

    blocked = shape((tok, 8, features // blocks + 2 * cols), HALF)
    part = kernel_call(functools.partial(image_kernel, blocks), blocked, found, known, hidden_states, ahead)
    part = exchange(part, "tok")
    part = kernel_call(functools.partial(total_kernel, factor, cols), blocked, part)
    gathered = exchange(part, "tok")
    gram = shape((3 * cols, 3 * cols), FLOAT)
    images, gram_image, gram_search = kernel_call(
        functools.partial(last_kernel, blocks, wide),
        [shape((3 * cols, features), FLOAT), gram, gram],
        gathered,
        first_total,
        found,
        known,
    )
    return (images.T, gram_image, gram_search)


def solution(mesh):
    return jax.shard_map(
        local,
        mesh=mesh,
        in_specs=(P("tok", "feat"), P("feat", None), P("feat", None)),
        out_specs=(P("feat", None), P(), P()),
        check_vma=False,
    )
```

time: 230 us -> 201 us (0.87)
  blocking collectives: 92.4 us -> 167 us
  waiting for transfers between devices: 51 us -> 8.5 us
  local copies, waits for them, and re-layouts: 34.9 us -> 10.1 us
  starting transfers between devices: 26.7 us -> 2.74 us
  matrix products: 5.62 us -> 0 us
  other arithmetic: 4.99 us -> 1.17 us
    all_to_all x4 -> x8, blocking collectives: 92.4 us -> 167 us  [exchange(): return lax.all_to_all(value, axis, 0, 0, tiled=True)]
    all_to_all x4 -> x0, waiting for transfers between devices: 41.9 us -> none  [exchange(): return lax.all_to_all(value, axis, 0, 0, tiled=True)]
    all_to_all x4 -> x0, starting transfers between devices: 20.6 us -> none  [exchange(): return lax.all_to_all(value, axis, 0, 0, tiled=True)]
    unnamed x57 -> x23, local copies, waits for them, and re-layouts: 20 us -> 7.68 us
    slice x8 -> x2, local copies, waits for them, and re-layouts: 10.2 us -> 2 us  [the longest x1 1.08 us: local(): hidden_states[:LAG]]
    dot_general x5 -> x0, matrix products: 5.62 us -> none  [times(): return jnp.dot(a, b, precision=HIGHEST, preferred_element_type=FLOAT)]
    ppermute x2 -> x1, starting transfers between devices: 6.12 us -> 2.74 us  [local(): lax.ppermute(hidden_states[:LAG], 'tok', [(i + 1, i) for i in range(tok -...]
    ppermute x2 -> x1, waiting for transfers between devices: 9.03 us -> 8.5 us  [local(): lax.ppermute(hidden_states[:LAG], 'tok', [(i + 1, i) for i in range(tok -...]
  transfers between devices with their start and end apart: 6 -> 1, of which waited for: 6 -> 1; matrix products, arithmetic and copies ran while one was open for 7% -> 0% of each run, Pallas kernels for 1% -> 1%
where the time goes in v4:
time: 201 us; the launch traced here: 200 us
  blocking collectives  167 us (83%)
  local copies, waits for them, and re-layouts  10.1 us (5%)
  Pallas kernels  9.53 us (5%)
  waiting for transfers between devices  8.5 us (4%)
  starting transfers between devices  2.74 us (1%)
    all_to_all x8, blocking collectives, exchange(): return lax.all_to_all(value, axis, 0, 0, tiled=True)  167 us
    pallas_call x9, Pallas kernels, kernel_call(): pl.pallas_call(body, out_shape=outputs, in_specs=[spec] * len(operands),...  9.53 us
    ppermute x1, waiting for transfers between devices, local(): lax.ppermute(hidden_states[:LAG], 'tok', [(i + 1, i) for i in range(tok -...  8.5 us
    unnamed x23, local copies, waits for them, and re-layouts  7.68 us
  transfers between devices with their start and end apart: 1, of which 1 were waited for; matrix products, arithmetic and copies ran while one was open for 0% of the time, Pallas kernels for 1%

profile of v4, /device:TPU:6, one launch (start us, length us, event | category | flops | bytes accessed | tf_op | source)
XLA Modules:
  0.0 199.8 jit_solution(8535530354205662592)
XLA Ops:
  0.6 1.1 slice.7
  1.7 2.7 %collective-permute-start = (bf16[256,1024]{1,0:T(8,128)(2,1)S(1)}, bf16[256,1024]{1,0:T(8,128)(2,1)S(1)}, u32[]{:S(2)}, u32[]{:S(2)}) collective-permute-start(bf16[256,1024]{1,0:T(8,128)(2,1)S(1)} %slice.7), channel_id=1, source_target_pairs={{8,0},{16,8},{24,16},{32,24},{40,32},{48,40},{56,48},{64,56},{72,6... | collective-permute-start | bytes 1572872 | tf_op jit(solution)/shard_map/ppermute | solution.py:265
  4.5 0.9 slice.6.tail
  5.4 0.0 copy-start
  5.4 2.0 copy-done
  7.4 0.0 copy-start.7
  7.4 0.9 copy-done.7
  8.3 0.0 copy-start.9
  8.3 0.9 copy-done.9
  9.3 1.6 shard_map.58.start
  10.9 0.0 copy-start.1
  10.9 8.5 %collective-permute-done.ahead = bf16[256,1024]{1,0:T(8,128)(2,1)S(1)} collective-permute-done((bf16[256,1024]{1,0:T(8,128)(2,1)S(1)}, bf16[256,1024]{1,0:T(8,128)(2,1)S(1)}, u32[]{:S(2)}, u32[]{:S(2)}) %collective-permute-start) | collective-permute-done | bytes 524320 | tf_op jit(solution)/shard_map/ppermute | solution.py:265
  19.4 0.0 copy-start.4
  19.4 0.4 shard_map.59
  19.8 29.9 %all_to_all.40.received = bf16[8,16,2304]{2,1,0:T(8,128)(2,1)S(1)} all-to-all(bf16[8,16,2304]{2,1,0:T(8,128)(2,1)S(1)} %bitcast.25), channel_id=1, replica_groups=mesh['tok'=64,'feat'=8] {'feat'}, dimensions={0} | all-to-all | bytes 1179648 | tf_op jit(solution)/shard_map/all_to_all | solution.py:24
  49.6 0.1 shard_map.60
  49.7 21.5 %all_to_all.41 = bf16[8,16,2304]{2,1,0:T(8,128)(2,1)S(1)} all-to-all(bf16[8,16,2304]{2,1,0:T(8,128)(2,1)S(1)} %shard_map.60), channel_id=1, replica_groups=mesh['tok'=64,'feat'=8] {'feat'}, dimensions={0} | all-to-all | bytes 1179648 | tf_op jit(solution)/shard_map/all_to_all | solution.py:24
  71.3 0.0 copy-done.1
  71.3 1.3 shard_map.61
  72.6 0.0 copy-done.4
  72.6 0.0 copy-start.2
  72.6 0.8 copy-done.2
  73.4 0.3 copy.6
  73.7 23.8 %all_to_all.42 = f32[64,1,1088]{2,1,0:T(1,128)} all-to-all(f32[64,1,1088]{2,1,0:T(1,128)S(1)} %copy.6), channel_id=1, replica_groups=mesh['tok'=64,'feat'=8] {'tok'}, dimensions={0} | all-to-all | bytes 557056 | tf_op jit(solution)/shard_map/all_to_all | solution.py:24
  97.5 1.2 reduce_sum.9
  98.7 0.2 broadcast_in_dim.3
  98.8 0.0 copy-start.3
  98.8 17.9 %all_to_all.43 = f32[64,1,1088]{2,1,0:T(1,128)S(1)} all-to-all(f32[64,1,1088]{2,1,0:T(1,128)S(1)} %broadcast_in_dim.3), channel_id=1, replica_groups=mesh['tok'=64,'feat'=8] {'tok'}, dimensions={0} | all-to-all | bytes 557056 | tf_op jit(solution)/shard_map/all_to_all | solution.py:24
  116.8 0.0 copy-start.5
  116.8 1.0 copy-done.5
  117.8 0.0 copy-start.8
  117.8 0.9 copy-done.8
  118.8 0.0 copy-start.10
  118.8 0.9 copy-done.10
  119.7 0.0 copy-start.6
  119.7 2.4 %shard_map.62 = bf16[64,2816]{1,0:T(8,128)(2,1)S(1)} custom-call(f32[64,1088]{1,0:T(8,128)S(1)} %bitcast.17, f32[64,1024]{1,0:T(8,128)S(1)} %bitcast.21, f32[64,1024]{1,0:T(8,128)S(1)} %bitcast.24, bf16[1728,1024]{1,0:T(8,128)(2,1)S(1)} %copy-done.1, bf16[256,1024]{1,0:T(8,128)(2,1)S(1)} %copy-done.5), custom_call_target="tpu_custom_call" | custom-call | tf_op jit(solution)/shard_map/pallas_call | solution.py:30
  122.1 16.3 %all_to_all.44.received = bf16[8,8,2816]{2,1,0:T(8,128)(2,1)S(1)} all-to-all(bf16[8,8,2816]{2,1,0:T(8,128)(2,1)S(1)} %bitcast.26), channel_id=1, replica_groups=mesh['tok'=64,'feat'=8] {'feat'}, dimensions={0} | all-to-all | bytes 720896 | tf_op jit(solution)/shard_map/all_to_all | solution.py:24
  138.4 0.0 copy-done.3
  138.4 0.2 shard_map.63
  138.6 17.1 %all_to_all.45 = bf16[8,8,2816]{2,1,0:T(8,128)(2,1)S(1)} all-to-all(bf16[8,8,2816]{2,1,0:T(8,128)(2,1)S(1)} %shard_map.63), channel_id=1, replica_groups=mesh['tok'=64,'feat'=8] {'feat'}, dimensions={0} | all-to-all | bytes 720896 | tf_op jit(solution)/shard_map/all_to_all | solution.py:24
  155.8 0.0 copy-done.6
  155.8 1.5 shard_map.64
  157.3 20.5 %all_to_all.46.received = bf16[64,8,384]{2,1,0:T(8,128)(2,1)S(1)} all-to-all(bf16[64,8,384]{2,1,0:T(8,128)(2,1)S(1)} %shard_map.64), channel_id=1, replica_groups=mesh['tok'=64,'feat'=8] {'tok'}, dimensions={0} | all-to-all | bytes 786432 | tf_op jit(solution)/shard_map/all_to_all | solution.py:24
  177.8 0.2 shard_map.65
  178.0 19.9 %all_to_all.47.gathered = bf16[64,8,384]{2,1,0:T(8,128)(2,1)S(1)} all-to-all(bf16[64,8,384]{2,1,0:T(8,128)(2,1)S(1)} %shard_map.65), channel_id=1, replica_groups=mesh['tok'=64,'feat'=8] {'tok'}, dimensions={0} | all-to-all | bytes 786432 | tf_op jit(solution)/shard_map/all_to_all | solution.py:24
  197.9 1.9 shard_map.66
  (2 shorter events, 0.0 us)
Async XLA Ops:
  1.7 17.7 %collective-permute-start = (bf16[256,1024]{1,0:T(8,128)(2,1)S(1)}, bf16[256,1024]{1,0:T(8,128)(2,1)S(1)}, u32[]{:S(2)}, u32[]{:S(2)}) collective-permute-start(bf16[256,1024]{1,0:T(8,128)(2,1)S(1)} %slice.7), channel_id=1, source_target_pairs={{8,0},{16,8},{24,16},{32,24},{40,32},{48,40},{56,48},{64,56},{72,6... | collective-permute-start | bytes 1572872 | tf_op jit(solution)/shard_map/ppermute | solution.py:265
  5.4 2.0 %copy-start = (bf16[1728,1024]{1,0:T(8,128)(2,1)S(1)}, bf16[1728,1024]{1,0:T(8,128)(2,1)}, u32[]{:S(2)}) copy-start(bf16[1728,1024]{1,0:T(8,128)(2,1)} %hidden.7) | copy-start | bytes 10616836
  7.4 0.9 copy-start.7
  8.3 0.9 copy-start.9
  10.9 60.4 %copy-start.1 = (bf16[1728,1024]{1,0:T(8,128)(2,1)S(1)}, bf16[1728,1024]{1,0:T(8,128)(2,1)}, u32[]{:S(2)}) copy-start(bf16[1728,1024]{1,0:T(8,128)(2,1)} %hidden.7) | copy-start | bytes 10616836
  19.4 53.2 %copy-start.4 = (bf16[256,1024]{1,0:T(8,128)(2,1)}, bf16[256,1024]{1,0:T(8,128)(2,1)S(1)}, u32[]{:S(2)}) copy-start(bf16[256,1024]{1,0:T(8,128)(2,1)S(1)} %collective-permute-done.ahead) | copy-start | bytes 1572868
  72.6 0.8 copy-start.2
  98.8 39.6 %copy-start.3 = (bf16[8,16,2304]{2,1,0:T(8,128)(2,1)S(1)}, bf16[8,16,2304]{2,1,0:T(8,128)(2,1)}, u32[]{:S(2)}) copy-start(bf16[8,16,2304]{2,1,0:T(8,128)(2,1)} %copy-done.2) | copy-start | bytes 1769476
  116.8 1.0 copy-start.5
  117.8 0.9 copy-start.8
  118.8 0.9 copy-start.10
  119.7 36.0 %copy-start.6 = (bf16[256,1024]{1,0:T(8,128)(2,1)S(1)}, bf16[256,1024]{1,0:T(8,128)(2,1)}, u32[]{:S(2)}) copy-start(bf16[256,1024]{1,0:T(8,128)(2,1)} %copy-done.4) | copy-start | bytes 1572868

commit v5 on v4

--- a/solution.py
+++ b/solution.py
@@ -24,14 +24,42 @@
     return lax.all_to_all(value, axis, 0, 0, tiled=True)
 
 
-def kernel_call(body, outputs, *operands):
+def kernel_call(body, outputs, *operands, far=0):
     many = isinstance(outputs, list)
-    spec = pl.BlockSpec(memory_space=pltpu.VMEM)
+    vmem, hbm = (pl.BlockSpec(memory_space=space) for space in (pltpu.VMEM, pltpu.HBM))
+    near, count = len(operands) - far, len(outputs) if many else 1
+
+    def kernel(*refs):
+        sources, rest = refs[near : len(operands)], refs[len(operands) :]
+        if not far:
+            return body(*refs)
+        buffers, semaphores = rest[count:-1], rest[-1]
+        copies = [
+            pltpu.make_async_copy(source, buffer, semaphores.at[i])
+            for i, (source, buffer) in enumerate(zip(sources, buffers))
+        ]
+        for copy in copies:
+            copy.start()
+        arrived = set()
+
+        def waiting(i):
+            def ref():
+                if i not in arrived:
+                    arrived.add(i)
+                    copies[i].wait()
+                return buffers[i]
+
+            return ref
+
+        body(*refs[:near], *[waiting(i) for i in range(far)], *rest[:count])
+
+    scratch = [pltpu.VMEM(value.shape, value.dtype) for value in operands[near:]]
     return pl.pallas_call(
-        body,
+        kernel,
         out_shape=outputs,
-        in_specs=[spec] * len(operands),
-        out_specs=[spec] * len(outputs) if many else spec,
+        in_specs=[vmem] * near + [hbm] * far,
+        out_specs=[vmem] * count if many else vmem,
+        scratch_shapes=scratch + [pltpu.SemaphoreType.DMA((far,))] if far else [],
         compiler_params=pltpu.CompilerParams(vmem_limit_bytes=16 * 2**20),
     )(*operands)
 
@@ -77,22 +105,35 @@
     return value
 
 
-def start_kernel(x, p, hidden, out):
-    cols = x.shape[0]
-    wide = out.shape[1] - 4 * cols
-    both = jnp.concatenate([x[...], p[...]])
-    project_own(both.astype(HALF), hidden, out)
-    high, low = high_low(exact(both, both))
-    out[:, wide : wide + 2 * cols] = high
-    out[:, wide + 2 * cols :] = low
-
-
-def edge_kernel(whole, x, p, tail, ahead, start, out):
-    wide = out.shape[1] - 4 * x.shape[0]
+def start_kernel(both, hidden, out, first):
+    both = both[...]
+    rounded = both.astype(HALF)
+    whole = hidden.shape[0] // LANES * LANES
+    wide = out.shape[1] - 2 * both.shape[0]
+    products = exact(both, both)
+    edge = rows_dot(rounded, hidden[:LAG]).astype(HALF)
+    first[...] = edge
+    out[:, :LAG] = edge
+    out[:, LAG:whole] = rows_dot(rounded, hidden[LAG:whole]).astype(HALF)
+    rest = hidden.shape[0] - whole
+    if rest:
+        tail = rows_dot(rounded, jnp.concatenate([hidden[whole:], hidden[: LANES - rest]])).astype(HALF)
+        out[:, whole : whole + LANES] = tail
+    high, low = high_low(products)
+    out[:, wide : wide + high.shape[1]] = high
+    out[:, wide + high.shape[1] :] = low
+
+
+def edge_kernel(tokens, start, ahead, out):
+    rows, whole = start.shape[0], tokens // LANES * LANES
+    wide = padded(tokens + LAG)
     out[:, :whole] = start[:, :whole]
     out[:, wide:] = start[:, wide:]
-    both = jnp.concatenate([x[...], p[...]]).astype(HALF)
-    out[:, whole:wide] = project_edge(both, tail[...], ahead)
+    pieces = [start[:, whole : whole + LANES][:, : tokens - whole]] if tokens > whole else []
+    pieces.append(ahead[...])
+    if wide > tokens + LAG:
+        pieces.append(jnp.zeros((rows, wide - tokens - LAG), HALF))
+    out[:, whole:wide] = jnp.concatenate(pieces, axis=1)
 
 
 def known_kernel(wide, received, out):
@@ -106,11 +147,12 @@
     tokens = hidden.shape[0]
     cut = tokens // LANES * LANES - LAG
     here, later = projected[:, :tokens], projected[:, LAG : LAG + tokens]
-    edge = jnp.concatenate([hidden[cut + LAG :], ahead[...]])
     image = jnp.dot(later, hidden[...], preferred_element_type=FLOAT)
     image += jnp.dot(here[:, :cut], hidden[LAG : LAG + cut], preferred_element_type=FLOAT)
+    cross = rows_dot(later, here) + rows_dot(here, later)
+    edge = jnp.concatenate([hidden[cut + LAG :], ahead()[...]])
     image += jnp.dot(here[:, cut:], edge, preferred_element_type=FLOAT)
-    return image, rows_dot(later, here) + rows_dot(here, later)
+    return image, cross
 
 
 def first_kernel(known, hidden, ahead, out):
@@ -120,21 +162,20 @@
     out[:, features:] = cross
 
 
-def residual_kernel(feat, total, x, p, hidden, ahead, out):
+def residual_kernel(feat, total, hidden, both, ahead, out):
     tokens, features = hidden.shape
-    cols = x.shape[0]
+    cols = total.shape[0]
     whole, at = tokens // LANES * LANES, padded(tokens + LAG)
     image = total[:, :features]
-    residual = (image - times(total[:, features:], x[...])) * SMALL
+    residual = (image - times(total[:, features:], both[:cols])) * SMALL
     rounded = residual.astype(HALF)
     project_own(rounded, hidden, out)
-    out[:, whole:at] = project_edge(rounded, hidden[whole:], ahead)
-    both = jnp.concatenate([x[...], p[...]])
-    products = exact(jnp.concatenate([residual, image]), both)
+    products = exact(jnp.concatenate([residual, image]), both[...])
+    own = exact(jnp.concatenate([residual, residual]), residual)[:cols]
+    own = jnp.concatenate([own, jnp.zeros_like(own)], axis=1)
+    out[:, whole:at] = project_edge(rounded, hidden[whole:], ahead())
     share = total[:, features:] * (1.0 / feat)
     lacks = products[cols:] - jnp.concatenate([share, jnp.zeros_like(share)], axis=1)
-    own = exact(jnp.concatenate([residual, residual]), residual)[:cols]
-    own = jnp.concatenate([own, jnp.zeros_like(own)], axis=1)
     for value in (products[:cols], lacks, own):
         high, low = high_low(value)
         out[:, at : at + 2 * cols] = high
@@ -259,22 +300,28 @@
     cols = current_block.shape[1]
     feat, tok = lax.axis_size("feat"), lax.axis_size("tok")
     factor = 0.5 / math.sqrt(tokens * tok - LAG)
-    whole, wide = tokens // LANES * LANES, padded(tokens + LAG)
+    wide = padded(tokens + LAG)
     blocks = tok * 8 // (2 * cols)
 
-    ahead = lax.ppermute(hidden_states[:LAG], "tok", [(i + 1, i) for i in range(tok - 1)])
-    x, p = current_block.T, directions.T
+    down = [(i + 1, i) for i in range(tok - 1)]
+    both = jnp.concatenate([current_block.T, directions.T])
 
     total = wide + 4 * cols
     flat = shape((2 * cols, total), HALF)
-    part = kernel_call(start_kernel, flat, x, p, hidden_states)
-    part = kernel_call(functools.partial(edge_kernel, whole), flat, x, p, hidden_states[whole:], ahead, part)
+    part, edge = kernel_call(
+        start_kernel, [flat, shape((2 * cols, LAG), HALF)], both, hidden_states
+    )
+    edge = lax.ppermute(edge, "tok", down)
+    rows, edge = lax.optimization_barrier((hidden_states[:LAG], edge))
+    ahead = lax.ppermute(rows, "tok", down)
+    part = kernel_call(functools.partial(edge_kernel, tokens), flat, part, edge)
     blocked = shape((feat, 2 * cols // feat, total), HALF)
     part = exchange(part.reshape(blocked.shape), "feat")
     part = kernel_call(functools.partial(known_kernel, wide), blocked, part)
+    part, ahead = lax.optimization_barrier((part, ahead))
     known = exchange(part, "feat").reshape(2 * cols, total)
 
-    part = kernel_call(first_kernel, shape((cols, features + cols), FLOAT), known, hidden_states, ahead)
+    part = kernel_call(first_kernel, shape((cols, features + cols), FLOAT), known, hidden_states, ahead, far=1)
     part = exchange(part.reshape(tok, 1, -1), "tok")
     part = jnp.sum(part, axis=0) * factor
     part = exchange(jnp.broadcast_to(part, (tok,) + part.shape), "tok")
@@ -282,7 +329,7 @@
 
     total = wide + 12 * cols
     part = kernel_call(
-        functools.partial(residual_kernel, feat), shape((cols, total), HALF), first_total, x, p, hidden_states, ahead
+        functools.partial(residual_kernel, feat), shape((cols, total), HALF), first_total, hidden_states, both, ahead, far=1
     )
     blocked = shape((feat, cols // feat, total), HALF)
     part = exchange(part.reshape(blocked.shape), "feat")
@@ -290,7 +337,7 @@
     found = exchange(part, "feat").reshape(cols, total)
 
     blocked = shape((tok, 8, features // blocks + 2 * cols), HALF)
-    part = kernel_call(functools.partial(image_kernel, blocks), blocked, found, known, hidden_states, ahead)
+    part = kernel_call(functools.partial(image_kernel, blocks), blocked, found, known, hidden_states, ahead, far=1)
     part = exchange(part, "tok")
     part = kernel_call(functools.partial(total_kernel, factor, cols), blocked, part)
     gathered = exchange(part, "tok")

time: 201 us -> 203 us (level)
  blocking collectives: 167 us -> 138 us
  waiting for transfers between devices: 8.5 us -> 26.8 us
  starting transfers between devices: 2.74 us -> 15.2 us
  local copies, waits for them, and re-layouts: 10.1 us -> 5.98 us
  Pallas kernels: 9.53 us -> 12.8 us
    all_to_all x8 -> x7, blocking collectives: 167 us -> 138 us  [exchange(): return lax.all_to_all(value, axis, 0, 0, tiled=True)]
    all_to_all x0 -> x1, waiting for transfers between devices: none -> 18 us  [exchange(): return lax.all_to_all(value, axis, 0, 0, tiled=True)]
    all_to_all x0 -> x1, starting transfers between devices: none -> 10.3 us  [exchange(): return lax.all_to_all(value, axis, 0, 0, tiled=True)]
    pallas_call x9, Pallas kernels: 9.53 us -> 12.8 us  [kernel_call(): pl.pallas_call(kernel, out_shape=outputs, in_specs=[vmem] * near + [hbm]...]
    unnamed x23 -> x15, local copies, waits for them, and re-layouts: 7.68 us -> 4.69 us
    ppermute x1 -> x2, starting transfers between devices: 2.74 us -> 4.91 us  [the longest x1 3 us: local(): edge = lax.ppermute(edge, 'tok', down)]
    ppermute x1 -> x2, waiting for transfers between devices: 8.5 us -> 8.87 us  [the longest x1 4.69 us: local(): edge = lax.ppermute(edge, 'tok', down)]
  transfers between devices with their start and end apart: 1 -> 3, of which waited for: 1 -> 3; matrix products, arithmetic and copies ran while one was open for 0% -> 0% of each run, Pallas kernels for 1% -> 1%
where the time goes in v5:
time: 203 us; the launch traced here: 202 us
  blocking collectives  138 us (68%)
  waiting for transfers between devices  26.8 us (13%)
  starting transfers between devices  15.2 us (7%)
  Pallas kernels  12.8 us (6%)
  local copies, waits for them, and re-layouts  5.98 us (3%)
  other arithmetic  2.24 us (1%)
    all_to_all x7, blocking collectives, exchange(): return lax.all_to_all(value, axis, 0, 0, tiled=True)  138 us
    all_to_all x1, waiting for transfers between devices, exchange(): return lax.all_to_all(value, axis, 0, 0, tiled=True)  18 us
    pallas_call x9, Pallas kernels, kernel_call(): pl.pallas_call(kernel, out_shape=outputs, in_specs=[vmem] * near + [hbm]...  12.8 us
    all_to_all x1, starting transfers between devices, exchange(): return lax.all_to_all(value, axis, 0, 0, tiled=True)  10.3 us
    ppermute x1, waiting for transfers between devices, local(): edge = lax.ppermute(edge, 'tok', down)  4.69 us
    unnamed x15, local copies, waits for them, and re-layouts  4.69 us
    ppermute x1, waiting for transfers between devices, local(): ahead = lax.ppermute(rows, 'tok', down)  4.18 us
  transfers between devices with their start and end apart: 3, of which 3 were waited for; matrix products, arithmetic and copies ran while one was open for 0% of the time, Pallas kernels for 1%

profile of v5, /device:TPU:6, one launch (start us, length us, event | category | flops | bytes accessed | tf_op | source)
XLA Modules:
  0.0 202.2 jit_solution(5208797461241684102)
XLA Ops:
  0.6 1.1 pad_maximum_fusion.refs_0_.refs_2_
  1.7 0.0 copy-start
  1.7 2.0 copy-done
  3.7 0.0 copy-start.4
  3.7 1.6 shard_map.58
  5.3 0.0 copy-start.1
  5.4 3.0 %collective-permute-start = (bf16[128,256]{1,0:T(8,128)(2,1)S(1)}, bf16[128,256]{1,0:T(8,128)(2,1)S(1)}, u32[]{:S(2)}, u32[]{:S(2)}) collective-permute-start(bf16[128,256]{1,0:T(8,128)(2,1)S(1)} %get-tuple-element.13), channel_id=1, source_target_pairs={{8,0},{16,8},{24,16},{32,24},{40,32},{48,40},{56,48},{64,56},{72,6... | collective-permute-start | bytes 196616 | tf_op jit(solution)/shard_map/ppermute | solution.py:314
  8.4 0.8 slice.3
  9.2 0.0 copy-done.4
  9.2 4.7 %collective-permute-done.refs_1_ = bf16[128,256]{1,0:T(8,128)(2,1)S(1)} collective-permute-done((bf16[128,256]{1,0:T(8,128)(2,1)S(1)}, bf16[128,256]{1,0:T(8,128)(2,1)S(1)}, u32[]{:S(2)}, u32[]{:S(2)}) %collective-permute-start) | collective-permute-done | bytes 65568 | tf_op jit(solution)/shard_map/ppermute | solution.py:314
  13.9 0.1 shard_map.59
  14.0 0.0 copy-start.6
  14.0 0.8 copy-done.6
  14.8 10.3 %all-to-all-start = ((bf16[8,16,2304]{2,1,0:T(8,128)(2,1)}), bf16[8,16,2304]{2,1,0:T(8,128)(2,1)}, u32[]{:S(2)}, u32[]{:S(2)}) async-start(bf16[8,16,2304]{2,1,0:T(8,128)(2,1)} %bitcast.19), calls=%async_computation | async-start | bytes 1179648 | tf_op jit(solution)/shard_map/all_to_all | solution.py:24
  25.1 1.9 collective-permute-start.1
  27.0 18.0 %all-to-all-done.refs_0_ = bf16[8,16,2304]{2,1,0:T(8,128)(2,1)} async-done(((bf16[8,16,2304]{2,1,0:T(8,128)(2,1)}), bf16[8,16,2304]{2,1,0:T(8,128)(2,1)}, u32[]{:S(2)}, u32[]{:S(2)}) %all-to-all-start) | async-done | bytes 589856 | tf_op jit(solution)/shard_map/all_to_all | solution.py:24
  45.0 1.1 shard_map.60
  46.1 4.2 %collective-permute-done.1.refs_2_.refs_3_ = bf16[256,1024]{1,0:T(8,128)(2,1)} collective-permute-done((bf16[256,1024]{1,0:T(8,128)(2,1)}, bf16[256,1024]{1,0:T(8,128)(2,1)}, u32[]{:S(2)}, u32[]{:S(2)}) %collective-permute-start.1) | collective-permute-done | bytes 524320 | tf_op jit(solution)/shard_map/ppermute | solution.py:316
  50.3 24.0 %all_to_all.40 = bf16[8,16,2304]{2,1,0:T(8,128)(2,1)S(1)} all-to-all(bf16[8,16,2304]{2,1,0:T(8,128)(2,1)S(1)} %shard_map.60), channel_id=1, replica_groups=mesh['tok'=64,'feat'=8] {'feat'}, dimensions={0} | all-to-all | bytes 1179648 | tf_op jit(solution)/shard_map/all_to_all | solution.py:24
  74.3 0.0 copy-done.1
  74.3 2.5 %shard_map.61 = f32[64,1088]{1,0:T(8,128)S(1)} custom-call(bf16[128,2304]{1,0:T(8,128)(2,1)S(1)} %bitcast.11, bf16[1728,1024]{1,0:T(8,128)(2,1)S(1)} %copy-done.1, bf16[256,1024]{1,0:T(8,128)(2,1)} %collective-permute-done.1.refs_2_.refs_3_), custom_call_target="tpu_custom_call" | custom-call | tf_op jit(solution)/shard_map/pallas_call | solution.py:57
  76.8 0.0 copy-start.2
  76.8 0.8 copy-done.2
  77.6 0.3 copy.6
  77.9 22.3 %all_to_all.41 = f32[64,1,1088]{2,1,0:T(1,128)} all-to-all(f32[64,1,1088]{2,1,0:T(1,128)S(1)} %copy.6), channel_id=1, replica_groups=mesh['tok'=64,'feat'=8] {'tok'}, dimensions={0} | all-to-all | bytes 557056 | tf_op jit(solution)/shard_map/all_to_all | solution.py:24
  100.2 1.2 reduce_sum.9
  101.3 0.2 broadcast_in_dim.3
  101.5 0.0 copy-start.3
  101.5 17.9 %all_to_all.42 = f32[64,1,1088]{2,1,0:T(1,128)S(1)} all-to-all(f32[64,1,1088]{2,1,0:T(1,128)S(1)} %broadcast_in_dim.3), channel_id=1, replica_groups=mesh['tok'=64,'feat'=8] {'tok'}, dimensions={0} | all-to-all | bytes 557056 | tf_op jit(solution)/shard_map/all_to_all | solution.py:24
  119.4 0.0 copy-start.5
  119.4 1.0 copy-done.5
  120.5 2.7 %shard_map.62 = bf16[64,2816]{1,0:T(8,128)(2,1)S(1)} custom-call(f32[64,1088]{1,0:T(8,128)S(1)} %bitcast.17, bf16[1728,1024]{1,0:T(8,128)(2,1)S(1)} %copy-done.1, f32[128,1024]{1,0:T(8,128)S(1)} %copy-done.5, bf16[256,1024]{1,0:T(8,128)(2,1)} %collective-permute-done.1.refs_2_.refs_3_), custom_call_target="tpu_custom_call" | custom-call | tf_op jit(solution)/shard_map/pallas_call | solution.py:57
  123.2 16.7 %all_to_all.43.refs_0_ = bf16[8,8,2816]{2,1,0:T(8,128)(2,1)S(1)} all-to-all(bf16[8,8,2816]{2,1,0:T(8,128)(2,1)S(1)} %bitcast.20), channel_id=1, replica_groups=mesh['tok'=64,'feat'=8] {'feat'}, dimensions={0} | all-to-all | bytes 720896 | tf_op jit(solution)/shard_map/all_to_all | solution.py:24
  139.9 0.0 copy-done.3
  139.9 0.2 shard_map.63
  140.1 17.1 %all_to_all.44 = bf16[8,8,2816]{2,1,0:T(8,128)(2,1)S(1)} all-to-all(bf16[8,8,2816]{2,1,0:T(8,128)(2,1)S(1)} %shard_map.63), channel_id=1, replica_groups=mesh['tok'=64,'feat'=8] {'feat'}, dimensions={0} | all-to-all | bytes 720896 | tf_op jit(solution)/shard_map/all_to_all | solution.py:24
  157.2 2.5 %shard_map.64 = bf16[64,8,384]{2,1,0:T(8,128)(2,1)S(1)} custom-call(bf16[64,2816]{1,0:T(8,128)(2,1)S(1)} %bitcast.15, bf16[128,2304]{1,0:T(8,128)(2,1)S(1)} %bitcast.13, bf16[1728,1024]{1,0:T(8,128)(2,1)S(1)} %copy-done.1, bf16[256,1024]{1,0:T(8,128)(2,1)} %collective-permute-done.1.refs_2_.refs_3_), custom_call_target="tpu_custom_call" | custom-call | tf_op jit(solution)/shard_map/pallas_call | solution.py:57
  159.8 20.5 %all_to_all.45.refs_0_ = bf16[64,8,384]{2,1,0:T(8,128)(2,1)S(1)} all-to-all(bf16[64,8,384]{2,1,0:T(8,128)(2,1)S(1)} %shard_map.64), channel_id=1, replica_groups=mesh['tok'=64,'feat'=8] {'tok'}, dimensions={0} | all-to-all | bytes 786432 | tf_op jit(solution)/shard_map/all_to_all | solution.py:24
  180.3 0.2 shard_map.65
  180.5 19.9 %all_to_all.46.refs_0_ = bf16[64,8,384]{2,1,0:T(8,128)(2,1)S(1)} all-to-all(bf16[64,8,384]{2,1,0:T(8,128)(2,1)S(1)} %shard_map.65), channel_id=1, replica_groups=mesh['tok'=64,'feat'=8] {'tok'}, dimensions={0} | all-to-all | bytes 786432 | tf_op jit(solution)/shard_map/all_to_all | solution.py:24
  200.4 1.9 shard_map.66
  (2 shorter events, 0.0 us)
Async XLA Ops:
  1.7 2.0 copy-start
  3.7 5.5 %copy-start.4 = (f32[128,1024]{1,0:T(8,128)}, f32[128,1024]{1,0:T(8,128)S(1)}, u32[]{:S(2)}) copy-start(f32[128,1024]{1,0:T(8,128)S(1)} %pad_maximum_fusion.refs_0_.refs_2_) | copy-start | bytes 1572868
  5.3 68.9 %copy-start.1 = (bf16[1728,1024]{1,0:T(8,128)(2,1)S(1)}, bf16[1728,1024]{1,0:T(8,128)(2,1)}, u32[]{:S(2)}) copy-start(bf16[1728,1024]{1,0:T(8,128)(2,1)} %refs_2_.1) | copy-start | bytes 10616836
  5.4 8.5 %collective-permute-start = (bf16[128,256]{1,0:T(8,128)(2,1)S(1)}, bf16[128,256]{1,0:T(8,128)(2,1)S(1)}, u32[]{:S(2)}, u32[]{:S(2)}) collective-permute-start(bf16[128,256]{1,0:T(8,128)(2,1)S(1)} %get-tuple-element.13), channel_id=1, source_target_pairs={{8,0},{16,8},{24,16},{32,24},{40,32},{48,40},{56,48},{64,56},{72,6... | collective-permute-start | bytes 196616 | tf_op jit(solution)/shard_map/ppermute | solution.py:314
  14.0 0.8 copy-start.6
  14.8 30.2 %all-to-all-start = ((bf16[8,16,2304]{2,1,0:T(8,128)(2,1)}), bf16[8,16,2304]{2,1,0:T(8,128)(2,1)}, u32[]{:S(2)}, u32[]{:S(2)}) async-start(bf16[8,16,2304]{2,1,0:T(8,128)(2,1)} %bitcast.19), calls=%async_computation | async-start | bytes 1179648 | tf_op jit(solution)/shard_map/all_to_all | solution.py:24
  25.1 25.2 %collective-permute-start.1 = (bf16[256,1024]{1,0:T(8,128)(2,1)}, bf16[256,1024]{1,0:T(8,128)(2,1)}, u32[]{:S(2)}, u32[]{:S(2)}) collective-permute-start(bf16[256,1024]{1,0:T(8,128)(2,1)} %slice.3), channel_id=1, source_target_pairs={{8,0},{16,8},{24,16},{32,24},{40,32},{48,40},{56,48},{64,56},{72,6... | collective-permute-start | bytes 1572872 | tf_op jit(solution)/shard_map/ppermute | solution.py:316
  76.8 0.8 copy-start.2
  101.5 38.4 %copy-start.3 = (bf16[8,16,2304]{2,1,0:T(8,128)(2,1)S(1)}, bf16[8,16,2304]{2,1,0:T(8,128)(2,1)}, u32[]{:S(2)}) copy-start(bf16[8,16,2304]{2,1,0:T(8,128)(2,1)} %copy-done.2) | copy-start | bytes 1769476
  119.4 1.0 copy-start.5

commit v6 on v5

--- a/solution.py
+++ b/solution.py
@@ -24,42 +24,14 @@
     return lax.all_to_all(value, axis, 0, 0, tiled=True)
 
 
-def kernel_call(body, outputs, *operands, far=0):
+def kernel_call(body, outputs, *operands):
     many = isinstance(outputs, list)
-    vmem, hbm = (pl.BlockSpec(memory_space=space) for space in (pltpu.VMEM, pltpu.HBM))
-    near, count = len(operands) - far, len(outputs) if many else 1
-
-    def kernel(*refs):
-        sources, rest = refs[near : len(operands)], refs[len(operands) :]
-        if not far:
-            return body(*refs)
-        buffers, semaphores = rest[count:-1], rest[-1]
-        copies = [
-            pltpu.make_async_copy(source, buffer, semaphores.at[i])
-            for i, (source, buffer) in enumerate(zip(sources, buffers))
-        ]
-        for copy in copies:
-            copy.start()
-        arrived = set()
-
-        def waiting(i):
-            def ref():
-                if i not in arrived:
-                    arrived.add(i)
-                    copies[i].wait()
-                return buffers[i]
-
-            return ref
-
-        body(*refs[:near], *[waiting(i) for i in range(far)], *rest[:count])
-
-    scratch = [pltpu.VMEM(value.shape, value.dtype) for value in operands[near:]]
+    spec = pl.BlockSpec(memory_space=pltpu.VMEM)
     return pl.pallas_call(
-        kernel,
+        body,
         out_shape=outputs,
-        in_specs=[vmem] * near + [hbm] * far,
-        out_specs=[vmem] * count if many else vmem,
-        scratch_shapes=scratch + [pltpu.SemaphoreType.DMA((far,))] if far else [],
+        in_specs=[spec] * len(operands),
+        out_specs=[spec] * len(outputs) if many else spec,
         compiler_params=pltpu.CompilerParams(vmem_limit_bytes=16 * 2**20),
     )(*operands)
 
@@ -150,7 +122,7 @@
     image = jnp.dot(later, hidden[...], preferred_element_type=FLOAT)
     image += jnp.dot(here[:, :cut], hidden[LAG : LAG + cut], preferred_element_type=FLOAT)
     cross = rows_dot(later, here) + rows_dot(here, later)
-    edge = jnp.concatenate([hidden[cut + LAG :], ahead()[...]])
+    edge = jnp.concatenate([hidden[cut + LAG :], ahead[...]])
     image += jnp.dot(here[:, cut:], edge, preferred_element_type=FLOAT)
     return image, cross
 
@@ -160,6 +132,11 @@
     image, cross = lag_image(known[: out.shape[0]], hidden, ahead)
     out[:, :features] = image
     out[:, features:] = cross
+
+
+def spread_kernel(factor, received, out):
+    total = jnp.sum(received[...], axis=0, keepdims=True) * factor
+    out[...] = jnp.broadcast_to(total, out.shape)
 
 
 def residual_kernel(feat, total, hidden, both, ahead, out):
@@ -173,7 +150,7 @@
     products = exact(jnp.concatenate([residual, image]), both[...])
     own = exact(jnp.concatenate([residual, residual]), residual)[:cols]
     own = jnp.concatenate([own, jnp.zeros_like(own)], axis=1)
-    out[:, whole:at] = project_edge(rounded, hidden[whole:], ahead())
+    out[:, whole:at] = project_edge(rounded, hidden[whole:], ahead)
     share = total[:, features:] * (1.0 / feat)
     lacks = products[cols:] - jnp.concatenate([share, jnp.zeros_like(share)], axis=1)
     for value in (products[:cols], lacks, own):
@@ -318,18 +295,18 @@
     blocked = shape((feat, 2 * cols // feat, total), HALF)
     part = exchange(part.reshape(blocked.shape), "feat")
     part = kernel_call(functools.partial(known_kernel, wide), blocked, part)
-    part, ahead = lax.optimization_barrier((part, ahead))
     known = exchange(part, "feat").reshape(2 * cols, total)
 
-    part = kernel_call(first_kernel, shape((cols, features + cols), FLOAT), known, hidden_states, ahead, far=1)
-    part = exchange(part.reshape(tok, 1, -1), "tok")
-    part = jnp.sum(part, axis=0) * factor
-    part = exchange(jnp.broadcast_to(part, (tok,) + part.shape), "tok")
+    part = kernel_call(first_kernel, shape((cols, features + cols), FLOAT), known, hidden_states, ahead)
+    flat = shape((tok, cols * (features + cols) // tok), FLOAT)
+    part = exchange(part.reshape(flat.shape), "tok")
+    part = kernel_call(functools.partial(spread_kernel, factor), flat, part)
+    part = exchange(part, "tok")
     first_total = part.reshape(cols, features + cols)
 
     total = wide + 12 * cols
     part = kernel_call(
-        functools.partial(residual_kernel, feat), shape((cols, total), HALF), first_total, hidden_states, both, ahead, far=1
+        functools.partial(residual_kernel, feat), shape((cols, total), HALF), first_total, hidden_states, both, ahead
     )
     blocked = shape((feat, cols // feat, total), HALF)
     part = exchange(part.reshape(blocked.shape), "feat")
@@ -337,7 +314,7 @@
     found = exchange(part, "feat").reshape(cols, total)
 
     blocked = shape((tok, 8, features // blocks + 2 * cols), HALF)
-    part = kernel_call(functools.partial(image_kernel, blocks), blocked, found, known, hidden_states, ahead, far=1)
+    part = kernel_call(functools.partial(image_kernel, blocks), blocked, found, known, hidden_states, ahead)
     part = exchange(part, "tok")
     part = kernel_call(functools.partial(total_kernel, factor, cols), blocked, part)
     gathered = exchange(part, "tok")

time: 203 us -> 207 us (1.020)
  blocking collectives: 138 us -> 149 us
  starting transfers between devices: 15.2 us -> 9.11 us
    all_to_all x1, waiting for transfers between devices: 18 us -> 0.01 us  [exchange(): return lax.all_to_all(value, axis, 0, 0, tiled=True)]
    ppermute x1, waiting for transfers between devices: 4.18 us -> 21.9 us  [local(): ahead = lax.ppermute(rows, 'tok', down)]
    all_to_all x7, blocking collectives: 138 us -> 149 us  [exchange(): return lax.all_to_all(value, axis, 0, 0, tiled=True)]
    all_to_all x1, starting transfers between devices: 10.3 us -> 4.19 us  [exchange(): return lax.all_to_all(value, axis, 0, 0, tiled=True)]
    pallas_call x9 -> x10, Pallas kernels: 12.8 us -> 13.6 us  [kernel_call(): pl.pallas_call(body, out_shape=outputs, in_specs=[spec] * len(operands),...]
    unnamed x15 -> x18, local copies, waits for them, and re-layouts: 4.69 us -> 4.72 us
  transfers between devices with their start and end apart: 3 -> 3, of which waited for: 3 -> 2; matrix products, arithmetic and copies ran while one was open for 0% -> 0% of each run, Pallas kernels for 1% -> 0%
where the time goes in v6:
time: 207 us
  blocking collectives  149 us (72%)
  waiting for transfers between devices  26.6 us (13%)
  Pallas kernels  13.6 us (7%)
  starting transfers between devices  9.11 us (4%)
  local copies, waits for them, and re-layouts  6.19 us (3%)
    all_to_all x7, blocking collectives, exchange(): return lax.all_to_all(value, axis, 0, 0, tiled=True)  149 us
    ppermute x1, waiting for transfers between devices, local(): ahead = lax.ppermute(rows, 'tok', down)  21.9 us
    pallas_call x10, Pallas kernels, kernel_call(): pl.pallas_call(body, out_shape=outputs, in_specs=[spec] * len(operands),...  13.6 us
    unnamed x18, local copies, waits for them, and re-layouts  4.72 us
    ppermute x1, waiting for transfers between devices, local(): edge = lax.ppermute(edge, 'tok', down)  4.67 us
    all_to_all x1, starting transfers between devices, exchange(): return lax.all_to_all(value, axis, 0, 0, tiled=True)  4.19 us
  transfers between devices with their start and end apart: 3, of which 2 were waited for; matrix products, arithmetic and copies ran while one was open for 0% of the time, Pallas kernels for 0%

profile of v6, /device:TPU:6, one launch (start us, length us, event | category | flops | bytes accessed | tf_op | source)
XLA Modules:
  0.0 206.6 jit_solution(3827226316757745607)
XLA Ops:
  0.6 1.1 pad_maximum_fusion.both
  1.7 0.0 copy-start
  1.7 2.0 copy-done
  3.7 0.0 copy-start.5
  3.7 1.6 shard_map.58
  5.3 0.0 copy-start.1
  5.4 3.0 %collective-permute-start = (bf16[128,256]{1,0:T(8,128)(2,1)S(1)}, bf16[128,256]{1,0:T(8,128)(2,1)S(1)}, u32[]{:S(2)}, u32[]{:S(2)}) collective-permute-start(bf16[128,256]{1,0:T(8,128)(2,1)S(1)} %get-tuple-element.11), channel_id=1, source_target_pairs={{8,0},{16,8},{24,16},{32,24},{40,32},{48,40},{56,48},{64,56},{72,6... | collective-permute-start | bytes 196616 | tf_op jit(solution)/shard_map/ppermute | solution.py:291
  8.4 0.9 slice.3
  9.2 0.0 copy-done.5
  9.2 4.7 %collective-permute-done.ahead = bf16[128,256]{1,0:T(8,128)(2,1)S(1)} collective-permute-done((bf16[128,256]{1,0:T(8,128)(2,1)S(1)}, bf16[128,256]{1,0:T(8,128)(2,1)S(1)}, u32[]{:S(2)}, u32[]{:S(2)}) %collective-permute-start) | collective-permute-done | bytes 65568 | tf_op jit(solution)/shard_map/ppermute | solution.py:291
  13.9 0.1 shard_map.59
  14.0 29.9 %all_to_all.52.received = bf16[8,16,2304]{2,1,0:T(8,128)(2,1)S(1)} all-to-all(bf16[8,16,2304]{2,1,0:T(8,128)(2,1)S(1)} %bitcast.19), channel_id=1, replica_groups=mesh['tok'=64,'feat'=8] {'feat'}, dimensions={0} | all-to-all | bytes 1179648 | tf_op jit(solution)/shard_map/all_to_all | solution.py:24
  43.9 0.1 shard_map.60
  43.9 0.0 copy-start.7
  44.0 0.8 copy-done.7
  44.8 4.2 %all-to-all-start.1 = ((bf16[8,16,2304]{2,1,0:T(8,128)(2,1)}), bf16[8,16,2304]{2,1,0:T(8,128)(2,1)}, u32[]{:S(2)}, u32[]{:S(2)}) async-start(bf16[8,16,2304]{2,1,0:T(8,128)(2,1)} %copy-done.7), calls=%async_computation.1 | async-start | bytes 1179648 | tf_op jit(solution)/shard_map/all_to_all | solution.py:24
  49.0 1.9 collective-permute-start.1
  50.9 21.9 %collective-permute-done.1.ahead = bf16[256,1024]{1,0:T(8,128)(2,1)S(1)} collective-permute-done((bf16[256,1024]{1,0:T(8,128)(2,1)}, bf16[256,1024]{1,0:T(8,128)(2,1)S(1)}, u32[]{:S(2)}, u32[]{:S(2)}) %collective-permute-start.1) | collective-permute-done | bytes 524320 | tf_op jit(solution)/shard_map/ppermute | solution.py:293
  72.8 0.0 copy-start.2
  72.8 0.8 copy-done.2
  73.6 0.0 all-to-all-done.1
  73.6 0.0 copy-done.1
  73.6 0.0 copy-start.3
  73.6 1.0 copy-done.3
  74.7 0.0 copy-start.4
  74.7 0.0 copy-start.6
  74.7 2.5 %shard_map.61 = f32[64,1088]{1,0:T(8,128)S(1)} custom-call(bf16[128,2304]{1,0:T(8,128)(2,1)} %bitcast.3.known, bf16[1728,1024]{1,0:T(8,128)(2,1)S(1)} %copy-done.1, bf16[256,1024]{1,0:T(8,128)(2,1)S(1)} %copy-done.3), custom_call_target="tpu_custom_call" | custom-call | tf_op jit(solution)/shard_map/pallas_call | solution.py:30
  77.2 0.3 copy.6
  77.5 24.9 %all_to_all.53 = f32[64,1,1088]{2,1,0:T(1,128)S(1)} all-to-all(f32[64,1,1088]{2,1,0:T(1,128)S(1)} %copy.6), channel_id=1, replica_groups=mesh['tok'=64,'feat'=8] {'tok'}, dimensions={0} | all-to-all | bytes 557056 | tf_op jit(solution)/shard_map/all_to_all | solution.py:24
  102.4 0.3 copy.7
  102.7 17.5 %all_to_all.54 = f32[64,1,1088]{2,1,0:T(1,128)S(1)} all-to-all(f32[64,1,1088]{2,1,0:T(1,128)S(1)} %copy.7), channel_id=1, replica_groups=mesh['tok'=64,'feat'=8] {'tok'}, dimensions={0} | all-to-all | bytes 557056 | tf_op jit(solution)/shard_map/all_to_all | solution.py:24
  120.3 0.0 copy-done.4
  120.3 0.0 copy-done.6
  120.3 2.4 %shard_map.63 = bf16[64,2816]{1,0:T(8,128)(2,1)S(1)} custom-call(f32[64,1088]{1,0:T(8,128)S(1)} %bitcast.17, bf16[1728,1024]{1,0:T(8,128)(2,1)S(1)} %copy-done.1, f32[128,1024]{1,0:T(8,128)S(1)} %copy-done.6, bf16[256,1024]{1,0:T(8,128)(2,1)S(1)} %copy-done.4), custom_call_target="tpu_custom_call" | custom-call | tf_op jit(solution)/shard_map/pallas_call | solution.py:30
  122.7 19.5 %all_to_all.55.received = bf16[8,8,2816]{2,1,0:T(8,128)(2,1)S(1)} all-to-all(bf16[8,8,2816]{2,1,0:T(8,128)(2,1)S(1)} %bitcast.20), channel_id=1, replica_groups=mesh['tok'=64,'feat'=8] {'feat'}, dimensions={0} | all-to-all | bytes 720896 | tf_op jit(solution)/shard_map/all_to_all | solution.py:24
  142.2 1.2 shard_map.64
  143.5 17.1 %all_to_all.56 = bf16[8,8,2816]{2,1,0:T(8,128)(2,1)S(1)} all-to-all(bf16[8,8,2816]{2,1,0:T(8,128)(2,1)S(1)} %shard_map.64), channel_id=1, replica_groups=mesh['tok'=64,'feat'=8] {'feat'}, dimensions={0} | all-to-all | bytes 720896 | tf_op jit(solution)/shard_map/all_to_all | solution.py:24
  160.6 2.5 %shard_map.65 = bf16[64,8,384]{2,1,0:T(8,128)(2,1)S(1)} custom-call(bf16[64,2816]{1,0:T(8,128)(2,1)S(1)} %bitcast.15, bf16[128,2304]{1,0:T(8,128)(2,1)} %bitcast.3.known, bf16[1728,1024]{1,0:T(8,128)(2,1)S(1)} %copy-done.1, bf16[256,1024]{1,0:T(8,128)(2,1)S(1)} %copy-done.4), custom_call_target="tpu_custom_call" | custom-call | tf_op jit(solution)/shard_map/pallas_call | solution.py:30
  163.1 20.5 %all_to_all.57.received = bf16[64,8,384]{2,1,0:T(8,128)(2,1)S(1)} all-to-all(bf16[64,8,384]{2,1,0:T(8,128)(2,1)S(1)} %shard_map.65), channel_id=1, replica_groups=mesh['tok'=64,'feat'=8] {'tok'}, dimensions={0} | all-to-all | bytes 786432 | tf_op jit(solution)/shard_map/all_to_all | solution.py:24
  183.6 0.2 shard_map.66
  183.8 19.9 %all_to_all.58.gathered = bf16[64,8,384]{2,1,0:T(8,128)(2,1)S(1)} all-to-all(bf16[64,8,384]{2,1,0:T(8,128)(2,1)S(1)} %shard_map.66), channel_id=1, replica_groups=mesh['tok'=64,'feat'=8] {'tok'}, dimensions={0} | all-to-all | bytes 786432 | tf_op jit(solution)/shard_map/all_to_all | solution.py:24
  203.7 2.9 %shard_map.67 = (f32[192,1024]{1,0:T(8,128)}, f32[192,192]{1,0:T(8,128)}, f32[192,192]{1,0:T(8,128)}) custom-call(bf16[64,8,384]{2,1,0:T(8,128)(2,1)S(1)} %all_to_all.58.gathered, f32[64,1088]{1,0:T(8,128)S(1)} %bitcast.18, bf16[64,2816]{1,0:T(8,128)(2,1)S(1)} %bitcast.16, bf16[128,2304]{1,0:T(8,128)(2,1)} %bitcast.3.known), custom_call_target="tpu_custom_call" | custom-call | tf_op jit(solution)/shard_map/pallas_call | solution.py:30
  (3 shorter events, 0.1 us)
Async XLA Ops:
  1.7 2.0 copy-start
  3.7 5.5 %copy-start.5 = (f32[128,1024]{1,0:T(8,128)}, f32[128,1024]{1,0:T(8,128)S(1)}, u32[]{:S(2)}) copy-start(f32[128,1024]{1,0:T(8,128)S(1)} %pad_maximum_fusion.both) | copy-start | bytes 1572868
  5.3 68.3 %copy-start.1 = (bf16[1728,1024]{1,0:T(8,128)(2,1)S(1)}, bf16[1728,1024]{1,0:T(8,128)(2,1)}, u32[]{:S(2)}) copy-start(bf16[1728,1024]{1,0:T(8,128)(2,1)} %hidden.7) | copy-start | bytes 10616836
  5.4 8.5 %collective-permute-start = (bf16[128,256]{1,0:T(8,128)(2,1)S(1)}, bf16[128,256]{1,0:T(8,128)(2,1)S(1)}, u32[]{:S(2)}, u32[]{:S(2)}) collective-permute-start(bf16[128,256]{1,0:T(8,128)(2,1)S(1)} %get-tuple-element.11), channel_id=1, source_target_pairs={{8,0},{16,8},{24,16},{32,24},{40,32},{48,40},{56,48},{64,56},{72,6... | collective-permute-start | bytes 196616 | tf_op jit(solution)/shard_map/ppermute | solution.py:291
  43.9 0.8 copy-start.7
  44.8 28.8 %all-to-all-start.1 = ((bf16[8,16,2304]{2,1,0:T(8,128)(2,1)}), bf16[8,16,2304]{2,1,0:T(8,128)(2,1)}, u32[]{:S(2)}, u32[]{:S(2)}) async-start(bf16[8,16,2304]{2,1,0:T(8,128)(2,1)} %copy-done.7), calls=%async_computation.1 | async-start | bytes 1179648 | tf_op jit(solution)/shard_map/all_to_all | solution.py:24
  49.0 23.8 %collective-permute-start.1 = (bf16[256,1024]{1,0:T(8,128)(2,1)}, bf16[256,1024]{1,0:T(8,128)(2,1)S(1)}, u32[]{:S(2)}, u32[]{:S(2)}) collective-permute-start(bf16[256,1024]{1,0:T(8,128)(2,1)} %slice.3), channel_id=1, source_target_pairs={{8,0},{16,8},{24,16},{32,24},{40,32},{48,40},{56,48},{64,56},{72,6... | collective-permute-start | bytes 1572872 | tf_op jit(solution)/shard_map/ppermute | solution.py:293
  72.8 0.8 copy-start.2
  73.6 1.0 copy-start.3
  74.7 45.6 %copy-start.4 = (bf16[256,1024]{1,0:T(8,128)(2,1)S(1)}, bf16[256,1024]{1,0:T(8,128)(2,1)}, u32[]{:S(2)}) copy-start(bf16[256,1024]{1,0:T(8,128)(2,1)} %copy-done.2) | copy-start | bytes 1572868
  74.7 45.6 %copy-start.6 = (f32[128,1024]{1,0:T(8,128)S(1)}, f32[128,1024]{1,0:T(8,128)}, u32[]{:S(2)}) copy-start(f32[128,1024]{1,0:T(8,128)} %copy-done.5) | copy-start | bytes 1572868

commit v7 on v4

--- a/solution.py
+++ b/solution.py
@@ -77,22 +77,20 @@
     return value
 
 
-def start_kernel(x, p, hidden, out):
-    cols = x.shape[0]
-    wide = out.shape[1] - 4 * cols
-    both = jnp.concatenate([x[...], p[...]])
-    project_own(both.astype(HALF), hidden, out)
-    high, low = high_low(exact(both, both))
-    out[:, wide : wide + 2 * cols] = high
-    out[:, wide + 2 * cols :] = low
-
-
-def edge_kernel(whole, x, p, tail, ahead, start, out):
-    wide = out.shape[1] - 4 * x.shape[0]
+def start_kernel(both, hidden, out):
+    rows = both.shape[0]
+    wide = out.shape[1] - 2 * rows
+    project_own(both[...].astype(HALF), hidden, out)
+    high, low = high_low(exact(both[...], both[...]))
+    out[:, wide : wide + rows] = high
+    out[:, wide + rows :] = low
+
+
+def edge_kernel(whole, both, tail, ahead, start, out):
+    wide = out.shape[1] - 2 * both.shape[0]
     out[:, :whole] = start[:, :whole]
     out[:, wide:] = start[:, wide:]
-    both = jnp.concatenate([x[...], p[...]]).astype(HALF)
-    out[:, whole:wide] = project_edge(both, tail[...], ahead)
+    out[:, whole:wide] = project_edge(both[...].astype(HALF), tail[...], ahead)
 
 
 def known_kernel(wide, received, out):
@@ -120,17 +118,21 @@
     out[:, features:] = cross
 
 
-def residual_kernel(feat, total, x, p, hidden, ahead, out):
+def spread_kernel(factor, received, out):
+    total = jnp.sum(received[...], axis=0, keepdims=True) * factor
+    out[...] = jnp.broadcast_to(total, out.shape)
+
+
+def residual_kernel(feat, total, both, hidden, ahead, out):
     tokens, features = hidden.shape
-    cols = x.shape[0]
+    cols = total.shape[0]
     whole, at = tokens // LANES * LANES, padded(tokens + LAG)
     image = total[:, :features]
-    residual = (image - times(total[:, features:], x[...])) * SMALL
+    residual = (image - times(total[:, features:], both[:cols])) * SMALL
     rounded = residual.astype(HALF)
     project_own(rounded, hidden, out)
     out[:, whole:at] = project_edge(rounded, hidden[whole:], ahead)
-    both = jnp.concatenate([x[...], p[...]])
-    products = exact(jnp.concatenate([residual, image]), both)
+    products = exact(jnp.concatenate([residual, image]), both[...])
     share = total[:, features:] * (1.0 / feat)
     lacks = products[cols:] - jnp.concatenate([share, jnp.zeros_like(share)], axis=1)
     own = exact(jnp.concatenate([residual, residual]), residual)[:cols]
@@ -263,26 +265,27 @@
     blocks = tok * 8 // (2 * cols)
 
     ahead = lax.ppermute(hidden_states[:LAG], "tok", [(i + 1, i) for i in range(tok - 1)])
-    x, p = current_block.T, directions.T
+    both = jnp.concatenate([current_block.T, directions.T])
 
     total = wide + 4 * cols
     flat = shape((2 * cols, total), HALF)
-    part = kernel_call(start_kernel, flat, x, p, hidden_states)
-    part = kernel_call(functools.partial(edge_kernel, whole), flat, x, p, hidden_states[whole:], ahead, part)
+    part = kernel_call(start_kernel, flat, both, hidden_states)
+    part = kernel_call(functools.partial(edge_kernel, whole), flat, both, hidden_states[whole:], ahead, part)
     blocked = shape((feat, 2 * cols // feat, total), HALF)
     part = exchange(part.reshape(blocked.shape), "feat")
     part = kernel_call(functools.partial(known_kernel, wide), blocked, part)
     known = exchange(part, "feat").reshape(2 * cols, total)
 
     part = kernel_call(first_kernel, shape((cols, features + cols), FLOAT), known, hidden_states, ahead)
-    part = exchange(part.reshape(tok, 1, -1), "tok")
-    part = jnp.sum(part, axis=0) * factor
-    part = exchange(jnp.broadcast_to(part, (tok,) + part.shape), "tok")
+    flat = shape((tok, cols * (features + cols) // tok), FLOAT)
+    part = exchange(part.reshape(flat.shape), "tok")
+    part = kernel_call(functools.partial(spread_kernel, factor), flat, part)
+    part = exchange(part, "tok")
     first_total = part.reshape(cols, features + cols)
 
     total = wide + 12 * cols
     part = kernel_call(
-        functools.partial(residual_kernel, feat), shape((cols, total), HALF), first_total, x, p, hidden_states, ahead
+        functools.partial(residual_kernel, feat), shape((cols, total), HALF), first_total, both, hidden_states, ahead
     )
     blocked = shape((feat, cols // feat, total), HALF)
     part = exchange(part.reshape(blocked.shape), "feat")

time: 201 us -> 195 us (0.970)
  local copies, waits for them, and re-layouts: 10.1 us -> 4.65 us
    unnamed x23 -> x6, local copies, waits for them, and re-layouts: 7.68 us -> 2.04 us
    pallas_call x9 -> x10, Pallas kernels: 9.53 us -> 9.57 us  [kernel_call(): pl.pallas_call(body, out_shape=outputs, in_specs=[spec] * len(operands),...]
  transfers between devices with their start and end apart: 1 -> 1, of which waited for: 1 -> 1; matrix products, arithmetic and copies ran while one was open for 0% -> 1% of each run, Pallas kernels for 1% -> 1%
where the time goes in v7:
time: 195 us
  blocking collectives  167 us (86%)
  Pallas kernels  9.57 us (5%)
  waiting for transfers between devices  9.31 us (5%)
  local copies, waits for them, and re-layouts  4.65 us (2%)
  starting transfers between devices  2.74 us (1%)
    all_to_all x8, blocking collectives, exchange(): return lax.all_to_all(value, axis, 0, 0, tiled=True)  167 us
    pallas_call x10, Pallas kernels, kernel_call(): pl.pallas_call(body, out_shape=outputs, in_specs=[spec] * len(operands),...  9.57 us
    ppermute x1, waiting for transfers between devices, local(): lax.ppermute(hidden_states[:LAG], 'tok', [(i + 1, i) for i in range(tok -...  9.31 us
  transfers between devices with their start and end apart: 1, of which 1 were waited for; matrix products, arithmetic and copies ran while one was open for 1% of the time, Pallas kernels for 1%

profile of v7, /device:TPU:6, one launch (start us, length us, event | category | flops | bytes accessed | tf_op | source)
XLA Modules:
  0.0 194.8 jit_solution(9191105119494698892)
XLA Ops:
  0.6 1.1 slice.7
  1.7 2.7 %collective-permute-start = (bf16[256,1024]{1,0:T(8,128)(2,1)S(1)}, bf16[256,1024]{1,0:T(8,128)(2,1)S(1)}, u32[]{:S(2)}, u32[]{:S(2)}) collective-permute-start(bf16[256,1024]{1,0:T(8,128)(2,1)S(1)} %slice.7), channel_id=1, source_target_pairs={{8,0},{16,8},{24,16},{32,24},{40,32},{48,40},{56,48},{64,56},{72,6... | collective-permute-start | bytes 1572872 | tf_op jit(solution)/shard_map/ppermute | solution.py:267
  4.5 0.9 slice.6.tail
  5.4 1.1 pad_maximum_fusion.both
  6.5 0.0 copy-start
  6.5 2.0 %copy-done = bf16[1728,1024]{1,0:T(8,128)(2,1)S(1)} copy-done((bf16[1728,1024]{1,0:T(8,128)(2,1)S(1)}, bf16[1728,1024]{1,0:T(8,128)(2,1)}, u32[]{:S(2)}) %copy-start) | copy-done | bytes 3538968
  8.5 1.6 shard_map.58.start
  10.1 0.0 copy-start.1
  10.1 9.3 %collective-permute-done.ahead = bf16[256,1024]{1,0:T(8,128)(2,1)S(1)} collective-permute-done((bf16[256,1024]{1,0:T(8,128)(2,1)S(1)}, bf16[256,1024]{1,0:T(8,128)(2,1)S(1)}, u32[]{:S(2)}, u32[]{:S(2)}) %collective-permute-start) | collective-permute-done | bytes 524320 | tf_op jit(solution)/shard_map/ppermute | solution.py:267
  19.4 0.4 shard_map.59
  19.8 29.9 %all_to_all.52.received = bf16[8,16,2304]{2,1,0:T(8,128)(2,1)S(1)} all-to-all(bf16[8,16,2304]{2,1,0:T(8,128)(2,1)S(1)} %bitcast.23), channel_id=1, replica_groups=mesh['tok'=64,'feat'=8] {'feat'}, dimensions={0} | all-to-all | bytes 1179648 | tf_op jit(solution)/shard_map/all_to_all | solution.py:24
  49.6 0.1 shard_map.60
  49.7 21.5 %all_to_all.53 = bf16[8,16,2304]{2,1,0:T(8,128)(2,1)S(1)} all-to-all(bf16[8,16,2304]{2,1,0:T(8,128)(2,1)S(1)} %shard_map.60), channel_id=1, replica_groups=mesh['tok'=64,'feat'=8] {'feat'}, dimensions={0} | all-to-all | bytes 1179648 | tf_op jit(solution)/shard_map/all_to_all | solution.py:24
  71.3 0.0 copy-done.1
  71.3 1.3 shard_map.61
  72.6 0.3 copy.6
  72.9 23.6 %all_to_all.54 = f32[64,1,1088]{2,1,0:T(1,128)S(1)} all-to-all(f32[64,1,1088]{2,1,0:T(1,128)S(1)} %copy.6), channel_id=1, replica_groups=mesh['tok'=64,'feat'=8] {'tok'}, dimensions={0} | all-to-all | bytes 557056 | tf_op jit(solution)/shard_map/all_to_all | solution.py:24
  96.6 0.3 copy.7
  97.0 17.8 %all_to_all.55 = f32[64,1,1088]{2,1,0:T(1,128)S(1)} all-to-all(f32[64,1,1088]{2,1,0:T(1,128)S(1)} %copy.7), channel_id=1, replica_groups=mesh['tok'=64,'feat'=8] {'tok'}, dimensions={0} | all-to-all | bytes 557056 | tf_op jit(solution)/shard_map/all_to_all | solution.py:24
  114.7 2.4 %shard_map.63 = bf16[64,2816]{1,0:T(8,128)(2,1)S(1)} custom-call(f32[64,1088]{1,0:T(8,128)S(1)} %bitcast.21, f32[128,1024]{1,0:T(8,128)S(1)} %pad_maximum_fusion.both, bf16[1728,1024]{1,0:T(8,128)(2,1)S(1)} %copy-done.1, bf16[256,1024]{1,0:T(8,128)(2,1)S(1)} %collective-permute-done.ahead), custom_call_target="tpu_custom_call" | custom-call | tf_op jit(solution)/shard_map/pallas_call | solution.py:30
  117.2 16.3 %all_to_all.56.received = bf16[8,8,2816]{2,1,0:T(8,128)(2,1)S(1)} all-to-all(bf16[8,8,2816]{2,1,0:T(8,128)(2,1)S(1)} %bitcast.24), channel_id=1, replica_groups=mesh['tok'=64,'feat'=8] {'feat'}, dimensions={0} | all-to-all | bytes 720896 | tf_op jit(solution)/shard_map/all_to_all | solution.py:24
  133.5 0.2 shard_map.64
  133.6 17.1 %all_to_all.57 = bf16[8,8,2816]{2,1,0:T(8,128)(2,1)S(1)} all-to-all(bf16[8,8,2816]{2,1,0:T(8,128)(2,1)S(1)} %shard_map.64), channel_id=1, replica_groups=mesh['tok'=64,'feat'=8] {'feat'}, dimensions={0} | all-to-all | bytes 720896 | tf_op jit(solution)/shard_map/all_to_all | solution.py:24
  150.8 1.5 shard_map.65
  152.3 20.5 %all_to_all.58.received = bf16[64,8,384]{2,1,0:T(8,128)(2,1)S(1)} all-to-all(bf16[64,8,384]{2,1,0:T(8,128)(2,1)S(1)} %shard_map.65), channel_id=1, replica_groups=mesh['tok'=64,'feat'=8] {'tok'}, dimensions={0} | all-to-all | bytes 786432 | tf_op jit(solution)/shard_map/all_to_all | solution.py:24
  172.9 0.2 shard_map.66
  173.0 19.9 %all_to_all.59.gathered = bf16[64,8,384]{2,1,0:T(8,128)(2,1)S(1)} all-to-all(bf16[64,8,384]{2,1,0:T(8,128)(2,1)S(1)} %shard_map.66), channel_id=1, replica_groups=mesh['tok'=64,'feat'=8] {'tok'}, dimensions={0} | all-to-all | bytes 786432 | tf_op jit(solution)/shard_map/all_to_all | solution.py:24
  192.9 1.9 shard_map.67
  (3 shorter events, 0.1 us)
Async XLA Ops:
  1.7 17.7 %collective-permute-start = (bf16[256,1024]{1,0:T(8,128)(2,1)S(1)}, bf16[256,1024]{1,0:T(8,128)(2,1)S(1)}, u32[]{:S(2)}, u32[]{:S(2)}) collective-permute-start(bf16[256,1024]{1,0:T(8,128)(2,1)S(1)} %slice.7), channel_id=1, source_target_pairs={{8,0},{16,8},{24,16},{32,24},{40,32},{48,40},{56,48},{64,56},{72,6... | collective-permute-start | bytes 1572872 | tf_op jit(solution)/shard_map/ppermute | solution.py:267
  6.5 2.0 %copy-start = (bf16[1728,1024]{1,0:T(8,128)(2,1)S(1)}, bf16[1728,1024]{1,0:T(8,128)(2,1)}, u32[]{:S(2)}) copy-start(bf16[1728,1024]{1,0:T(8,128)(2,1)} %hidden.7) | copy-start | bytes 10616836
  10.1 61.2 %copy-start.1 = (bf16[1728,1024]{1,0:T(8,128)(2,1)S(1)}, bf16[1728,1024]{1,0:T(8,128)(2,1)}, u32[]{:S(2)}) copy-start(bf16[1728,1024]{1,0:T(8,128)(2,1)} %hidden.7) | copy-start | bytes 10616836

commit v8 on v7

--- a/solution.py
+++ b/solution.py
@@ -100,7 +100,7 @@
     out[...] = jnp.broadcast_to(total, out.shape)
 
 
-def lag_image(projected, hidden, ahead):
+def lag_image(projected, rows, hidden, ahead):
     tokens = hidden.shape[0]
     cut = tokens // LANES * LANES - LAG
     here, later = projected[:, :tokens], projected[:, LAG : LAG + tokens]
@@ -108,14 +108,21 @@
     image = jnp.dot(later, hidden[...], preferred_element_type=FLOAT)
     image += jnp.dot(here[:, :cut], hidden[LAG : LAG + cut], preferred_element_type=FLOAT)
     image += jnp.dot(here[:, cut:], edge, preferred_element_type=FLOAT)
-    return image, rows_dot(later, here) + rows_dot(here, later)
+    cross = rows_dot(rows[:, LAG : LAG + tokens], here) + rows_dot(rows[:, :tokens], later)
+    return image, cross
+
+
+def lag_cross(projected, tokens):
+    here, later = projected[:, :tokens], projected[:, LAG : LAG + tokens]
+    return rows_dot(later, here) + rows_dot(here, later)
 
 
 def first_kernel(known, hidden, ahead, out):
-    features = hidden.shape[1]
-    image, cross = lag_image(known[: out.shape[0]], hidden, ahead)
+    tokens, features = hidden.shape
+    cols = out.shape[0]
+    image, cross = lag_image(known[:cols], known[:cols], hidden, ahead)
     out[:, :features] = image
-    out[:, features:] = cross
+    out[:, features:] = jnp.concatenate([cross, lag_cross(known[cols:, : padded(tokens + LAG)], tokens)], axis=1)
 
 
 def spread_kernel(factor, received, out):
@@ -128,12 +135,12 @@
     cols = total.shape[0]
     whole, at = tokens // LANES * LANES, padded(tokens + LAG)
     image = total[:, :features]
-    residual = (image - times(total[:, features:], both[:cols])) * SMALL
+    residual = (image - times(total[:, features : features + cols], both[:cols])) * SMALL
     rounded = residual.astype(HALF)
     project_own(rounded, hidden, out)
     out[:, whole:at] = project_edge(rounded, hidden[whole:], ahead)
     products = exact(jnp.concatenate([residual, image]), both[...])
-    share = total[:, features:] * (1.0 / feat)
+    share = total[:, features : features + cols] * (1.0 / feat)
     lacks = products[cols:] - jnp.concatenate([share, jnp.zeros_like(share)], axis=1)
     own = exact(jnp.concatenate([residual, residual]), residual)[:cols]
     own = jnp.concatenate([own, jnp.zeros_like(own)], axis=1)
@@ -157,42 +164,26 @@
     out[...] = jnp.broadcast_to(total, out.shape)
 
 
-def side_by_side(first, second):
-    cols = first.shape[1] // 2
-    left = lax.broadcasted_iota(jnp.int32, first.shape, 1) < cols
-    return jnp.where(left, first, pltpu.roll(second, cols, 1))
-
-
-def image_kernel(blocks, found, known, hidden, ahead, out):
+def image_kernel(found, known, hidden, ahead, out):
     tokens, features = hidden.shape
     cols = found.shape[0]
-    span = features // blocks
     wide = padded(tokens + LAG)
-    image, cross = lag_image(jnp.concatenate([found[:, :wide], known[cols:, :wide]]), hidden, ahead)
+    rows = found[:, :wide]
+    image, cross = lag_image(jnp.concatenate([rows, known[cols:, :wide]]), rows, hidden, ahead)
+    image = image.astype(HALF)
     high = cross.astype(HALF).astype(FLOAT)
     low = cross - high
-    pieces = [side_by_side(high, low), side_by_side(pltpu.roll(high, cols, 1), pltpu.roll(low, cols, 1))]
-    groups = 2 * cols // 8
-    for g in range(groups):
-        for b in range(blocks):
-            out[g * blocks + b, :, :span] = image[8 * g : 8 * g + 8, b * span : (b + 1) * span].astype(HALF)
-    for k in range(out.shape[0]):
-        if k < 2 * groups:
-            g = k % groups
-            out[k, :, span:] = pieces[k // groups][8 * g : 8 * g + 8].astype(HALF)
-        else:
-            out[k, :, span:] = jnp.zeros((8, 2 * cols), HALF)
-
-
-def total_kernel(factor, cols, received, out):
-    span = received.shape[2] - 2 * cols
+    for d in range(out.shape[0]):
+        out[d, :, :features] = image[2 * d : 2 * d + 2]
+        out[d, :, features:] = jnp.concatenate([high[d : d + 1], low[d : d + 1]]).astype(HALF)
+
+
+def total_kernel(factor, features, received, out):
     total = jnp.sum(received[...].astype(FLOAT), axis=0) * factor
-    cross = total[:, span:]
-    cross = cross + pltpu.roll(cross, cols, 1)
+    cross = total[:1, features:] + total[1:, features:]
     high = cross.astype(HALF).astype(FLOAT)
-    left = lax.broadcasted_iota(jnp.int32, cross.shape, 1) < cols
-    cross = jnp.where(left, high, cross - high)
-    total = jnp.concatenate([total[:, :span], cross], axis=1).astype(HALF)
+    cross = jnp.concatenate([high, cross - high])
+    total = jnp.concatenate([total[:, :features], cross], axis=1).astype(HALF)
     out[...] = jnp.broadcast_to(total, out.shape)
 
 
@@ -202,7 +193,8 @@
     r_x, r_p, lacks, image_x_p, r_r = (products[:, i * cols : (i + 1) * cols] for i in range(5))
     products = joined(known[:, wide:])
     x_x, p_x, p_p = products[:cols, :cols], products[cols:, :cols], products[cols:, cols:]
-    rayleigh_t = first_total[:, first_total.shape[1] - cols :] + lacks
+    features = first_total.shape[1] - 2 * cols
+    rayleigh_t = first_total[:, features : features + cols] + lacks
     lacks = lacks * SMALL
     lacks_xx = times(lacks, x_x)
     r_r = r_r - exact(lacks, r_x) - exact(r_x, lacks) + exact(lacks_xx, lacks)
@@ -224,33 +216,28 @@
     rows = [[x_x, turned[3], turned[4]], [u_x, r_r * scale * across, u_p], [p_x, turned[5], p_p]]
     for i, row in enumerate(rows):
         search[i * cols : (i + 1) * cols] = jnp.concatenate(row, axis=1)
-    return scale, across, turned[:3], u_image_x, image_x_p
-
-
-def last_kernel(blocks, wide, gathered, first_total, found, known, images, gram, search):
-    cols = found.shape[0]
-    scale, across, turned, u_image_x, image_x_p = inner_products(wide, first_total, found, known, search)
-    features = images.shape[1]
-    span = features // blocks
-    groups = cols // 8
+    return scale, across, eye.astype(FLOAT), turned[:3], u_image_x, image_x_p
+
+
+def last_kernel(wide, gathered, first_total, found, known, images, gram, search):
+    cols, features = found.shape[0], images.shape[1]
+    scale, across, eye, turned, u_image_x, image_x_p = inner_products(wide, first_total, found, known, search)
     images[:cols] = first_total[:, :features]
-    for g in range(groups):
-        for b in range(blocks):
-            at = slice(b * span, (b + 1) * span)
-            rows = slice(cols + 8 * g, cols + 8 * g + 8)
-            images[rows, at] = gathered[g * blocks + b, :, :span].astype(FLOAT) * scale[8 * g : 8 * g + 8]
-            rows = slice(2 * cols + 8 * g, 2 * cols + 8 * g + 8)
-            images[rows, at] = gathered[(groups + g) * blocks + b, :, :span].astype(FLOAT)
-
-    def piece(first):
-        value = jnp.concatenate([gathered[k, :, span:].astype(FLOAT) for k in range(first, first + groups)])
-        return (value + pltpu.roll(value, cols, 1))[:, :cols]
-
-    rr, pr, rp, pp = (piece(i * groups) for i in range(4))
+    cross = []
+    for d in range(gathered.shape[0]):
+        rows = gathered[d, :, :features].astype(FLOAT)
+        if 2 * d < cols:
+            rows = rows * scale[2 * d : 2 * d + 2]
+        images[cols + 2 * d : cols + 2 * d + 2] = rows
+        pair = gathered[d, :, features:].astype(FLOAT)
+        cross.append(pair[:1] + pair[1:])
+    cross = jnp.concatenate(cross) * scale
+    u_u, u_p = cross[:, :cols] * across, cross[:, cols:]
+    p_p = first_total[:, features + cols :]
     rows = [
         [turned[0], turned[1], image_x_p],
-        [u_image_x, rr * scale * across, rp * scale],
-        [turned[2], pr * across, pp],
+        [u_image_x, u_u, u_p],
+        [turned[2], exact(eye, u_p), p_p],
     ]
     for i, row in enumerate(rows):
         gram[i * cols : (i + 1) * cols] = jnp.concatenate(row, axis=1)
@@ -262,7 +249,6 @@
     feat, tok = lax.axis_size("feat"), lax.axis_size("tok")
     factor = 0.5 / math.sqrt(tokens * tok - LAG)
     whole, wide = tokens // LANES * LANES, padded(tokens + LAG)
-    blocks = tok * 8 // (2 * cols)
 
     ahead = lax.ppermute(hidden_states[:LAG], "tok", [(i + 1, i) for i in range(tok - 1)])
     both = jnp.concatenate([current_block.T, directions.T])
@@ -276,12 +262,12 @@
     part = kernel_call(functools.partial(known_kernel, wide), blocked, part)
     known = exchange(part, "feat").reshape(2 * cols, total)
 
-    part = kernel_call(first_kernel, shape((cols, features + cols), FLOAT), known, hidden_states, ahead)
-    flat = shape((tok, cols * (features + cols) // tok), FLOAT)
+    part = kernel_call(first_kernel, shape((cols, features + 2 * cols), FLOAT), known, hidden_states, ahead)
+    flat = shape((tok, cols * (features + 2 * cols) // tok), FLOAT)
     part = exchange(part.reshape(flat.shape), "tok")
     part = kernel_call(functools.partial(spread_kernel, factor), flat, part)
     part = exchange(part, "tok")
-    first_total = part.reshape(cols, features + cols)
+    first_total = part.reshape(cols, features + 2 * cols)
 
     total = wide + 12 * cols
     part = kernel_call(
@@ -292,14 +278,14 @@
     part = kernel_call(functools.partial(found_kernel, wide), blocked, part, known)
     found = exchange(part, "feat").reshape(cols, total)
 
-    blocked = shape((tok, 8, features // blocks + 2 * cols), HALF)
-    part = kernel_call(functools.partial(image_kernel, blocks), blocked, found, known, hidden_states, ahead)
+    blocked = shape((tok, 2, features + 2 * cols), HALF)
+    part = kernel_call(image_kernel, blocked, found, known, hidden_states, ahead)
     part = exchange(part, "tok")
-    part = kernel_call(functools.partial(total_kernel, factor, cols), blocked, part)
+    part = kernel_call(functools.partial(total_kernel, factor, features), blocked, part)
     gathered = exchange(part, "tok")
     gram = shape((3 * cols, 3 * cols), FLOAT)
     images, gram_image, gram_search = kernel_call(
-        functools.partial(last_kernel, blocks, wide),
+        functools.partial(last_kernel, wide),
         [shape((3 * cols, features), FLOAT), gram, gram],
         gathered,
         first_total,

time: 195 us -> 192 us (0.985)
  blocking collectives: 167 us -> 163 us
    all_to_all x8, blocking collectives: 167 us -> 163 us  [exchange(): return lax.all_to_all(value, axis, 0, 0, tiled=True)]
where the time goes in v8:
time: 192 us
  blocking collectives  163 us (85%)
  Pallas kernels  10.2 us (5%)
  waiting for transfers between devices  9.31 us (5%)
  local copies, waits for them, and re-layouts  4.65 us (2%)
  starting transfers between devices  2.74 us (1%)
    all_to_all x8, blocking collectives, exchange(): return lax.all_to_all(value, axis, 0, 0, tiled=True)  163 us
    pallas_call x10, Pallas kernels, kernel_call(): pl.pallas_call(body, out_shape=outputs, in_specs=[spec] * len(operands),...  10.2 us
    ppermute x1, waiting for transfers between devices, local(): lax.ppermute(hidden_states[:LAG], 'tok', [(i + 1, i) for i in range(tok -...  9.31 us
  transfers between devices with their start and end apart: 1, of which 1 were waited for; matrix products, arithmetic and copies ran while one was open for 1% of the time, Pallas kernels for 1%

profile of v8, /device:TPU:6, one launch (start us, length us, event | category | flops | bytes accessed | tf_op | source)
XLA Modules:
  0.0 191.5 jit_solution(18119991593237290477)
XLA Ops:
  0.6 1.1 slice.7
  1.7 2.7 %collective-permute-start = (bf16[256,1024]{1,0:T(8,128)(2,1)S(1)}, bf16[256,1024]{1,0:T(8,128)(2,1)S(1)}, u32[]{:S(2)}, u32[]{:S(2)}) collective-permute-start(bf16[256,1024]{1,0:T(8,128)(2,1)S(1)} %slice.7), channel_id=1, source_target_pairs={{8,0},{16,8},{24,16},{32,24},{40,32},{48,40},{56,48},{64,56},{72,6... | collective-permute-start | bytes 1572872 | tf_op jit(solution)/shard_map/ppermute | solution.py:253
  4.5 0.9 slice.6.tail
  5.4 1.1 pad_maximum_fusion.both
  6.5 0.0 copy-start
  6.5 2.0 %copy-done = bf16[1728,1024]{1,0:T(8,128)(2,1)S(1)} copy-done((bf16[1728,1024]{1,0:T(8,128)(2,1)S(1)}, bf16[1728,1024]{1,0:T(8,128)(2,1)}, u32[]{:S(2)}) %copy-start) | copy-done | bytes 3538968
  8.5 1.6 shard_map.58.start
  10.1 0.0 copy-start.1
  10.1 9.3 %collective-permute-done.ahead = bf16[256,1024]{1,0:T(8,128)(2,1)S(1)} collective-permute-done((bf16[256,1024]{1,0:T(8,128)(2,1)S(1)}, bf16[256,1024]{1,0:T(8,128)(2,1)S(1)}, u32[]{:S(2)}, u32[]{:S(2)}) %collective-permute-start) | collective-permute-done | bytes 524320 | tf_op jit(solution)/shard_map/ppermute | solution.py:253
  19.4 0.4 shard_map.59
  19.8 29.9 %all_to_all.52.received = bf16[8,16,2304]{2,1,0:T(8,128)(2,1)S(1)} all-to-all(bf16[8,16,2304]{2,1,0:T(8,128)(2,1)S(1)} %bitcast.23), channel_id=1, replica_groups=mesh['tok'=64,'feat'=8] {'feat'}, dimensions={0} | all-to-all | bytes 1179648 | tf_op jit(solution)/shard_map/all_to_all | solution.py:24
  49.6 0.1 shard_map.60
  49.7 21.5 %all_to_all.53 = bf16[8,16,2304]{2,1,0:T(8,128)(2,1)S(1)} all-to-all(bf16[8,16,2304]{2,1,0:T(8,128)(2,1)S(1)} %shard_map.60), channel_id=1, replica_groups=mesh['tok'=64,'feat'=8] {'feat'}, dimensions={0} | all-to-all | bytes 1179648 | tf_op jit(solution)/shard_map/all_to_all | solution.py:24
  71.3 0.0 copy-done.1
  71.3 1.7 shard_map.61
  73.0 0.3 copy.6
  73.3 23.6 %all_to_all.54 = f32[64,1,1152]{2,1,0:T(1,128)S(1)} all-to-all(f32[64,1,1152]{2,1,0:T(1,128)S(1)} %copy.6), channel_id=1, replica_groups=mesh['tok'=64,'feat'=8] {'tok'}, dimensions={0} | all-to-all | bytes 589824 | tf_op jit(solution)/shard_map/all_to_all | solution.py:24
  97.0 0.3 copy.7
  97.3 17.8 %all_to_all.55 = f32[64,1,1152]{2,1,0:T(1,128)S(1)} all-to-all(f32[64,1,1152]{2,1,0:T(1,128)S(1)} %copy.7), channel_id=1, replica_groups=mesh['tok'=64,'feat'=8] {'tok'}, dimensions={0} | all-to-all | bytes 589824 | tf_op jit(solution)/shard_map/all_to_all | solution.py:24
  115.1 2.4 %shard_map.63 = bf16[64,2816]{1,0:T(8,128)(2,1)S(1)} custom-call(f32[64,1152]{1,0:T(8,128)S(1)} %bitcast.21, f32[128,1024]{1,0:T(8,128)S(1)} %pad_maximum_fusion.both, bf16[1728,1024]{1,0:T(8,128)(2,1)S(1)} %copy-done.1, bf16[256,1024]{1,0:T(8,128)(2,1)S(1)} %collective-permute-done.ahead), custom_call_target="tpu_custom_call" | custom-call | tf_op jit(solution)/shard_map/pallas_call | solution.py:30
  117.5 16.3 %all_to_all.56.received = bf16[8,8,2816]{2,1,0:T(8,128)(2,1)S(1)} all-to-all(bf16[8,8,2816]{2,1,0:T(8,128)(2,1)S(1)} %bitcast.24), channel_id=1, replica_groups=mesh['tok'=64,'feat'=8] {'feat'}, dimensions={0} | all-to-all | bytes 720896 | tf_op jit(solution)/shard_map/all_to_all | solution.py:24
  133.8 0.2 shard_map.64
  134.0 17.1 %all_to_all.57 = bf16[8,8,2816]{2,1,0:T(8,128)(2,1)S(1)} all-to-all(bf16[8,8,2816]{2,1,0:T(8,128)(2,1)S(1)} %shard_map.64), channel_id=1, replica_groups=mesh['tok'=64,'feat'=8] {'feat'}, dimensions={0} | all-to-all | bytes 720896 | tf_op jit(solution)/shard_map/all_to_all | solution.py:24
  151.1 1.5 shard_map.65
  152.6 18.7 %all_to_all.58.received = bf16[64,2,1152]{2,1,0:T(2,128)(2,1)S(1)} all-to-all(bf16[64,2,1152]{2,1,0:T(2,128)(2,1)S(1)} %shard_map.65), channel_id=1, replica_groups=mesh['tok'=64,'feat'=8] {'tok'}, dimensions={0} | all-to-all | bytes 589824 | tf_op jit(solution)/shard_map/all_to_all | solution.py:24
  171.3 0.4 shard_map.66
  171.7 17.8 %all_to_all.59.gathered = bf16[64,2,1152]{2,1,0:T(2,128)(2,1)S(1)} all-to-all(bf16[64,2,1152]{2,1,0:T(2,128)(2,1)S(1)} %shard_map.66), channel_id=1, replica_groups=mesh['tok'=64,'feat'=8] {'tok'}, dimensions={0} | all-to-all | bytes 589824 | tf_op jit(solution)/shard_map/all_to_all | solution.py:24
  189.5 2.0 %shard_map.67 = (f32[192,1024]{1,0:T(8,128)}, f32[192,192]{1,0:T(8,128)}, f32[192,192]{1,0:T(8,128)}) custom-call(bf16[64,2,1152]{2,1,0:T(2,128)(2,1)S(1)} %all_to_all.59.gathered, f32[64,1152]{1,0:T(8,128)S(1)} %bitcast.22, bf16[64,2816]{1,0:T(8,128)(2,1)S(1)} %bitcast.20, bf16[128,2304]{1,0:T(8,128)(2,1)S(1)} %bitcast.18), custom_call_target="tpu_custom_call" | custom-call | tf_op jit(solution)/shard_map/pallas_call | solution.py:30
  (3 shorter events, 0.1 us)
Async XLA Ops:
  1.7 17.7 %collective-permute-start = (bf16[256,1024]{1,0:T(8,128)(2,1)S(1)}, bf16[256,1024]{1,0:T(8,128)(2,1)S(1)}, u32[]{:S(2)}, u32[]{:S(2)}) collective-permute-start(bf16[256,1024]{1,0:T(8,128)(2,1)S(1)} %slice.7), channel_id=1, source_target_pairs={{8,0},{16,8},{24,16},{32,24},{40,32},{48,40},{56,48},{64,56},{72,6... | collective-permute-start | bytes 1572872 | tf_op jit(solution)/shard_map/ppermute | solution.py:253
  6.5 2.0 %copy-start = (bf16[1728,1024]{1,0:T(8,128)(2,1)S(1)}, bf16[1728,1024]{1,0:T(8,128)(2,1)}, u32[]{:S(2)}) copy-start(bf16[1728,1024]{1,0:T(8,128)(2,1)} %hidden.7) | copy-start | bytes 10616836
  10.1 61.2 %copy-start.1 = (bf16[1728,1024]{1,0:T(8,128)(2,1)S(1)}, bf16[1728,1024]{1,0:T(8,128)(2,1)}, u32[]{:S(2)}) copy-start(bf16[1728,1024]{1,0:T(8,128)(2,1)} %hidden.7) | copy-start | bytes 10616836

commit v9 on v8

--- a/solution.py
+++ b/solution.py
@@ -77,17 +77,25 @@
     return value
 
 
+def two_terms(value):
+    high = value.astype(HALF).astype(FLOAT)
+    left = lax.broadcasted_iota(jnp.int32, value.shape, 1) < value.shape[1] // 2
+    return jnp.where(left, high, value - high).astype(HALF)
+
+
 def start_kernel(both, hidden, out):
     rows = both.shape[0]
-    wide = out.shape[1] - 2 * rows
+    cols, wide = rows // 2, out.shape[1] - rows
     project_own(both[...].astype(HALF), hidden, out)
-    high, low = high_low(exact(both[...], both[...]))
-    out[:, wide : wide + rows] = high
-    out[:, wide + rows :] = low
+    products = exact(both[...], both[...])
+    turned = pltpu.roll(products, cols, 1)
+    left = lax.broadcasted_iota(jnp.int32, (cols, rows), 1) < cols
+    out[:cols, wide:] = two_terms(jnp.where(left, products[:cols], turned[:cols]))
+    out[cols:, wide:] = two_terms(jnp.where(left, turned[cols:], products[cols:]))
 
 
 def edge_kernel(whole, both, tail, ahead, start, out):
-    wide = out.shape[1] - 2 * both.shape[0]
+    wide = out.shape[1] - both.shape[0]
     out[:, :whole] = start[:, :whole]
     out[:, wide:] = start[:, wide:]
     out[:, whole:wide] = project_edge(both[...].astype(HALF), tail[...], ahead)
@@ -95,8 +103,9 @@
 
 def known_kernel(wide, received, out):
     total = jnp.sum(received[...].astype(FLOAT), axis=0)
-    high, low = high_low(joined(total[:, wide:]))
-    total = jnp.concatenate([total[:, :wide].astype(HALF), high, low], axis=1)
+    products = total[:, wide:]
+    products = two_terms(products + pltpu.roll(products, products.shape[1] // 2, 1))
+    total = jnp.concatenate([total[:, :wide].astype(HALF), products], axis=1)
     out[...] = jnp.broadcast_to(total, out.shape)
 
 
@@ -139,12 +148,11 @@
     rounded = residual.astype(HALF)
     project_own(rounded, hidden, out)
     out[:, whole:at] = project_edge(rounded, hidden[whole:], ahead)
-    products = exact(jnp.concatenate([residual, image]), both[...])
+    products = exact(jnp.concatenate([residual, image, both[:cols]]), jnp.concatenate([both[...], residual]))
     share = total[:, features : features + cols] * (1.0 / feat)
-    lacks = products[cols:] - jnp.concatenate([share, jnp.zeros_like(share)], axis=1)
-    own = exact(jnp.concatenate([residual, residual]), residual)[:cols]
-    own = jnp.concatenate([own, jnp.zeros_like(own)], axis=1)
-    for value in (products[:cols], lacks, own):
+    lacks = products[cols : 2 * cols, : 2 * cols] - jnp.concatenate([share, jnp.zeros_like(share)], axis=1)
+    own = jnp.concatenate([products[:cols, 2 * cols :], products[2 * cols :, cols : 2 * cols]], axis=1)
+    for value in (products[:cols, : 2 * cols], lacks, own):
         high, low = high_low(value)
         out[:, at : at + 2 * cols] = high
         out[:, at + 6 * cols : at + 8 * cols] = low
@@ -190,16 +198,16 @@
 def inner_products(wide, first_total, found, known, search):
     cols = found.shape[0]
     products = joined(found[:, wide:])
-    r_x, r_p, lacks, image_x_p, r_r = (products[:, i * cols : (i + 1) * cols] for i in range(5))
+    r_x, r_p, lacks, image_x_p, r_r, x_p = (products[:, i * cols : (i + 1) * cols] for i in range(6))
     products = joined(known[:, wide:])
-    x_x, p_x, p_p = products[:cols, :cols], products[cols:, :cols], products[cols:, cols:]
+    x_x, p_p = products[:cols], products[cols:]
     features = first_total.shape[1] - 2 * cols
     rayleigh_t = first_total[:, features : features + cols] + lacks
     lacks = lacks * SMALL
     lacks_xx = times(lacks, x_x)
     r_r = r_r - exact(lacks, r_x) - exact(r_x, lacks) + exact(lacks_xx, lacks)
     r_x = r_x - lacks_xx
-    r_p = r_p - exact(lacks, p_x)
+    r_p = r_p - times(lacks, x_p)
     square = (cols, cols)
     eye = lax.broadcasted_iota(jnp.int32, square, 0) == lax.broadcasted_iota(jnp.int32, square, 1)
     lengths = jnp.where(eye, r_r, 0.0)
@@ -211,9 +219,9 @@
     across = scaling(jnp.sum(lengths, axis=0, keepdims=True))
     u_image_x = (r_r * (1.0 / SMALL) + exact(r_x, rayleigh_t)) * scale
     u_x, u_p = r_x * scale, r_p * scale
-    turned = exact(eye.astype(FLOAT), jnp.concatenate([rayleigh_t, u_image_x, image_x_p, u_x, p_x, u_p]))
+    turned = exact(eye.astype(FLOAT), jnp.concatenate([rayleigh_t, u_image_x, image_x_p, u_x, x_p, u_p]))
     turned = [turned[:, i * cols : (i + 1) * cols] for i in range(6)]
-    rows = [[x_x, turned[3], turned[4]], [u_x, r_r * scale * across, u_p], [p_x, turned[5], p_p]]
+    rows = [[x_x, turned[3], x_p], [u_x, r_r * scale * across, u_p], [turned[4], turned[5], p_p]]
     for i, row in enumerate(rows):
         search[i * cols : (i + 1) * cols] = jnp.concatenate(row, axis=1)
     return scale, across, eye.astype(FLOAT), turned[:3], u_image_x, image_x_p
@@ -253,7 +261,7 @@
     ahead = lax.ppermute(hidden_states[:LAG], "tok", [(i + 1, i) for i in range(tok - 1)])
     both = jnp.concatenate([current_block.T, directions.T])
 
-    total = wide + 4 * cols
+    total = wide + 2 * cols
     flat = shape((2 * cols, total), HALF)
     part = kernel_call(start_kernel, flat, both, hidden_states)
     part = kernel_call(functools.partial(edge_kernel, whole), flat, both, hidden_states[whole:], ahead, part)

time: 192 us -> 191 us (level)
  blocking collectives: 163 us -> 161 us
where the time goes in v9:
time: 191 us; the launch traced here: 190 us
  blocking collectives  161 us (84%)
  Pallas kernels  10.1 us (5%)
  waiting for transfers between devices  9.25 us (5%)
  local copies, waits for them, and re-layouts  4.65 us (2%)
  starting transfers between devices  2.74 us (1%)
    all_to_all x8, blocking collectives, exchange(): return lax.all_to_all(value, axis, 0, 0, tiled=True)  161 us
    pallas_call x10, Pallas kernels, kernel_call(): pl.pallas_call(body, out_shape=outputs, in_specs=[spec] * len(operands),...  10.1 us
    ppermute x1, waiting for transfers between devices, local(): lax.ppermute(hidden_states[:LAG], 'tok', [(i + 1, i) for i in range(tok -...  9.25 us
  transfers between devices with their start and end apart: 1, of which 1 were waited for; matrix products, arithmetic and copies ran while one was open for 1% of the time, Pallas kernels for 1%

profile of v9, /device:TPU:6, one launch (start us, length us, event | category | flops | bytes accessed | tf_op | source)
XLA Modules:
  0.0 190.0 jit_solution(14881348726982928034)
XLA Ops:
  0.6 1.1 slice.7
  1.7 2.7 %collective-permute-start = (bf16[256,1024]{1,0:T(8,128)(2,1)S(1)}, bf16[256,1024]{1,0:T(8,128)(2,1)S(1)}, u32[]{:S(2)}, u32[]{:S(2)}) collective-permute-start(bf16[256,1024]{1,0:T(8,128)(2,1)S(1)} %slice.7), channel_id=1, source_target_pairs={{8,0},{16,8},{24,16},{32,24},{40,32},{48,40},{56,48},{64,56},{72,6... | collective-permute-start | bytes 1572872 | tf_op jit(solution)/shard_map/ppermute | solution.py:261
  4.5 0.9 slice.6.tail
  5.4 1.1 pad_maximum_fusion.both
  6.5 0.0 copy-start
  6.5 2.0 %copy-done = bf16[1728,1024]{1,0:T(8,128)(2,1)S(1)} copy-done((bf16[1728,1024]{1,0:T(8,128)(2,1)S(1)}, bf16[1728,1024]{1,0:T(8,128)(2,1)}, u32[]{:S(2)}) %copy-start) | copy-done | bytes 3538968
  8.5 1.7 shard_map.58.start
  10.1 0.0 copy-start.1
  10.1 9.2 %collective-permute-done.ahead = bf16[256,1024]{1,0:T(8,128)(2,1)S(1)} collective-permute-done((bf16[256,1024]{1,0:T(8,128)(2,1)S(1)}, bf16[256,1024]{1,0:T(8,128)(2,1)S(1)}, u32[]{:S(2)}, u32[]{:S(2)}) %collective-permute-start) | collective-permute-done | bytes 524320 | tf_op jit(solution)/shard_map/ppermute | solution.py:261
  19.4 0.4 shard_map.59
  19.8 29.2 %all_to_all.52.received = bf16[8,16,2176]{2,1,0:T(8,128)(2,1)S(1)} all-to-all(bf16[8,16,2176]{2,1,0:T(8,128)(2,1)S(1)} %bitcast.23), channel_id=1, replica_groups=mesh['tok'=64,'feat'=8] {'feat'}, dimensions={0} | all-to-all | bytes 1114112 | tf_op jit(solution)/shard_map/all_to_all | solution.py:24
  48.9 0.1 shard_map.60
  49.1 20.8 %all_to_all.53 = bf16[8,16,2176]{2,1,0:T(8,128)(2,1)S(1)} all-to-all(bf16[8,16,2176]{2,1,0:T(8,128)(2,1)S(1)} %shard_map.60), channel_id=1, replica_groups=mesh['tok'=64,'feat'=8] {'feat'}, dimensions={0} | all-to-all | bytes 1114112 | tf_op jit(solution)/shard_map/all_to_all | solution.py:24
  69.9 0.0 copy-done.1
  69.9 1.7 shard_map.61
  71.6 0.3 copy.6
  71.9 23.7 %all_to_all.54 = f32[64,1,1152]{2,1,0:T(1,128)S(1)} all-to-all(f32[64,1,1152]{2,1,0:T(1,128)S(1)} %copy.6), channel_id=1, replica_groups=mesh['tok'=64,'feat'=8] {'tok'}, dimensions={0} | all-to-all | bytes 589824 | tf_op jit(solution)/shard_map/all_to_all | solution.py:24
  95.7 0.3 copy.7
  96.0 17.8 %all_to_all.55 = f32[64,1,1152]{2,1,0:T(1,128)S(1)} all-to-all(f32[64,1,1152]{2,1,0:T(1,128)S(1)} %copy.7), channel_id=1, replica_groups=mesh['tok'=64,'feat'=8] {'tok'}, dimensions={0} | all-to-all | bytes 589824 | tf_op jit(solution)/shard_map/all_to_all | solution.py:24
  113.8 2.1 %shard_map.63 = bf16[64,2816]{1,0:T(8,128)(2,1)S(1)} custom-call(f32[64,1152]{1,0:T(8,128)S(1)} %bitcast.21, f32[128,1024]{1,0:T(8,128)S(1)} %pad_maximum_fusion.both, bf16[1728,1024]{1,0:T(8,128)(2,1)S(1)} %copy-done.1, bf16[256,1024]{1,0:T(8,128)(2,1)S(1)} %collective-permute-done.ahead), custom_call_target="tpu_custom_call" | custom-call | tf_op jit(solution)/shard_map/pallas_call | solution.py:30
  115.9 16.3 %all_to_all.56.received = bf16[8,8,2816]{2,1,0:T(8,128)(2,1)S(1)} all-to-all(bf16[8,8,2816]{2,1,0:T(8,128)(2,1)S(1)} %bitcast.24), channel_id=1, replica_groups=mesh['tok'=64,'feat'=8] {'feat'}, dimensions={0} | all-to-all | bytes 720896 | tf_op jit(solution)/shard_map/all_to_all | solution.py:24
  132.2 0.2 shard_map.64
  132.4 17.1 %all_to_all.57 = bf16[8,8,2816]{2,1,0:T(8,128)(2,1)S(1)} all-to-all(bf16[8,8,2816]{2,1,0:T(8,128)(2,1)S(1)} %shard_map.64), channel_id=1, replica_groups=mesh['tok'=64,'feat'=8] {'feat'}, dimensions={0} | all-to-all | bytes 720896 | tf_op jit(solution)/shard_map/all_to_all | solution.py:24
  149.5 1.5 shard_map.65
  151.0 18.7 %all_to_all.58.received = bf16[64,2,1152]{2,1,0:T(2,128)(2,1)S(1)} all-to-all(bf16[64,2,1152]{2,1,0:T(2,128)(2,1)S(1)} %shard_map.65), channel_id=1, replica_groups=mesh['tok'=64,'feat'=8] {'tok'}, dimensions={0} | all-to-all | bytes 589824 | tf_op jit(solution)/shard_map/all_to_all | solution.py:24
  169.8 0.4 shard_map.66
  170.1 17.8 %all_to_all.59.gathered = bf16[64,2,1152]{2,1,0:T(2,128)(2,1)S(1)} all-to-all(bf16[64,2,1152]{2,1,0:T(2,128)(2,1)S(1)} %shard_map.66), channel_id=1, replica_groups=mesh['tok'=64,'feat'=8] {'tok'}, dimensions={0} | all-to-all | bytes 589824 | tf_op jit(solution)/shard_map/all_to_all | solution.py:24
  187.9 2.1 %shard_map.67 = (f32[192,1024]{1,0:T(8,128)}, f32[192,192]{1,0:T(8,128)}, f32[192,192]{1,0:T(8,128)}) custom-call(bf16[64,2,1152]{2,1,0:T(2,128)(2,1)S(1)} %all_to_all.59.gathered, f32[64,1152]{1,0:T(8,128)S(1)} %bitcast.22, bf16[64,2816]{1,0:T(8,128)(2,1)S(1)} %bitcast.20, bf16[128,2176]{1,0:T(8,128)(2,1)S(1)} %bitcast.18), custom_call_target="tpu_custom_call" | custom-call | tf_op jit(solution)/shard_map/pallas_call | solution.py:30
  (3 shorter events, 0.1 us)
Async XLA Ops:
  1.7 17.7 %collective-permute-start = (bf16[256,1024]{1,0:T(8,128)(2,1)S(1)}, bf16[256,1024]{1,0:T(8,128)(2,1)S(1)}, u32[]{:S(2)}, u32[]{:S(2)}) collective-permute-start(bf16[256,1024]{1,0:T(8,128)(2,1)S(1)} %slice.7), channel_id=1, source_target_pairs={{8,0},{16,8},{24,16},{32,24},{40,32},{48,40},{56,48},{64,56},{72,6... | collective-permute-start | bytes 1572872 | tf_op jit(solution)/shard_map/ppermute | solution.py:261
  6.5 2.0 %copy-start = (bf16[1728,1024]{1,0:T(8,128)(2,1)S(1)}, bf16[1728,1024]{1,0:T(8,128)(2,1)}, u32[]{:S(2)}) copy-start(bf16[1728,1024]{1,0:T(8,128)(2,1)} %hidden.7) | copy-start | bytes 10616836
  10.1 59.8 %copy-start.1 = (bf16[1728,1024]{1,0:T(8,128)(2,1)S(1)}, bf16[1728,1024]{1,0:T(8,128)(2,1)}, u32[]{:S(2)}) copy-start(bf16[1728,1024]{1,0:T(8,128)(2,1)} %hidden.7) | copy-start | bytes 10616836

commit v10 on v9

--- a/solution.py
+++ b/solution.py
@@ -9,6 +9,7 @@
 from jax.sharding import PartitionSpec as P
 
 LAG = 256
+HALO = LAG // 2
 SMALL = 2.0**-20
 LANES = 128
 HIGHEST = lax.Precision.HIGHEST
@@ -65,13 +66,14 @@
 
 def project_own(vectors, hidden, out):
     whole = hidden.shape[0] // LANES * LANES
-    out[:, :whole] = rows_dot(vectors, hidden[:whole]).astype(HALF)
-
-
-def project_edge(vectors, tail, ahead):
-    rows, rest = vectors.shape[0], tail.shape[0]
+    out[:, HALO : HALO + whole] = rows_dot(vectors, hidden[:whole]).astype(HALF)
+
+
+def project_edges(vectors, tail, behind, ahead, out):
+    rows = vectors.shape[0]
+    out[:, :HALO] = rows_dot(vectors, behind[...]).astype(HALF)
     value = rows_dot(vectors, jnp.concatenate([tail, ahead[...]])).astype(HALF)
-    spare = padded(rest + LAG) - rest - LAG
+    spare = padded(value.shape[1]) - value.shape[1]
     if spare:
         value = jnp.concatenate([value, jnp.zeros((rows, spare), HALF)], axis=1)
     return value
@@ -94,11 +96,11 @@
     out[cols:, wide:] = two_terms(jnp.where(left, turned[cols:], products[cols:]))
 
 
-def edge_kernel(whole, both, tail, ahead, start, out):
+def edge_kernel(whole, both, tail, behind, ahead, start, out):
     wide = out.shape[1] - both.shape[0]
-    out[:, :whole] = start[:, :whole]
+    out[:, HALO : HALO + whole] = start[:, HALO : HALO + whole]
     out[:, wide:] = start[:, wide:]
-    out[:, whole:wide] = project_edge(both[...].astype(HALF), tail[...], ahead)
+    out[:, HALO + whole : wide] = project_edges(both[...].astype(HALF), tail[...], behind, ahead, out)
 
 
 def known_kernel(wide, received, out):
@@ -109,14 +111,16 @@
     out[...] = jnp.broadcast_to(total, out.shape)
 
 
-def lag_image(projected, rows, hidden, ahead):
+def lag_image(projected, rows, hidden, behind, ahead):
     tokens = hidden.shape[0]
-    cut = tokens // LANES * LANES - LAG
+    whole = tokens // LANES * LANES
+    cut = whole - HALO
     here, later = projected[:, :tokens], projected[:, LAG : LAG + tokens]
-    edge = jnp.concatenate([hidden[cut + LAG :], ahead[...]])
-    image = jnp.dot(later, hidden[...], preferred_element_type=FLOAT)
-    image += jnp.dot(here[:, :cut], hidden[LAG : LAG + cut], preferred_element_type=FLOAT)
+    edge = jnp.concatenate([hidden[whole:], ahead[...]])
+    image = jnp.dot(later[:, HALO:], hidden[: tokens - HALO], preferred_element_type=FLOAT)
+    image += jnp.dot(here[:, :cut], hidden[HALO:whole], preferred_element_type=FLOAT)
     image += jnp.dot(here[:, cut:], edge, preferred_element_type=FLOAT)
+    image += jnp.dot(later[:, :HALO], behind[...], preferred_element_type=FLOAT)
     cross = rows_dot(rows[:, LAG : LAG + tokens], here) + rows_dot(rows[:, :tokens], later)
     return image, cross
 
@@ -126,10 +130,10 @@
     return rows_dot(later, here) + rows_dot(here, later)
 
 
-def first_kernel(known, hidden, ahead, out):
+def first_kernel(known, hidden, behind, ahead, out):
     tokens, features = hidden.shape
     cols = out.shape[0]
-    image, cross = lag_image(known[:cols], known[:cols], hidden, ahead)
+    image, cross = lag_image(known[:cols], known[:cols], hidden, behind, ahead)
     out[:, :features] = image
     out[:, features:] = jnp.concatenate([cross, lag_cross(known[cols:, : padded(tokens + LAG)], tokens)], axis=1)
 
@@ -139,7 +143,7 @@
     out[...] = jnp.broadcast_to(total, out.shape)
 
 
-def residual_kernel(feat, total, both, hidden, ahead, out):
+def residual_kernel(feat, total, both, hidden, behind, ahead, out):
     tokens, features = hidden.shape
     cols = total.shape[0]
     whole, at = tokens // LANES * LANES, padded(tokens + LAG)
@@ -147,7 +151,7 @@
     residual = (image - times(total[:, features : features + cols], both[:cols])) * SMALL
     rounded = residual.astype(HALF)
     project_own(rounded, hidden, out)
-    out[:, whole:at] = project_edge(rounded, hidden[whole:], ahead)
+    out[:, HALO + whole : at] = project_edges(rounded, hidden[whole:], behind, ahead, out)
     products = exact(jnp.concatenate([residual, image, both[:cols]]), jnp.concatenate([both[...], residual]))
     share = total[:, features : features + cols] * (1.0 / feat)
     lacks = products[cols : 2 * cols, : 2 * cols] - jnp.concatenate([share, jnp.zeros_like(share)], axis=1)
@@ -172,12 +176,12 @@
     out[...] = jnp.broadcast_to(total, out.shape)
 
 
-def image_kernel(found, known, hidden, ahead, out):
+def image_kernel(found, known, hidden, behind, ahead, out):
     tokens, features = hidden.shape
     cols = found.shape[0]
     wide = padded(tokens + LAG)
     rows = found[:, :wide]
-    image, cross = lag_image(jnp.concatenate([rows, known[cols:, :wide]]), rows, hidden, ahead)
+    image, cross = lag_image(jnp.concatenate([rows, known[cols:, :wide]]), rows, hidden, behind, ahead)
     image = image.astype(HALF)
     high = cross.astype(HALF).astype(FLOAT)
     low = cross - high
@@ -258,19 +262,20 @@
     factor = 0.5 / math.sqrt(tokens * tok - LAG)
     whole, wide = tokens // LANES * LANES, padded(tokens + LAG)
 
-    ahead = lax.ppermute(hidden_states[:LAG], "tok", [(i + 1, i) for i in range(tok - 1)])
+    behind = lax.ppermute(hidden_states[tokens - HALO :], "tok", [(i, i + 1) for i in range(tok - 1)])
+    ahead = lax.ppermute(hidden_states[:HALO], "tok", [(i + 1, i) for i in range(tok - 1)])
     both = jnp.concatenate([current_block.T, directions.T])
 
     total = wide + 2 * cols
     flat = shape((2 * cols, total), HALF)
     part = kernel_call(start_kernel, flat, both, hidden_states)
-    part = kernel_call(functools.partial(edge_kernel, whole), flat, both, hidden_states[whole:], ahead, part)
+    part = kernel_call(functools.partial(edge_kernel, whole), flat, both, hidden_states[whole:], behind, ahead, part)
     blocked = shape((feat, 2 * cols // feat, total), HALF)
     part = exchange(part.reshape(blocked.shape), "feat")
     part = kernel_call(functools.partial(known_kernel, wide), blocked, part)
     known = exchange(part, "feat").reshape(2 * cols, total)
 
-    part = kernel_call(first_kernel, shape((cols, features + 2 * cols), FLOAT), known, hidden_states, ahead)
+    part = kernel_call(first_kernel, shape((cols, features + 2 * cols), FLOAT), known, hidden_states, behind, ahead)
     flat = shape((tok, cols * (features + 2 * cols) // tok), FLOAT)
     part = exchange(part.reshape(flat.shape), "tok")
     part = kernel_call(functools.partial(spread_kernel, factor), flat, part)
@@ -279,7 +284,7 @@
 
     total = wide + 12 * cols
     part = kernel_call(
-        functools.partial(residual_kernel, feat), shape((cols, total), HALF), first_total, both, hidden_states, ahead
+        functools.partial(residual_kernel, feat), shape((cols, total), HALF), first_total, both, hidden_states, behind, ahead
     )
     blocked = shape((feat, cols // feat, total), HALF)
     part = exchange(part.reshape(blocked.shape), "feat")
@@ -287,7 +292,7 @@
     found = exchange(part, "feat").reshape(cols, total)
 
     blocked = shape((tok, 2, features + 2 * cols), HALF)
-    part = kernel_call(image_kernel, blocked, found, known, hidden_states, ahead)
+    part = kernel_call(image_kernel, blocked, found, known, hidden_states, behind, ahead)
     part = exchange(part, "tok")
     part = kernel_call(functools.partial(total_kernel, factor, features), blocked, part)
     gathered = exchange(part, "tok")

time: 191 us -> 188 us (0.984)
  waiting for transfers between devices: 9.25 us -> 0.01 us
  starting transfers between devices: 2.74 us -> 7.95 us
  blocking collectives: 161 us -> 163 us
    ppermute x1 -> x2, waiting for transfers between devices: 9.25 us -> 0.01 us  [the longest x1 0.01 us: local(): lax.ppermute(hidden_states[:HALO], 'tok', [(i + 1, i) for i in range(tok...]
    ppermute x1 -> x2, starting transfers between devices: 2.74 us -> 7.95 us  [the longest x1 5.22 us: local(): lax.ppermute(hidden_states[tokens - HALO:], 'tok', [(i, i + 1) for i in r...]
  transfers between devices with their start and end apart: 1 -> 2, of which waited for: 1 -> 0; matrix products, arithmetic and copies ran while one was open for 1% -> 1% of each run, Pallas kernels for 1% -> 1%
where the time goes in v10:
time: 188 us; the launch traced here: 187 us
  blocking collectives  163 us (87%)
  Pallas kernels  10.1 us (5%)
  starting transfers between devices  7.95 us (4%)
  local copies, waits for them, and re-layouts  4.64 us (2%)
    all_to_all x8, blocking collectives, exchange(): return lax.all_to_all(value, axis, 0, 0, tiled=True)  163 us
    pallas_call x10, Pallas kernels, kernel_call(): pl.pallas_call(body, out_shape=outputs, in_specs=[spec] * len(operands),...  10.1 us
    ppermute x1, starting transfers between devices, local(): lax.ppermute(hidden_states[tokens - HALO:], 'tok', [(i, i + 1) for i in r...  5.22 us
  transfers between devices with their start and end apart: 2, of which 0 were waited for; matrix products, arithmetic and copies ran while one was open for 1% of the time, Pallas kernels for 1%

profile of v10, /device:TPU:6, one launch (start us, length us, event | category | flops | bytes accessed | tf_op | source)
XLA Modules:
  0.0 187.3 jit_solution(9023516323780611951)
XLA Ops:
  0.6 1.1 fusion
  1.7 2.7 %collective-permute-start.1 = (bf16[128,1024]{1,0:T(8,128)(2,1)S(1)}, bf16[128,1024]{1,0:T(8,128)(2,1)S(1)}, u32[]{:S(2)}, u32[]{:S(2)}) collective-permute-start(bf16[128,1024]{1,0:T(8,128)(2,1)S(1)} %get-tuple-element.9), channel_id=1, source_target_pairs={{8,0},{16,8},{24,16},{32,24},{40,32},{48,40},{56,48},{64,56},{72,6... | collective-permute-start | bytes 786440 | tf_op jit(solution)/shard_map/ppermute | solution.py:266
  4.4 5.2 %collective-permute-start = (bf16[128,1024]{1,0:T(8,128)(2,1)S(1)}, bf16[128,1024]{1,0:T(8,128)(2,1)S(1)}, u32[]{:S(2)}, u32[]{:S(2)}) collective-permute-start(bf16[128,1024]{1,0:T(8,128)(2,1)S(1)} %get-tuple-element.10), channel_id=1, source_target_pairs={{0,8},{8,16},{16,24},{24,32},{32,40},{40,48},{48,56},{56,64},{64,7... | collective-permute-start | bytes 786440 | tf_op jit(solution)/shard_map/ppermute | solution.py:265
  9.7 0.9 slice.9.tail
  10.6 1.1 pad_maximum_fusion.both
  11.7 0.0 copy-start
  11.7 2.0 %copy-done = bf16[1728,1024]{1,0:T(8,128)(2,1)S(1)} copy-done((bf16[1728,1024]{1,0:T(8,128)(2,1)S(1)}, bf16[1728,1024]{1,0:T(8,128)(2,1)}, u32[]{:S(2)}) %copy-start) | copy-done | bytes 3538968
  13.7 1.7 shard_map.58.start
  15.3 0.0 copy-start.1
  15.3 0.0 collective-permute-done.1.ahead
  15.4 0.0 collective-permute-done.behind
  15.4 0.4 shard_map.59
  15.7 29.3 %all_to_all.52.received = bf16[8,16,2176]{2,1,0:T(8,128)(2,1)S(1)} all-to-all(bf16[8,16,2176]{2,1,0:T(8,128)(2,1)S(1)} %bitcast.23), channel_id=1, replica_groups=mesh['tok'=64,'feat'=8] {'feat'}, dimensions={0} | all-to-all | bytes 1114112 | tf_op jit(solution)/shard_map/all_to_all | solution.py:25
  45.0 0.1 shard_map.60
  45.2 20.8 %all_to_all.53 = bf16[8,16,2176]{2,1,0:T(8,128)(2,1)S(1)} all-to-all(bf16[8,16,2176]{2,1,0:T(8,128)(2,1)S(1)} %shard_map.60), channel_id=1, replica_groups=mesh['tok'=64,'feat'=8] {'feat'}, dimensions={0} | all-to-all | bytes 1114112 | tf_op jit(solution)/shard_map/all_to_all | solution.py:25
  66.0 0.0 copy-done.1
  66.0 1.7 shard_map.61
  67.7 0.3 copy.6
  68.0 24.8 %all_to_all.54 = f32[64,1,1152]{2,1,0:T(1,128)S(1)} all-to-all(f32[64,1,1152]{2,1,0:T(1,128)S(1)} %copy.6), channel_id=1, replica_groups=mesh['tok'=64,'feat'=8] {'tok'}, dimensions={0} | all-to-all | bytes 589824 | tf_op jit(solution)/shard_map/all_to_all | solution.py:25
  92.9 0.3 copy.7
  93.2 17.8 %all_to_all.55 = f32[64,1,1152]{2,1,0:T(1,128)S(1)} all-to-all(f32[64,1,1152]{2,1,0:T(1,128)S(1)} %copy.7), channel_id=1, replica_groups=mesh['tok'=64,'feat'=8] {'tok'}, dimensions={0} | all-to-all | bytes 589824 | tf_op jit(solution)/shard_map/all_to_all | solution.py:25
  111.0 2.2 %shard_map.63 = bf16[64,2816]{1,0:T(8,128)(2,1)S(1)} custom-call(f32[64,1152]{1,0:T(8,128)S(1)} %bitcast.21, f32[128,1024]{1,0:T(8,128)S(1)} %pad_maximum_fusion.both, bf16[1728,1024]{1,0:T(8,128)(2,1)S(1)} %copy-done.1, bf16[128,1024]{1,0:T(8,128)(2,1)S(1)} %collective-permute-done.behind, bf16[128,1024]{1,0:T(8,128)(2,1)S(1)} %collective-permute-done.1.ahead), custom_call_target="tpu_custom_call" | custom-call | tf_op jit(solution)/shard_map/pallas_call | solution.py:31
  113.2 16.3 %all_to_all.56.received = bf16[8,8,2816]{2,1,0:T(8,128)(2,1)S(1)} all-to-all(bf16[8,8,2816]{2,1,0:T(8,128)(2,1)S(1)} %bitcast.24), channel_id=1, replica_groups=mesh['tok'=64,'feat'=8] {'feat'}, dimensions={0} | all-to-all | bytes 720896 | tf_op jit(solution)/shard_map/all_to_all | solution.py:25
  129.5 0.2 shard_map.64
  129.7 17.1 %all_to_all.57 = bf16[8,8,2816]{2,1,0:T(8,128)(2,1)S(1)} all-to-all(bf16[8,8,2816]{2,1,0:T(8,128)(2,1)S(1)} %shard_map.64), channel_id=1, replica_groups=mesh['tok'=64,'feat'=8] {'feat'}, dimensions={0} | all-to-all | bytes 720896 | tf_op jit(solution)/shard_map/all_to_all | solution.py:25
  146.8 1.5 shard_map.65
  148.3 18.7 %all_to_all.58.received = bf16[64,2,1152]{2,1,0:T(2,128)(2,1)S(1)} all-to-all(bf16[64,2,1152]{2,1,0:T(2,128)(2,1)S(1)} %shard_map.65), channel_id=1, replica_groups=mesh['tok'=64,'feat'=8] {'tok'}, dimensions={0} | all-to-all | bytes 589824 | tf_op jit(solution)/shard_map/all_to_all | solution.py:25
  167.1 0.4 shard_map.66
  167.4 17.8 %all_to_all.59.gathered = bf16[64,2,1152]{2,1,0:T(2,128)(2,1)S(1)} all-to-all(bf16[64,2,1152]{2,1,0:T(2,128)(2,1)S(1)} %shard_map.66), channel_id=1, replica_groups=mesh['tok'=64,'feat'=8] {'tok'}, dimensions={0} | all-to-all | bytes 589824 | tf_op jit(solution)/shard_map/all_to_all | solution.py:25
  185.2 2.1 %shard_map.67 = (f32[192,1024]{1,0:T(8,128)}, f32[192,192]{1,0:T(8,128)}, f32[192,192]{1,0:T(8,128)}) custom-call(bf16[64,2,1152]{2,1,0:T(2,128)(2,1)S(1)} %all_to_all.59.gathered, f32[64,1152]{1,0:T(8,128)S(1)} %bitcast.22, bf16[64,2816]{1,0:T(8,128)(2,1)S(1)} %bitcast.20, bf16[128,2176]{1,0:T(8,128)(2,1)S(1)} %bitcast.18), custom_call_target="tpu_custom_call" | custom-call | tf_op jit(solution)/shard_map/pallas_call | solution.py:31
  (3 shorter events, 0.1 us)
Async XLA Ops:
  1.7 13.6 %collective-permute-start.1 = (bf16[128,1024]{1,0:T(8,128)(2,1)S(1)}, bf16[128,1024]{1,0:T(8,128)(2,1)S(1)}, u32[]{:S(2)}, u32[]{:S(2)}) collective-permute-start(bf16[128,1024]{1,0:T(8,128)(2,1)S(1)} %get-tuple-element.9), channel_id=1, source_target_pairs={{8,0},{16,8},{24,16},{32,24},{40,32},{48,40},{56,48},{64,56},{72,6... | collective-permute-start | bytes 786440 | tf_op jit(solution)/shard_map/ppermute | solution.py:266
  4.4 10.9 %collective-permute-start = (bf16[128,1024]{1,0:T(8,128)(2,1)S(1)}, bf16[128,1024]{1,0:T(8,128)(2,1)S(1)}, u32[]{:S(2)}, u32[]{:S(2)}) collective-permute-start(bf16[128,1024]{1,0:T(8,128)(2,1)S(1)} %get-tuple-element.10), channel_id=1, source_target_pairs={{0,8},{8,16},{16,24},{24,32},{32,40},{40,48},{48,56},{56,64},{64,7... | collective-permute-start | bytes 786440 | tf_op jit(solution)/shard_map/ppermute | solution.py:265
  11.7 2.0 %copy-start = (bf16[1728,1024]{1,0:T(8,128)(2,1)S(1)}, bf16[1728,1024]{1,0:T(8,128)(2,1)}, u32[]{:S(2)}) copy-start(bf16[1728,1024]{1,0:T(8,128)(2,1)} %hidden.7) | copy-start | bytes 10616836
  15.3 50.7 %copy-start.1 = (bf16[1728,1024]{1,0:T(8,128)(2,1)S(1)}, bf16[1728,1024]{1,0:T(8,128)(2,1)}, u32[]{:S(2)}) copy-start(bf16[1728,1024]{1,0:T(8,128)(2,1)} %hidden.7) | copy-start | bytes 10616836

commit v11 on v10

--- a/solution.py
+++ b/solution.py
@@ -6,6 +6,7 @@
 from jax import lax
 from jax.experimental import pallas as pl
 from jax.experimental.pallas import tpu as pltpu
+from jax.sharding import Mesh
 from jax.sharding import PartitionSpec as P
 
 LAG = 256
@@ -23,6 +24,12 @@
 
 def exchange(value, axis):
     return lax.all_to_all(value, axis, 0, 0, tiled=True)
+
+
+def gathered_rows(part):
+    part = exchange(part, "chip")
+    part = part.reshape(-1, part.shape[2])
+    return lax.all_gather(part, "core", axis=0, tiled=True)
 
 
 def kernel_call(body, outputs, *operands):
@@ -66,16 +73,16 @@
 
 def project_own(vectors, hidden, out):
     whole = hidden.shape[0] // LANES * LANES
-    out[:, HALO : HALO + whole] = rows_dot(vectors, hidden[:whole]).astype(HALF)
+    out[:, HALO : HALO + whole] = rows_dot(vectors, hidden[:whole])
 
 
 def project_edges(vectors, tail, behind, ahead, out):
     rows = vectors.shape[0]
-    out[:, :HALO] = rows_dot(vectors, behind[...]).astype(HALF)
-    value = rows_dot(vectors, jnp.concatenate([tail, ahead[...]])).astype(HALF)
+    out[:, :HALO] = rows_dot(vectors, behind[...])
+    value = rows_dot(vectors, jnp.concatenate([tail, ahead[...]]))
     spare = padded(value.shape[1]) - value.shape[1]
     if spare:
-        value = jnp.concatenate([value, jnp.zeros((rows, spare), HALF)], axis=1)
+        value = jnp.concatenate([value, jnp.zeros((rows, spare), FLOAT)], axis=1)
     return value
 
 
@@ -92,8 +99,8 @@
     products = exact(both[...], both[...])
     turned = pltpu.roll(products, cols, 1)
     left = lax.broadcasted_iota(jnp.int32, (cols, rows), 1) < cols
-    out[:cols, wide:] = two_terms(jnp.where(left, products[:cols], turned[:cols]))
-    out[cols:, wide:] = two_terms(jnp.where(left, turned[cols:], products[cols:]))
+    out[:cols, wide:] = jnp.where(left, products[:cols], turned[:cols])
+    out[cols:, wide:] = jnp.where(left, turned[cols:], products[cols:])
 
 
 def edge_kernel(whole, both, tail, behind, ahead, start, out):
@@ -101,6 +108,20 @@
     out[:, HALO : HALO + whole] = start[:, HALO : HALO + whole]
     out[:, wide:] = start[:, wide:]
     out[:, HALO + whole : wide] = project_edges(both[...].astype(HALF), tail[...], behind, ahead, out)
+
+
+def chip_known_kernel(wide, received, out):
+    rows = out.shape[1]
+    for i in range(out.shape[0]):
+        total = received[0, i * rows : (i + 1) * rows] + received[1, i * rows : (i + 1) * rows]
+        out[i] = jnp.concatenate([total[:, :wide].astype(HALF), two_terms(total[:, wide:])], axis=1)
+
+
+def chip_found_kernel(wide, received, out):
+    rows = out.shape[1]
+    for i in range(out.shape[0]):
+        total = received[0, i * rows : (i + 1) * rows] + received[1, i * rows : (i + 1) * rows]
+        out[i] = jnp.concatenate([total[:, :wide].astype(HALF), *high_low(total[:, wide:])], axis=1)
 
 
 def known_kernel(wide, received, out):
@@ -157,9 +178,7 @@
     lacks = products[cols : 2 * cols, : 2 * cols] - jnp.concatenate([share, jnp.zeros_like(share)], axis=1)
     own = jnp.concatenate([products[:cols, 2 * cols :], products[2 * cols :, cols : 2 * cols]], axis=1)
     for value in (products[:cols, : 2 * cols], lacks, own):
-        high, low = high_low(value)
-        out[:, at : at + 2 * cols] = high
-        out[:, at + 6 * cols : at + 8 * cols] = low
+        out[:, at : at + 2 * cols] = value
         at += 2 * cols
 
 
@@ -258,7 +277,7 @@
 def local(hidden_states, current_block, directions):
     tokens, features = hidden_states.shape
     cols = current_block.shape[1]
-    feat, tok = lax.axis_size("feat"), lax.axis_size("tok")
+    chips, cores, tok = lax.axis_size("chip"), lax.axis_size("core"), lax.axis_size("tok")
     factor = 0.5 / math.sqrt(tokens * tok - LAG)
     whole, wide = tokens // LANES * LANES, padded(tokens + LAG)
 
@@ -267,13 +286,16 @@
     both = jnp.concatenate([current_block.T, directions.T])
 
     total = wide + 2 * cols
-    flat = shape((2 * cols, total), HALF)
+    whole = tokens // LANES * LANES
+    flat = shape((cores * cols, total), FLOAT)
     part = kernel_call(start_kernel, flat, both, hidden_states)
     part = kernel_call(functools.partial(edge_kernel, whole), flat, both, hidden_states[whole:], behind, ahead, part)
-    blocked = shape((feat, 2 * cols // feat, total), HALF)
-    part = exchange(part.reshape(blocked.shape), "feat")
+    part = exchange(part.reshape(cores, cols, total), "core")
+    blocked = shape((chips, cols // chips, total), HALF)
+    part = kernel_call(functools.partial(chip_known_kernel, wide), blocked, part)
+    part = exchange(part, "chip")
     part = kernel_call(functools.partial(known_kernel, wide), blocked, part)
-    known = exchange(part, "feat").reshape(2 * cols, total)
+    known = gathered_rows(part)
 
     part = kernel_call(first_kernel, shape((cols, features + 2 * cols), FLOAT), known, hidden_states, behind, ahead)
     flat = shape((tok, cols * (features + 2 * cols) // tok), FLOAT)
@@ -282,14 +304,21 @@
     part = exchange(part, "tok")
     first_total = part.reshape(cols, features + 2 * cols)
 
-    total = wide + 12 * cols
     part = kernel_call(
-        functools.partial(residual_kernel, feat), shape((cols, total), HALF), first_total, both, hidden_states, behind, ahead
+        functools.partial(residual_kernel, chips * cores),
+        shape((cols, wide + 6 * cols), FLOAT),
+        first_total,
+        both,
+        hidden_states,
+        behind,
+        ahead,
     )
-    blocked = shape((feat, cols // feat, total), HALF)
-    part = exchange(part.reshape(blocked.shape), "feat")
+    part = exchange(part.reshape(cores, cols // cores, -1), "core")
+    blocked = shape((chips, cols // (cores * chips), wide + 12 * cols), HALF)
+    part = kernel_call(functools.partial(chip_found_kernel, wide), blocked, part)
+    part = exchange(part, "chip")
     part = kernel_call(functools.partial(found_kernel, wide), blocked, part, known)
-    found = exchange(part, "feat").reshape(cols, total)
+    found = gathered_rows(part)
 
     blocked = shape((tok, 2, features + 2 * cols), HALF)
     part = kernel_call(image_kernel, blocked, found, known, hidden_states, behind, ahead)
@@ -309,10 +338,12 @@
 
 
 def solution(mesh):
+    devices = mesh.devices.reshape(mesh.shape["tok"], -1, 2)
+    feat = ("chip", "core")
     return jax.shard_map(
         local,
-        mesh=mesh,
-        in_specs=(P("tok", "feat"), P("feat", None), P("feat", None)),
-        out_specs=(P("feat", None), P(), P()),
+        mesh=Mesh(devices, ("tok",) + feat),
+        in_specs=(P("tok", feat), P(feat, None), P(feat, None)),
+        out_specs=(P(feat, None), P(), P()),
         check_vma=False,
     )

time: 188 us -> 179 us (0.952)
  blocking collectives: 163 us -> 154 us
    all_to_all x8 -> x10, blocking collectives: 163 us -> 150 us  [exchange(): return lax.all_to_all(value, axis, 0, 0, tiled=True)]
    all_gather x0 -> x2, blocking collectives: none -> 4.24 us  [gathered_rows(): return lax.all_gather(part, 'core', axis=0, tiled=True)]
    pallas_call x10 -> x12, Pallas kernels: 10.1 us -> 10.2 us  [kernel_call(): pl.pallas_call(body, out_shape=outputs, in_specs=[spec] * len(operands),...]
  transfers between devices with their start and end apart: 2 -> 2, of which waited for: 0 -> 1; matrix products, arithmetic and copies ran while one was open for 1% -> 1% of each run, Pallas kernels for 1% -> 1%
where the time goes in v11:
time: 179 us; the launch traced here: 178 us
  blocking collectives  154 us (86%)
  Pallas kernels  10.2 us (6%)
  starting transfers between devices  7.95 us (4%)
  local copies, waits for them, and re-layouts  4.7 us (3%)
    all_to_all x10, blocking collectives, exchange(): return lax.all_to_all(value, axis, 0, 0, tiled=True)  150 us
    pallas_call x12, Pallas kernels, kernel_call(): pl.pallas_call(body, out_shape=outputs, in_specs=[spec] * len(operands),...  10.2 us
    ppermute x1, starting transfers between devices, local(): lax.ppermute(hidden_states[tokens - HALO:], 'tok', [(i, i + 1) for i in r...  5.22 us
    all_gather x2, blocking collectives, gathered_rows(): return lax.all_gather(part, 'core', axis=0, tiled=True)  4.24 us
  transfers between devices with their start and end apart: 2, of which 1 were waited for; matrix products, arithmetic and copies ran while one was open for 1% of the time, Pallas kernels for 1%

profile of v11, /device:TPU:6, one launch (start us, length us, event | category | flops | bytes accessed | tf_op | source)
XLA Modules:
  0.0 178.4 jit_solution(14601856809257794966)
XLA Ops:
  0.6 0.0 copy-start.2
  0.6 0.0 copy-start.3
  0.7 1.1 fusion
  1.8 2.7 %collective-permute-start.1 = (bf16[128,1024]{1,0:T(8,128)(2,1)S(1)}, bf16[128,1024]{1,0:T(8,128)(2,1)S(1)}, u32[]{:S(2)}, u32[]{:S(2)}) collective-permute-start(bf16[128,1024]{1,0:T(8,128)(2,1)S(1)} %get-tuple-element.9), channel_id=1, source_target_pairs={{8,0},{16,8},{24,16},{32,24},{40,32},{48,40},{56,48},{64,56},{72,6... | collective-permute-start | bytes 786440 | tf_op jit(solution)/shard_map/ppermute | solution.py:285
  4.5 5.2 %collective-permute-start = (bf16[128,1024]{1,0:T(8,128)(2,1)S(1)}, bf16[128,1024]{1,0:T(8,128)(2,1)S(1)}, u32[]{:S(2)}, u32[]{:S(2)}) collective-permute-start(bf16[128,1024]{1,0:T(8,128)(2,1)S(1)} %get-tuple-element.10), channel_id=1, source_target_pairs={{0,8},{8,16},{16,24},{24,32},{32,40},{40,48},{48,56},{56,64},{64,7... | collective-permute-start | bytes 786440 | tf_op jit(solution)/shard_map/ppermute | solution.py:284
  9.7 0.9 slice.9.tail
  10.7 0.0 copy-done.2
  10.7 0.0 copy-done.3
  10.7 0.0 copy-start
  10.7 2.0 %copy-done = bf16[1728,1024]{1,0:T(8,128)(2,1)S(1)} copy-done((bf16[1728,1024]{1,0:T(8,128)(2,1)S(1)}, bf16[1728,1024]{1,0:T(8,128)(2,1)}, u32[]{:S(2)}) %copy-start) | copy-done | bytes 3538968
  12.7 1.6 shard_map.58.start
  14.4 0.0 collective-permute-done.1.ahead
  14.4 0.6 collective-permute-done.behind
  15.0 0.4 shard_map.59
  15.4 4.6 %all_to_all.62.received = f32[2,64,2176]{2,1,0:T(8,128)S(1)} all-to-all(f32[2,64,2176]{2,1,0:T(8,128)S(1)} %bitcast.15), channel_id=1, replica_groups=mesh['tok'=64,'chip'=4,'core'=2] {'core'}, dimensions={0} | all-to-all | bytes 2228224 | tf_op jit(solution)/shard_map/all_to_all | solution.py:26
  20.1 0.0 copy-start.1
  20.1 0.1 shard_map.60
  20.1 22.8 %all_to_all.63.received = bf16[4,16,2176]{2,1,0:T(8,128)(2,1)S(1)} all-to-all(bf16[4,16,2176]{2,1,0:T(8,128)(2,1)S(1)} %shard_map.60), channel_id=1, replica_groups=mesh['tok'=64,'chip'=4,'core'=2] {'chip'}, dimensions={0} | all-to-all | bytes 557056 | tf_op jit(solution)/shard_map/all_to_all | solution.py:26
  42.9 0.1 shard_map.61
  43.0 12.9 %all_to_all.64 = bf16[4,16,2176]{2,1,0:T(8,128)(2,1)S(1)} all-to-all(bf16[4,16,2176]{2,1,0:T(8,128)(2,1)S(1)} %shard_map.61), channel_id=1, replica_groups=mesh['tok'=64,'chip'=4,'core'=2] {'chip'}, dimensions={0} | all-to-all | bytes 557056 | tf_op jit(solution)/shard_map/all_to_all | solution.py:26
  55.9 2.2 %all_gather.6.known = bf16[128,2176]{1,0:T(8,128)(2,1)S(1)} all-gather(bf16[64,2176]{1,0:T(8,128)(2,1)S(1)} %bitcast.22), channel_id=1, replica_groups=mesh['tok'=64,'chip'=4,'core'=2] {'core'}, dimensions={0}, use_global_device_ids=true | all-gather | bytes 835584 | tf_op jit(solution)/shard_map/all_gather | solution.py:32
  58.1 0.0 copy-done.1
  58.1 1.7 shard_map.62
  59.8 0.3 copy.6
  60.1 24.9 %all_to_all.65 = f32[64,1,1152]{2,1,0:T(1,128)S(1)} all-to-all(f32[64,1,1152]{2,1,0:T(1,128)S(1)} %copy.6), channel_id=1, replica_groups=mesh['tok'=64,'chip'=4,'core'=2] {'tok'}, dimensions={0} | all-to-all | bytes 589824 | tf_op jit(solution)/shard_map/all_to_all | solution.py:26
  85.1 0.3 copy.7
  85.4 17.9 %all_to_all.66 = f32[64,1,1152]{2,1,0:T(1,128)S(1)} all-to-all(f32[64,1,1152]{2,1,0:T(1,128)S(1)} %copy.7), channel_id=1, replica_groups=mesh['tok'=64,'chip'=4,'core'=2] {'tok'}, dimensions={0} | all-to-all | bytes 589824 | tf_op jit(solution)/shard_map/all_to_all | solution.py:26
  103.3 2.2 %shard_map.64 = f32[64,2432]{1,0:T(8,128)S(1)} custom-call(f32[64,1152]{1,0:T(8,128)S(1)} %bitcast.16, f32[128,1024]{1,0:T(8,128)S(1)} %pad_maximum_fusion.both, bf16[1728,1024]{1,0:T(8,128)(2,1)S(1)} %copy-done.1, bf16[128,1024]{1,0:T(8,128)(2,1)S(1)} %collective-permute-done.behind, bf16[128,1024]{1,0:T(8,128)(2,1)S(1)} %collective-permute-done.1.ahead), custom_call_target="tpu_custom_call" | custom-call | tf_op jit(solution)/shard_map/pallas_call | solution.py:38
  105.5 4.2 %all_to_all.67.received = f32[2,32,2432]{2,1,0:T(8,128)S(1)} all-to-all(f32[2,32,2432]{2,1,0:T(8,128)S(1)} %bitcast.18), channel_id=1, replica_groups=mesh['tok'=64,'chip'=4,'core'=2] {'core'}, dimensions={0} | all-to-all | bytes 1245184 | tf_op jit(solution)/shard_map/all_to_all | solution.py:26
  109.8 13.6 %all_to_all.68.received = bf16[4,8,2816]{2,1,0:T(8,128)(2,1)S(1)} all-to-all(bf16[4,8,2816]{2,1,0:T(8,128)(2,1)S(1)} %shard_map.65), channel_id=1, replica_groups=mesh['tok'=64,'chip'=4,'core'=2] {'chip'}, dimensions={0} | all-to-all | bytes 360448 | tf_op jit(solution)/shard_map/all_to_all | solution.py:26
  123.3 0.2 shard_map.66
  123.5 12.0 %all_to_all.69 = bf16[4,8,2816]{2,1,0:T(8,128)(2,1)S(1)} all-to-all(bf16[4,8,2816]{2,1,0:T(8,128)(2,1)S(1)} %shard_map.66), channel_id=1, replica_groups=mesh['tok'=64,'chip'=4,'core'=2] {'chip'}, dimensions={0} | all-to-all | bytes 360448 | tf_op jit(solution)/shard_map/all_to_all | solution.py:26
  135.5 2.1 %all_gather.7.found = bf16[64,2816]{1,0:T(8,128)(2,1)S(1)} all-gather(bf16[32,2816]{1,0:T(8,128)(2,1)S(1)} %bitcast.23), channel_id=1, replica_groups=mesh['tok'=64,'chip'=4,'core'=2] {'core'}, dimensions={0}, use_global_device_ids=true | all-gather | bytes 540672 | tf_op jit(solution)/shard_map/all_gather | solution.py:32
  137.5 1.5 shard_map.67
  139.0 18.9 %all_to_all.70.received = bf16[64,2,1152]{2,1,0:T(2,128)(2,1)S(1)} all-to-all(bf16[64,2,1152]{2,1,0:T(2,128)(2,1)S(1)} %shard_map.67), channel_id=1, replica_groups=mesh['tok'=64,'chip'=4,'core'=2] {'tok'}, dimensions={0} | all-to-all | bytes 589824 | tf_op jit(solution)/shard_map/all_to_all | solution.py:26
  157.9 0.4 shard_map.68
  158.2 18.1 %all_to_all.71.gathered = bf16[64,2,1152]{2,1,0:T(2,128)(2,1)S(1)} all-to-all(bf16[64,2,1152]{2,1,0:T(2,128)(2,1)S(1)} %shard_map.68), channel_id=1, replica_groups=mesh['tok'=64,'chip'=4,'core'=2] {'tok'}, dimensions={0} | all-to-all | bytes 589824 | tf_op jit(solution)/shard_map/all_to_all | solution.py:26
  176.3 2.1 %shard_map.69 = (f32[192,1024]{1,0:T(8,128)}, f32[192,192]{1,0:T(8,128)}, f32[192,192]{1,0:T(8,128)}) custom-call(bf16[64,2,1152]{2,1,0:T(2,128)(2,1)S(1)} %all_to_all.71.gathered, f32[64,1152]{1,0:T(8,128)S(1)} %bitcast.17, bf16[64,2816]{1,0:T(8,128)(2,1)S(1)} %all_gather.7.found, bf16[128,2176]{1,0:T(8,128)(2,1)S(1)} %all_gather.6.known), custom_call_target="tpu_custom_call" | custom-call | tf_op jit(solution)/shard_map/pallas_call | solution.py:38
  (5 shorter events, 0.1 us)
Async XLA Ops:
  0.6 10.0 %copy-start.2 = (f32[1024,64]{0,1:T(8,128)S(1)}, f32[1024,64]{0,1:T(8,128)}, u32[]{:S(2)}) copy-start(f32[1024,64]{0,1:T(8,128)} %param.5) | copy-start | bytes 786436
  0.6 10.0 %copy-start.3 = (f32[1024,64]{0,1:T(8,128)S(1)}, f32[1024,64]{0,1:T(8,128)}, u32[]{:S(2)}) copy-start(f32[1024,64]{0,1:T(8,128)} %param.4) | copy-start | bytes 786436
  1.8 12.6 %collective-permute-start.1 = (bf16[128,1024]{1,0:T(8,128)(2,1)S(1)}, bf16[128,1024]{1,0:T(8,128)(2,1)S(1)}, u32[]{:S(2)}, u32[]{:S(2)}) collective-permute-start(bf16[128,1024]{1,0:T(8,128)(2,1)S(1)} %get-tuple-element.9), channel_id=1, source_target_pairs={{8,0},{16,8},{24,16},{32,24},{40,32},{48,40},{56,48},{64,56},{72,6... | collective-permute-start | bytes 786440 | tf_op jit(solution)/shard_map/ppermute | solution.py:285
  4.5 10.5 %collective-permute-start = (bf16[128,1024]{1,0:T(8,128)(2,1)S(1)}, bf16[128,1024]{1,0:T(8,128)(2,1)S(1)}, u32[]{:S(2)}, u32[]{:S(2)}) collective-permute-start(bf16[128,1024]{1,0:T(8,128)(2,1)S(1)} %get-tuple-element.10), channel_id=1, source_target_pairs={{0,8},{8,16},{16,24},{24,32},{32,40},{40,48},{48,56},{56,64},{64,7... | collective-permute-start | bytes 786440 | tf_op jit(solution)/shard_map/ppermute | solution.py:284
  10.7 2.0 %copy-start = (bf16[1728,1024]{1,0:T(8,128)(2,1)S(1)}, bf16[1728,1024]{1,0:T(8,128)(2,1)}, u32[]{:S(2)}) copy-start(bf16[1728,1024]{1,0:T(8,128)(2,1)} %hidden.7) | copy-start | bytes 10616836
  20.1 38.1 %copy-start.1 = (bf16[1728,1024]{1,0:T(8,128)(2,1)S(1)}, bf16[1728,1024]{1,0:T(8,128)(2,1)}, u32[]{:S(2)}) copy-start(bf16[1728,1024]{1,0:T(8,128)(2,1)} %hidden.7) | copy-start | bytes 10616836

commit v12 on v11

--- a/solution.py
+++ b/solution.py
@@ -71,15 +71,19 @@
     return value[:, :middle] + value[:, middle:]
 
 
+def folded(value, rows):
+    return value if value.shape[0] == rows else value[:rows] + value[rows:]
+
+
 def project_own(vectors, hidden, out):
     whole = hidden.shape[0] // LANES * LANES
-    out[:, HALO : HALO + whole] = rows_dot(vectors, hidden[:whole])
+    out[:, HALO : HALO + whole] = folded(rows_dot(vectors, hidden[:whole]), out.shape[0])
 
 
 def project_edges(vectors, tail, behind, ahead, out):
-    rows = vectors.shape[0]
-    out[:, :HALO] = rows_dot(vectors, behind[...])
-    value = rows_dot(vectors, jnp.concatenate([tail, ahead[...]]))
+    rows = out.shape[0]
+    out[:, :HALO] = folded(rows_dot(vectors, behind[...]), rows)
+    value = folded(rows_dot(vectors, jnp.concatenate([tail, ahead[...]])), rows)
     spare = padded(value.shape[1]) - value.shape[1]
     if spare:
         value = jnp.concatenate([value, jnp.zeros((rows, spare), FLOAT)], axis=1)
@@ -153,15 +157,20 @@
 
 def first_kernel(known, hidden, behind, ahead, out):
     tokens, features = hidden.shape
-    cols = out.shape[0]
+    cols, middle = known.shape[0] // 2, features // 2
     image, cross = lag_image(known[:cols], known[:cols], hidden, behind, ahead)
-    out[:, :features] = image
-    out[:, features:] = jnp.concatenate([cross, lag_cross(known[cols:, : padded(tokens + LAG)], tokens)], axis=1)
-
-
-def spread_kernel(factor, received, out):
-    total = jnp.sum(received[...], axis=0, keepdims=True) * factor
-    out[...] = jnp.broadcast_to(total, out.shape)
+    other = lag_cross(known[cols:, : padded(tokens + LAG)], tokens)
+    upper = jnp.concatenate([image[:, :middle], cross], axis=1)
+    lower = jnp.concatenate([image[:, middle:], other], axis=1)
+    for d in range(out.shape[0]):
+        out[d] = jnp.concatenate([upper[d : d + 1], lower[d : d + 1]]).astype(HALF)
+
+
+def spread_kernel(factor, cols, received, out):
+    total = jnp.sum(received[...].astype(FLOAT), axis=0) * factor
+    middle = total.shape[1] - cols
+    pieces = [total[i : i + 1, part] for part in (slice(0, middle), slice(middle, None)) for i in (0, 1)]
+    out[...] = jnp.broadcast_to(jnp.concatenate(pieces, axis=1), out.shape)
 
 
 def residual_kernel(feat, total, both, hidden, behind, ahead, out):
@@ -170,9 +179,9 @@
     whole, at = tokens // LANES * LANES, padded(tokens + LAG)
     image = total[:, :features]
     residual = (image - times(total[:, features : features + cols], both[:cols])) * SMALL
-    rounded = residual.astype(HALF)
-    project_own(rounded, hidden, out)
-    out[:, HALO + whole : at] = project_edges(rounded, hidden[whole:], behind, ahead, out)
+    terms = jnp.concatenate(high_low(residual))
+    project_own(terms, hidden, out)
+    out[:, HALO + whole : at] = project_edges(terms, hidden[whole:], behind, ahead, out)
     products = exact(jnp.concatenate([residual, image, both[:cols]]), jnp.concatenate([both[...], residual]))
     share = total[:, features : features + cols] * (1.0 / feat)
     lacks = products[cols : 2 * cols, : 2 * cols] - jnp.concatenate([share, jnp.zeros_like(share)], axis=1)
@@ -297,10 +306,11 @@
     part = kernel_call(functools.partial(known_kernel, wide), blocked, part)
     known = gathered_rows(part)
 
-    part = kernel_call(first_kernel, shape((cols, features + 2 * cols), FLOAT), known, hidden_states, behind, ahead)
-    flat = shape((tok, cols * (features + 2 * cols) // tok), FLOAT)
-    part = exchange(part.reshape(flat.shape), "tok")
-    part = kernel_call(functools.partial(spread_kernel, factor), flat, part)
+    blocked = shape((tok, 2, features // 2 + cols), HALF)
+    part = kernel_call(first_kernel, blocked, known, hidden_states, behind, ahead)
+    part = exchange(part, "tok")
+    flat = shape((tok, features + 2 * cols), FLOAT)
+    part = kernel_call(functools.partial(spread_kernel, factor, cols), flat, part)
     part = exchange(part, "tok")
     first_total = part.reshape(cols, features + 2 * cols)
 

time: 179 us -> 176 us (0.983)
  blocking collectives: 154 us -> 151 us
    all_to_all x10, blocking collectives: 150 us -> 147 us  [exchange(): return lax.all_to_all(value, axis, 0, 0, tiled=True)]
where the time goes in v12:
time: 176 us; the launch traced here: 175 us
  blocking collectives  151 us (86%)
  Pallas kernels  10.4 us (6%)
  starting transfers between devices  7.95 us (5%)
  local copies, waits for them, and re-layouts  4.37 us (2%)
    all_to_all x10, blocking collectives, exchange(): return lax.all_to_all(value, axis, 0, 0, tiled=True)  147 us
    pallas_call x12, Pallas kernels, kernel_call(): pl.pallas_call(body, out_shape=outputs, in_specs=[spec] * len(operands),...  10.4 us
    ppermute x1, starting transfers between devices, local(): lax.ppermute(hidden_states[tokens - HALO:], 'tok', [(i, i + 1) for i in r...  5.22 us
    all_gather x2, blocking collectives, gathered_rows(): return lax.all_gather(part, 'core', axis=0, tiled=True)  4.24 us
  transfers between devices with their start and end apart: 2, of which 1 were waited for; matrix products, arithmetic and copies ran while one was open for 1% of the time, Pallas kernels for 1%

profile of v12, /device:TPU:6, one launch (start us, length us, event | category | flops | bytes accessed | tf_op | source)
XLA Modules:
  0.0 175.4 jit_solution(14786645007325910378)
XLA Ops:
  0.6 0.0 copy-start.2
  0.6 0.0 copy-start.3
  0.7 1.1 fusion
  1.8 2.7 %collective-permute-start.1 = (bf16[128,1024]{1,0:T(8,128)(2,1)S(1)}, bf16[128,1024]{1,0:T(8,128)(2,1)S(1)}, u32[]{:S(2)}, u32[]{:S(2)}) collective-permute-start(bf16[128,1024]{1,0:T(8,128)(2,1)S(1)} %get-tuple-element.9), channel_id=1, source_target_pairs={{8,0},{16,8},{24,16},{32,24},{40,32},{48,40},{56,48},{64,56},{72,6... | collective-permute-start | bytes 786440 | tf_op jit(solution)/shard_map/ppermute | solution.py:294
  4.5 5.2 %collective-permute-start = (bf16[128,1024]{1,0:T(8,128)(2,1)S(1)}, bf16[128,1024]{1,0:T(8,128)(2,1)S(1)}, u32[]{:S(2)}, u32[]{:S(2)}) collective-permute-start(bf16[128,1024]{1,0:T(8,128)(2,1)S(1)} %get-tuple-element.10), channel_id=1, source_target_pairs={{0,8},{8,16},{16,24},{24,32},{32,40},{40,48},{48,56},{56,64},{64,7... | collective-permute-start | bytes 786440 | tf_op jit(solution)/shard_map/ppermute | solution.py:293
  9.7 0.9 slice.9.tail
  10.7 0.0 copy-done.2
  10.7 0.0 copy-done.3
  10.7 0.0 copy-start
  10.7 2.0 %copy-done = bf16[1728,1024]{1,0:T(8,128)(2,1)S(1)} copy-done((bf16[1728,1024]{1,0:T(8,128)(2,1)S(1)}, bf16[1728,1024]{1,0:T(8,128)(2,1)}, u32[]{:S(2)}) %copy-start) | copy-done | bytes 3538968
  12.7 1.6 shard_map.58.start
  14.4 0.0 collective-permute-done.1.ahead
  14.4 0.6 collective-permute-done.behind
  15.0 0.4 shard_map.59
  15.4 4.6 %all_to_all.56.received = f32[2,64,2176]{2,1,0:T(8,128)S(1)} all-to-all(f32[2,64,2176]{2,1,0:T(8,128)S(1)} %bitcast.11), channel_id=1, replica_groups=mesh['tok'=64,'chip'=4,'core'=2] {'core'}, dimensions={0} | all-to-all | bytes 2228224 | tf_op jit(solution)/shard_map/all_to_all | solution.py:26
  20.1 0.0 copy-start.1
  20.1 0.1 shard_map.60
  20.1 22.8 %all_to_all.57.received = bf16[4,16,2176]{2,1,0:T(8,128)(2,1)S(1)} all-to-all(bf16[4,16,2176]{2,1,0:T(8,128)(2,1)S(1)} %shard_map.60), channel_id=1, replica_groups=mesh['tok'=64,'chip'=4,'core'=2] {'chip'}, dimensions={0} | all-to-all | bytes 557056 | tf_op jit(solution)/shard_map/all_to_all | solution.py:26
  42.9 0.1 shard_map.61
  43.0 12.9 %all_to_all.58 = bf16[4,16,2176]{2,1,0:T(8,128)(2,1)S(1)} all-to-all(bf16[4,16,2176]{2,1,0:T(8,128)(2,1)S(1)} %shard_map.61), channel_id=1, replica_groups=mesh['tok'=64,'chip'=4,'core'=2] {'chip'}, dimensions={0} | all-to-all | bytes 557056 | tf_op jit(solution)/shard_map/all_to_all | solution.py:26
  55.9 2.2 %all_gather.6.known = bf16[128,2176]{1,0:T(8,128)(2,1)S(1)} all-gather(bf16[64,2176]{1,0:T(8,128)(2,1)S(1)} %bitcast.16), channel_id=1, replica_groups=mesh['tok'=64,'chip'=4,'core'=2] {'core'}, dimensions={0}, use_global_device_ids=true | all-gather | bytes 835584 | tf_op jit(solution)/shard_map/all_gather | solution.py:32
  58.1 0.0 copy-done.1
  58.1 1.7 shard_map.62
  59.8 22.4 %all_to_all.59.received = bf16[64,2,576]{2,1,0:T(2,128)(2,1)S(1)} all-to-all(bf16[64,2,576]{2,1,0:T(2,128)(2,1)S(1)} %shard_map.62), channel_id=1, replica_groups=mesh['tok'=64,'chip'=4,'core'=2] {'tok'}, dimensions={0} | all-to-all | bytes 294912 | tf_op jit(solution)/shard_map/all_to_all | solution.py:26
  82.2 0.2 shard_map.63
  82.4 0.3 copy.6
  82.7 17.7 %all_to_all.60 = f32[64,1,1152]{2,1,0:T(1,128)S(1)} all-to-all(f32[64,1,1152]{2,1,0:T(1,128)S(1)} %copy.6), channel_id=1, replica_groups=mesh['tok'=64,'chip'=4,'core'=2] {'tok'}, dimensions={0} | all-to-all | bytes 589824 | tf_op jit(solution)/shard_map/all_to_all | solution.py:26
  100.5 2.2 %shard_map.64 = f32[64,2432]{1,0:T(8,128)S(1)} custom-call(f32[64,1152]{1,0:T(8,128)S(1)} %bitcast.12, f32[128,1024]{1,0:T(8,128)S(1)} %pad_maximum_fusion.both, bf16[1728,1024]{1,0:T(8,128)(2,1)S(1)} %copy-done.1, bf16[128,1024]{1,0:T(8,128)(2,1)S(1)} %collective-permute-done.behind, bf16[128,1024]{1,0:T(8,128)(2,1)S(1)} %collective-permute-done.1.ahead), custom_call_target="tpu_custom_call" | custom-call | tf_op jit(solution)/shard_map/pallas_call | solution.py:38
  102.7 4.2 %all_to_all.61.received = f32[2,32,2432]{2,1,0:T(8,128)S(1)} all-to-all(f32[2,32,2432]{2,1,0:T(8,128)S(1)} %bitcast.14), channel_id=1, replica_groups=mesh['tok'=64,'chip'=4,'core'=2] {'core'}, dimensions={0} | all-to-all | bytes 1245184 | tf_op jit(solution)/shard_map/all_to_all | solution.py:26
  106.9 13.6 %all_to_all.62.received = bf16[4,8,2816]{2,1,0:T(8,128)(2,1)S(1)} all-to-all(bf16[4,8,2816]{2,1,0:T(8,128)(2,1)S(1)} %shard_map.65), channel_id=1, replica_groups=mesh['tok'=64,'chip'=4,'core'=2] {'chip'}, dimensions={0} | all-to-all | bytes 360448 | tf_op jit(solution)/shard_map/all_to_all | solution.py:26
  120.5 0.2 shard_map.66
  120.7 12.0 %all_to_all.63 = bf16[4,8,2816]{2,1,0:T(8,128)(2,1)S(1)} all-to-all(bf16[4,8,2816]{2,1,0:T(8,128)(2,1)S(1)} %shard_map.66), channel_id=1, replica_groups=mesh['tok'=64,'chip'=4,'core'=2] {'chip'}, dimensions={0} | all-to-all | bytes 360448 | tf_op jit(solution)/shard_map/all_to_all | solution.py:26
  132.6 2.1 %all_gather.7.found = bf16[64,2816]{1,0:T(8,128)(2,1)S(1)} all-gather(bf16[32,2816]{1,0:T(8,128)(2,1)S(1)} %bitcast.17), channel_id=1, replica_groups=mesh['tok'=64,'chip'=4,'core'=2] {'core'}, dimensions={0}, use_global_device_ids=true | all-gather | bytes 540672 | tf_op jit(solution)/shard_map/all_gather | solution.py:32
  134.7 1.5 shard_map.67
  136.2 18.8 %all_to_all.64.received = bf16[64,2,1152]{2,1,0:T(2,128)(2,1)S(1)} all-to-all(bf16[64,2,1152]{2,1,0:T(2,128)(2,1)S(1)} %shard_map.67), channel_id=1, replica_groups=mesh['tok'=64,'chip'=4,'core'=2] {'tok'}, dimensions={0} | all-to-all | bytes 589824 | tf_op jit(solution)/shard_map/all_to_all | solution.py:26
  155.0 0.4 shard_map.68
  155.4 17.9 %all_to_all.65.gathered = bf16[64,2,1152]{2,1,0:T(2,128)(2,1)S(1)} all-to-all(bf16[64,2,1152]{2,1,0:T(2,128)(2,1)S(1)} %shard_map.68), channel_id=1, replica_groups=mesh['tok'=64,'chip'=4,'core'=2] {'tok'}, dimensions={0} | all-to-all | bytes 589824 | tf_op jit(solution)/shard_map/all_to_all | solution.py:26
  173.3 2.1 %shard_map.69 = (f32[192,1024]{1,0:T(8,128)}, f32[192,192]{1,0:T(8,128)}, f32[192,192]{1,0:T(8,128)}) custom-call(bf16[64,2,1152]{2,1,0:T(2,128)(2,1)S(1)} %all_to_all.65.gathered, f32[64,1152]{1,0:T(8,128)S(1)} %bitcast.13, bf16[64,2816]{1,0:T(8,128)(2,1)S(1)} %all_gather.7.found, bf16[128,2176]{1,0:T(8,128)(2,1)S(1)} %all_gather.6.known), custom_call_target="tpu_custom_call" | custom-call | tf_op jit(solution)/shard_map/pallas_call | solution.py:38
  (3 shorter events, 0.1 us)
Async XLA Ops:
  0.6 10.0 %copy-start.2 = (f32[1024,64]{0,1:T(8,128)S(1)}, f32[1024,64]{0,1:T(8,128)}, u32[]{:S(2)}) copy-start(f32[1024,64]{0,1:T(8,128)} %param.5) | copy-start | bytes 786436
  0.6 10.0 %copy-start.3 = (f32[1024,64]{0,1:T(8,128)S(1)}, f32[1024,64]{0,1:T(8,128)}, u32[]{:S(2)}) copy-start(f32[1024,64]{0,1:T(8,128)} %param.4) | copy-start | bytes 786436
  1.8 12.6 %collective-permute-start.1 = (bf16[128,1024]{1,0:T(8,128)(2,1)S(1)}, bf16[128,1024]{1,0:T(8,128)(2,1)S(1)}, u32[]{:S(2)}, u32[]{:S(2)}) collective-permute-start(bf16[128,1024]{1,0:T(8,128)(2,1)S(1)} %get-tuple-element.9), channel_id=1, source_target_pairs={{8,0},{16,8},{24,16},{32,24},{40,32},{48,40},{56,48},{64,56},{72,6... | collective-permute-start | bytes 786440 | tf_op jit(solution)/shard_map/ppermute | solution.py:294
  4.5 10.5 %collective-permute-start = (bf16[128,1024]{1,0:T(8,128)(2,1)S(1)}, bf16[128,1024]{1,0:T(8,128)(2,1)S(1)}, u32[]{:S(2)}, u32[]{:S(2)}) collective-permute-start(bf16[128,1024]{1,0:T(8,128)(2,1)S(1)} %get-tuple-element.10), channel_id=1, source_target_pairs={{0,8},{8,16},{16,24},{24,32},{32,40},{40,48},{48,56},{56,64},{64,7... | collective-permute-start | bytes 786440 | tf_op jit(solution)/shard_map/ppermute | solution.py:293
  10.7 2.0 %copy-start = (bf16[1728,1024]{1,0:T(8,128)(2,1)S(1)}, bf16[1728,1024]{1,0:T(8,128)(2,1)}, u32[]{:S(2)}) copy-start(bf16[1728,1024]{1,0:T(8,128)(2,1)} %hidden.7) | copy-start | bytes 10616836
  20.1 38.1 %copy-start.1 = (bf16[1728,1024]{1,0:T(8,128)(2,1)S(1)}, bf16[1728,1024]{1,0:T(8,128)(2,1)}, u32[]{:S(2)}) copy-start(bf16[1728,1024]{1,0:T(8,128)(2,1)} %hidden.7) | copy-start | bytes 10616836

commit v13 on v12

--- a/solution.py
+++ b/solution.py
@@ -99,7 +99,13 @@
 def start_kernel(both, hidden, out):
     rows = both.shape[0]
     cols, wide = rows // 2, out.shape[1] - rows
-    project_own(both[...].astype(HALF), hidden, out)
+    rounded = both[...].astype(HALF)
+    project_own(rounded, hidden, out)
+    tokens = hidden.shape[0]
+    whole = tokens // LANES * LANES
+    if tokens > whole:
+        last = rows_dot(rounded, hidden[tokens - LANES :])
+        out[:, HALO + whole : HALO + whole + LANES] = pltpu.roll(last, tokens - whole, 1)
     products = exact(both[...], both[...])
     turned = pltpu.roll(products, cols, 1)
     left = lax.broadcasted_iota(jnp.int32, (cols, rows), 1) < cols
@@ -107,11 +113,19 @@
     out[cols:, wide:] = jnp.where(left, turned[cols:], products[cols:])
 
 
-def edge_kernel(whole, both, tail, behind, ahead, start, out):
-    wide = out.shape[1] - both.shape[0]
+def edge_kernel(tokens, both, behind, ahead, start, out):
+    rows, whole = both.shape[0], tokens // LANES * LANES
+    wide, rest = out.shape[1] - rows, tokens - whole
     out[:, HALO : HALO + whole] = start[:, HALO : HALO + whole]
     out[:, wide:] = start[:, wide:]
-    out[:, HALO + whole : wide] = project_edges(both[...].astype(HALF), tail[...], behind, ahead, out)
+    rounded = both[...].astype(HALF)
+    out[:, :HALO] = rows_dot(rounded, behind[...])
+    pieces = [start[:, HALO + whole : HALO + whole + LANES][:, :rest]] if rest else []
+    pieces.append(rows_dot(rounded, ahead[...]))
+    spare = wide - HALO - tokens - HALO
+    if spare:
+        pieces.append(jnp.zeros((rows, spare), FLOAT))
+    out[:, HALO + whole : wide] = jnp.concatenate(pieces, axis=1)
 
 
 def chip_known_kernel(wide, received, out):
@@ -288,17 +302,16 @@
     cols = current_block.shape[1]
     chips, cores, tok = lax.axis_size("chip"), lax.axis_size("core"), lax.axis_size("tok")
     factor = 0.5 / math.sqrt(tokens * tok - LAG)
-    whole, wide = tokens // LANES * LANES, padded(tokens + LAG)
+    wide = padded(tokens + LAG)
 
     behind = lax.ppermute(hidden_states[tokens - HALO :], "tok", [(i, i + 1) for i in range(tok - 1)])
     ahead = lax.ppermute(hidden_states[:HALO], "tok", [(i + 1, i) for i in range(tok - 1)])
     both = jnp.concatenate([current_block.T, directions.T])
 
     total = wide + 2 * cols
-    whole = tokens // LANES * LANES
     flat = shape((cores * cols, total), FLOAT)
     part = kernel_call(start_kernel, flat, both, hidden_states)
-    part = kernel_call(functools.partial(edge_kernel, whole), flat, both, hidden_states[whole:], behind, ahead, part)
+    part = kernel_call(functools.partial(edge_kernel, tokens), flat, both, behind, ahead, part)
     part = exchange(part.reshape(cores, cols, total), "core")
     blocked = shape((chips, cols // chips, total), HALF)
     part = kernel_call(functools.partial(chip_known_kernel, wide), blocked, part)

time: 176 us -> 176 us (level)
  transfers between devices with their start and end apart: 2 -> 2, of which waited for: 1 -> 2; matrix products, arithmetic and copies ran while one was open for 1% -> 0% of each run, Pallas kernels for 1% -> 1%
where the time goes in v13:
time: 176 us; the launch traced here: 175 us
  blocking collectives  151 us (86%)
  Pallas kernels  10.4 us (6%)
  starting transfers between devices  7.95 us (5%)
  local copies, waits for them, and re-layouts  3.45 us (2%)
    all_to_all x10, blocking collectives, exchange(): return lax.all_to_all(value, axis, 0, 0, tiled=True)  147 us
    pallas_call x12, Pallas kernels, kernel_call(): pl.pallas_call(body, out_shape=outputs, in_specs=[spec] * len(operands),...  10.4 us
    ppermute x1, starting transfers between devices, local(): lax.ppermute(hidden_states[tokens - HALO:], 'tok', [(i, i + 1) for i in r...  5.22 us
    all_gather x2, blocking collectives, gathered_rows(): return lax.all_gather(part, 'core', axis=0, tiled=True)  4.24 us
  transfers between devices with their start and end apart: 2, of which 2 were waited for; matrix products, arithmetic and copies ran while one was open for 0% of the time, Pallas kernels for 1%

profile of v13, /device:TPU:6, one launch (start us, length us, event | category | flops | bytes accessed | tf_op | source)
XLA Modules:
  0.0 175.3 jit_solution(1455919047012529765)
XLA Ops:
  0.6 0.0 copy-start.2
  0.6 0.0 copy-start.3
  0.7 1.1 fusion
  1.8 2.7 %collective-permute-start.1 = (bf16[128,1024]{1,0:T(8,128)(2,1)S(1)}, bf16[128,1024]{1,0:T(8,128)(2,1)S(1)}, u32[]{:S(2)}, u32[]{:S(2)}) collective-permute-start(bf16[128,1024]{1,0:T(8,128)(2,1)S(1)} %get-tuple-element.9), channel_id=1, source_target_pairs={{8,0},{16,8},{24,16},{32,24},{40,32},{48,40},{56,48},{64,56},{72,6... | collective-permute-start | bytes 786440 | tf_op jit(solution)/shard_map/ppermute | solution.py:308
  4.5 5.2 %collective-permute-start = (bf16[128,1024]{1,0:T(8,128)(2,1)S(1)}, bf16[128,1024]{1,0:T(8,128)(2,1)S(1)}, u32[]{:S(2)}, u32[]{:S(2)}) collective-permute-start(bf16[128,1024]{1,0:T(8,128)(2,1)S(1)} %get-tuple-element.10), channel_id=1, source_target_pairs={{0,8},{8,16},{16,24},{24,32},{32,40},{40,48},{48,56},{56,64},{64,7... | collective-permute-start | bytes 786440 | tf_op jit(solution)/shard_map/ppermute | solution.py:307
  9.7 0.0 copy-done.2
  9.8 0.0 copy-done.3
  9.8 0.0 copy-start
  9.8 2.0 %copy-done = bf16[1728,1024]{1,0:T(8,128)(2,1)S(1)} copy-done((bf16[1728,1024]{1,0:T(8,128)(2,1)S(1)}, bf16[1728,1024]{1,0:T(8,128)(2,1)}, u32[]{:S(2)}) %copy-start) | copy-done | bytes 3538968
  11.8 1.7 shard_map.58.start
  13.5 0.3 collective-permute-done.1.ahead
  13.8 1.2 collective-permute-done.behind
  15.0 0.4 shard_map.59
  15.4 4.6 %all_to_all.56.received = f32[2,64,2176]{2,1,0:T(8,128)S(1)} all-to-all(f32[2,64,2176]{2,1,0:T(8,128)S(1)} %bitcast.11), channel_id=1, replica_groups=mesh['tok'=64,'chip'=4,'core'=2] {'core'}, dimensions={0} | all-to-all | bytes 2228224 | tf_op jit(solution)/shard_map/all_to_all | solution.py:26
  20.0 0.0 copy-start.1
  20.0 0.1 shard_map.60
  20.1 22.8 %all_to_all.57.received = bf16[4,16,2176]{2,1,0:T(8,128)(2,1)S(1)} all-to-all(bf16[4,16,2176]{2,1,0:T(8,128)(2,1)S(1)} %shard_map.60), channel_id=1, replica_groups=mesh['tok'=64,'chip'=4,'core'=2] {'chip'}, dimensions={0} | all-to-all | bytes 557056 | tf_op jit(solution)/shard_map/all_to_all | solution.py:26
  42.9 0.1 shard_map.61
  43.0 12.9 %all_to_all.58 = bf16[4,16,2176]{2,1,0:T(8,128)(2,1)S(1)} all-to-all(bf16[4,16,2176]{2,1,0:T(8,128)(2,1)S(1)} %shard_map.61), channel_id=1, replica_groups=mesh['tok'=64,'chip'=4,'core'=2] {'chip'}, dimensions={0} | all-to-all | bytes 557056 | tf_op jit(solution)/shard_map/all_to_all | solution.py:26
  55.9 2.2 %all_gather.6.known = bf16[128,2176]{1,0:T(8,128)(2,1)S(1)} all-gather(bf16[64,2176]{1,0:T(8,128)(2,1)S(1)} %bitcast.16), channel_id=1, replica_groups=mesh['tok'=64,'chip'=4,'core'=2] {'core'}, dimensions={0}, use_global_device_ids=true | all-gather | bytes 835584 | tf_op jit(solution)/shard_map/all_gather | solution.py:32
  58.1 0.0 copy-done.1
  58.1 1.7 shard_map.62
  59.7 22.4 %all_to_all.59.received = bf16[64,2,576]{2,1,0:T(2,128)(2,1)S(1)} all-to-all(bf16[64,2,576]{2,1,0:T(2,128)(2,1)S(1)} %shard_map.62), channel_id=1, replica_groups=mesh['tok'=64,'chip'=4,'core'=2] {'tok'}, dimensions={0} | all-to-all | bytes 294912 | tf_op jit(solution)/shard_map/all_to_all | solution.py:26
  82.1 0.2 shard_map.63
  82.4 0.3 copy.6
  82.7 17.7 %all_to_all.60 = f32[64,1,1152]{2,1,0:T(1,128)S(1)} all-to-all(f32[64,1,1152]{2,1,0:T(1,128)S(1)} %copy.6), channel_id=1, replica_groups=mesh['tok'=64,'chip'=4,'core'=2] {'tok'}, dimensions={0} | all-to-all | bytes 589824 | tf_op jit(solution)/shard_map/all_to_all | solution.py:26
  100.4 2.2 %shard_map.64 = f32[64,2432]{1,0:T(8,128)S(1)} custom-call(f32[64,1152]{1,0:T(8,128)S(1)} %bitcast.12, f32[128,1024]{1,0:T(8,128)S(1)} %pad_maximum_fusion.both, bf16[1728,1024]{1,0:T(8,128)(2,1)S(1)} %copy-done.1, bf16[128,1024]{1,0:T(8,128)(2,1)S(1)} %collective-permute-done.behind, bf16[128,1024]{1,0:T(8,128)(2,1)S(1)} %collective-permute-done.1.ahead), custom_call_target="tpu_custom_call" | custom-call | tf_op jit(solution)/shard_map/pallas_call | solution.py:38
  102.6 4.2 %all_to_all.61.received = f32[2,32,2432]{2,1,0:T(8,128)S(1)} all-to-all(f32[2,32,2432]{2,1,0:T(8,128)S(1)} %bitcast.14), channel_id=1, replica_groups=mesh['tok'=64,'chip'=4,'core'=2] {'core'}, dimensions={0} | all-to-all | bytes 1245184 | tf_op jit(solution)/shard_map/all_to_all | solution.py:26
  106.8 13.6 %all_to_all.62.received = bf16[4,8,2816]{2,1,0:T(8,128)(2,1)S(1)} all-to-all(bf16[4,8,2816]{2,1,0:T(8,128)(2,1)S(1)} %shard_map.65), channel_id=1, replica_groups=mesh['tok'=64,'chip'=4,'core'=2] {'chip'}, dimensions={0} | all-to-all | bytes 360448 | tf_op jit(solution)/shard_map/all_to_all | solution.py:26
  120.4 0.2 shard_map.66
  120.6 12.0 %all_to_all.63 = bf16[4,8,2816]{2,1,0:T(8,128)(2,1)S(1)} all-to-all(bf16[4,8,2816]{2,1,0:T(8,128)(2,1)S(1)} %shard_map.66), channel_id=1, replica_groups=mesh['tok'=64,'chip'=4,'core'=2] {'chip'}, dimensions={0} | all-to-all | bytes 360448 | tf_op jit(solution)/shard_map/all_to_all | solution.py:26
  132.6 2.1 %all_gather.7.found = bf16[64,2816]{1,0:T(8,128)(2,1)S(1)} all-gather(bf16[32,2816]{1,0:T(8,128)(2,1)S(1)} %bitcast.17), channel_id=1, replica_groups=mesh['tok'=64,'chip'=4,'core'=2] {'core'}, dimensions={0}, use_global_device_ids=true | all-gather | bytes 540672 | tf_op jit(solution)/shard_map/all_gather | solution.py:32
  134.6 1.5 shard_map.67
  136.1 18.8 %all_to_all.64.received = bf16[64,2,1152]{2,1,0:T(2,128)(2,1)S(1)} all-to-all(bf16[64,2,1152]{2,1,0:T(2,128)(2,1)S(1)} %shard_map.67), channel_id=1, replica_groups=mesh['tok'=64,'chip'=4,'core'=2] {'tok'}, dimensions={0} | all-to-all | bytes 589824 | tf_op jit(solution)/shard_map/all_to_all | solution.py:26
  155.0 0.4 shard_map.68
  155.3 17.9 %all_to_all.65.gathered = bf16[64,2,1152]{2,1,0:T(2,128)(2,1)S(1)} all-to-all(bf16[64,2,1152]{2,1,0:T(2,128)(2,1)S(1)} %shard_map.68), channel_id=1, replica_groups=mesh['tok'=64,'chip'=4,'core'=2] {'tok'}, dimensions={0} | all-to-all | bytes 589824 | tf_op jit(solution)/shard_map/all_to_all | solution.py:26
  173.2 2.1 %shard_map.69 = (f32[192,1024]{1,0:T(8,128)}, f32[192,192]{1,0:T(8,128)}, f32[192,192]{1,0:T(8,128)}) custom-call(bf16[64,2,1152]{2,1,0:T(2,128)(2,1)S(1)} %all_to_all.65.gathered, f32[64,1152]{1,0:T(8,128)S(1)} %bitcast.13, bf16[64,2816]{1,0:T(8,128)(2,1)S(1)} %all_gather.7.found, bf16[128,2176]{1,0:T(8,128)(2,1)S(1)} %all_gather.6.known), custom_call_target="tpu_custom_call" | custom-call | tf_op jit(solution)/shard_map/pallas_call | solution.py:38
  (3 shorter events, 0.1 us)
Async XLA Ops:
  0.6 9.1 %copy-start.2 = (f32[1024,64]{0,1:T(8,128)S(1)}, f32[1024,64]{0,1:T(8,128)}, u32[]{:S(2)}) copy-start(f32[1024,64]{0,1:T(8,128)} %param.5) | copy-start | bytes 786436
  0.6 9.1 %copy-start.3 = (f32[1024,64]{0,1:T(8,128)S(1)}, f32[1024,64]{0,1:T(8,128)}, u32[]{:S(2)}) copy-start(f32[1024,64]{0,1:T(8,128)} %param.4) | copy-start | bytes 786436
  1.8 12.0 %collective-permute-start.1 = (bf16[128,1024]{1,0:T(8,128)(2,1)S(1)}, bf16[128,1024]{1,0:T(8,128)(2,1)S(1)}, u32[]{:S(2)}, u32[]{:S(2)}) collective-permute-start(bf16[128,1024]{1,0:T(8,128)(2,1)S(1)} %get-tuple-element.9), channel_id=1, source_target_pairs={{8,0},{16,8},{24,16},{32,24},{40,32},{48,40},{56,48},{64,56},{72,6... | collective-permute-start | bytes 786440 | tf_op jit(solution)/shard_map/ppermute | solution.py:308
  4.5 10.5 %collective-permute-start = (bf16[128,1024]{1,0:T(8,128)(2,1)S(1)}, bf16[128,1024]{1,0:T(8,128)(2,1)S(1)}, u32[]{:S(2)}, u32[]{:S(2)}) collective-permute-start(bf16[128,1024]{1,0:T(8,128)(2,1)S(1)} %get-tuple-element.10), channel_id=1, source_target_pairs={{0,8},{8,16},{16,24},{24,32},{32,40},{40,48},{48,56},{56,64},{64,7... | collective-permute-start | bytes 786440 | tf_op jit(solution)/shard_map/ppermute | solution.py:307
  9.8 2.0 %copy-start = (bf16[1728,1024]{1,0:T(8,128)(2,1)S(1)}, bf16[1728,1024]{1,0:T(8,128)(2,1)}, u32[]{:S(2)}) copy-start(bf16[1728,1024]{1,0:T(8,128)(2,1)} %hidden.7) | copy-start | bytes 10616836
  20.0 38.1 %copy-start.1 = (bf16[1728,1024]{1,0:T(8,128)(2,1)S(1)}, bf16[1728,1024]{1,0:T(8,128)(2,1)}, u32[]{:S(2)}) copy-start(bf16[1728,1024]{1,0:T(8,128)(2,1)} %hidden.7) | copy-start | bytes 10616836

commit v14 on v13

--- a/solution.py
+++ b/solution.py
@@ -32,7 +32,7 @@
     return lax.all_gather(part, "core", axis=0, tiled=True)
 
 
-def kernel_call(body, outputs, *operands):
+def kernel_call(body, outputs, *operands, reuse=None):
     many = isinstance(outputs, list)
     spec = pl.BlockSpec(memory_space=pltpu.VMEM)
     return pl.pallas_call(
@@ -40,6 +40,7 @@
         out_shape=outputs,
         in_specs=[spec] * len(operands),
         out_specs=[spec] * len(outputs) if many else spec,
+        input_output_aliases={} if reuse is None else {reuse: 0},
         compiler_params=pltpu.CompilerParams(vmem_limit_bytes=16 * 2**20),
     )(*operands)
 
@@ -116,8 +117,6 @@
 def edge_kernel(tokens, both, behind, ahead, start, out):
     rows, whole = both.shape[0], tokens // LANES * LANES
     wide, rest = out.shape[1] - rows, tokens - whole
-    out[:, HALO : HALO + whole] = start[:, HALO : HALO + whole]
-    out[:, wide:] = start[:, wide:]
     rounded = both[...].astype(HALF)
     out[:, :HALO] = rows_dot(rounded, behind[...])
     pieces = [start[:, HALO + whole : HALO + whole + LANES][:, :rest]] if rest else []
@@ -311,7 +310,7 @@
     total = wide + 2 * cols
     flat = shape((cores * cols, total), FLOAT)
     part = kernel_call(start_kernel, flat, both, hidden_states)
-    part = kernel_call(functools.partial(edge_kernel, tokens), flat, both, behind, ahead, part)
+    part = kernel_call(functools.partial(edge_kernel, tokens), flat, both, behind, ahead, part, reuse=3)
     part = exchange(part.reshape(cores, cols, total), "core")
     blocked = shape((chips, cols // chips, total), HALF)
     part = kernel_call(functools.partial(chip_known_kernel, wide), blocked, part)

time: 176 us -> 176 us (level)
  no operation moved by 1% of the time
where the time goes in v14:
time: 176 us; the launch traced here: 175 us
  blocking collectives  151 us (86%)
  Pallas kernels  10.4 us (6%)
  starting transfers between devices  7.95 us (5%)
  local copies, waits for them, and re-layouts  3.45 us (2%)
    all_to_all x10, blocking collectives, exchange(): return lax.all_to_all(value, axis, 0, 0, tiled=True)  147 us
    pallas_call x12, Pallas kernels, kernel_call(): pl.pallas_call(body, out_shape=outputs, in_specs=[spec] * len(operands),...  10.4 us
    ppermute x1, starting transfers between devices, local(): lax.ppermute(hidden_states[tokens - HALO:], 'tok', [(i, i + 1) for i in r...  5.22 us
    all_gather x2, blocking collectives, gathered_rows(): return lax.all_gather(part, 'core', axis=0, tiled=True)  4.24 us
  transfers between devices with their start and end apart: 2, of which 2 were waited for; matrix products, arithmetic and copies ran while one was open for 0% of the time, Pallas kernels for 1%

profile of v14, /device:TPU:6, one launch (start us, length us, event | category | flops | bytes accessed | tf_op | source)
XLA Modules:
  0.0 175.3 jit_solution(5793930231865095984)
XLA Ops:
  0.6 0.0 copy-start.2
  0.6 0.0 copy-start.3
  0.7 1.1 fusion
  1.8 2.7 %collective-permute-start.1 = (bf16[128,1024]{1,0:T(8,128)(2,1)S(1)}, bf16[128,1024]{1,0:T(8,128)(2,1)S(1)}, u32[]{:S(2)}, u32[]{:S(2)}) collective-permute-start(bf16[128,1024]{1,0:T(8,128)(2,1)S(1)} %get-tuple-element.9), channel_id=1, source_target_pairs={{8,0},{16,8},{24,16},{32,24},{40,32},{48,40},{56,48},{64,56},{72,6... | collective-permute-start | bytes 786440 | tf_op jit(solution)/shard_map/ppermute | solution.py:307
  4.5 5.2 %collective-permute-start = (bf16[128,1024]{1,0:T(8,128)(2,1)S(1)}, bf16[128,1024]{1,0:T(8,128)(2,1)S(1)}, u32[]{:S(2)}, u32[]{:S(2)}) collective-permute-start(bf16[128,1024]{1,0:T(8,128)(2,1)S(1)} %get-tuple-element.10), channel_id=1, source_target_pairs={{0,8},{8,16},{16,24},{24,32},{32,40},{40,48},{48,56},{56,64},{64,7... | collective-permute-start | bytes 786440 | tf_op jit(solution)/shard_map/ppermute | solution.py:306
  9.7 0.0 copy-done.2
  9.8 0.0 copy-done.3
  9.8 0.0 copy-start
  9.8 2.0 %copy-done = bf16[1728,1024]{1,0:T(8,128)(2,1)S(1)} copy-done((bf16[1728,1024]{1,0:T(8,128)(2,1)S(1)}, bf16[1728,1024]{1,0:T(8,128)(2,1)}, u32[]{:S(2)}) %copy-start) | copy-done | bytes 3538968
  11.8 1.7 shard_map.58.start
  13.5 0.3 collective-permute-done.1.ahead
  13.8 1.2 collective-permute-done.behind
  15.0 0.4 shard_map.59
  15.4 4.6 %all_to_all.56.received = f32[2,64,2176]{2,1,0:T(8,128)S(1)} all-to-all(f32[2,64,2176]{2,1,0:T(8,128)S(1)} %bitcast.11), channel_id=1, replica_groups=mesh['tok'=64,'chip'=4,'core'=2] {'core'}, dimensions={0} | all-to-all | bytes 2228224 | tf_op jit(solution)/shard_map/all_to_all | solution.py:26
  20.0 0.0 copy-start.1
  20.0 0.1 shard_map.60
  20.1 22.8 %all_to_all.57.received = bf16[4,16,2176]{2,1,0:T(8,128)(2,1)S(1)} all-to-all(bf16[4,16,2176]{2,1,0:T(8,128)(2,1)S(1)} %shard_map.60), channel_id=1, replica_groups=mesh['tok'=64,'chip'=4,'core'=2] {'chip'}, dimensions={0} | all-to-all | bytes 557056 | tf_op jit(solution)/shard_map/all_to_all | solution.py:26
  42.9 0.1 shard_map.61
  43.0 12.9 %all_to_all.58 = bf16[4,16,2176]{2,1,0:T(8,128)(2,1)S(1)} all-to-all(bf16[4,16,2176]{2,1,0:T(8,128)(2,1)S(1)} %shard_map.61), channel_id=1, replica_groups=mesh['tok'=64,'chip'=4,'core'=2] {'chip'}, dimensions={0} | all-to-all | bytes 557056 | tf_op jit(solution)/shard_map/all_to_all | solution.py:26
  55.9 2.2 %all_gather.6.known = bf16[128,2176]{1,0:T(8,128)(2,1)S(1)} all-gather(bf16[64,2176]{1,0:T(8,128)(2,1)S(1)} %bitcast.16), channel_id=1, replica_groups=mesh['tok'=64,'chip'=4,'core'=2] {'core'}, dimensions={0}, use_global_device_ids=true | all-gather | bytes 835584 | tf_op jit(solution)/shard_map/all_gather | solution.py:32
  58.1 0.0 copy-done.1
  58.1 1.7 shard_map.62
  59.8 22.4 %all_to_all.59.received = bf16[64,2,576]{2,1,0:T(2,128)(2,1)S(1)} all-to-all(bf16[64,2,576]{2,1,0:T(2,128)(2,1)S(1)} %shard_map.62), channel_id=1, replica_groups=mesh['tok'=64,'chip'=4,'core'=2] {'tok'}, dimensions={0} | all-to-all | bytes 294912 | tf_op jit(solution)/shard_map/all_to_all | solution.py:26
  82.1 0.2 shard_map.63
  82.4 0.3 copy.7
  82.7 17.7 %all_to_all.60 = f32[64,1,1152]{2,1,0:T(1,128)S(1)} all-to-all(f32[64,1,1152]{2,1,0:T(1,128)S(1)} %copy.7), channel_id=1, replica_groups=mesh['tok'=64,'chip'=4,'core'=2] {'tok'}, dimensions={0} | all-to-all | bytes 589824 | tf_op jit(solution)/shard_map/all_to_all | solution.py:26
  100.4 2.2 %shard_map.64 = f32[64,2432]{1,0:T(8,128)S(1)} custom-call(f32[64,1152]{1,0:T(8,128)S(1)} %bitcast.12, f32[128,1024]{1,0:T(8,128)S(1)} %pad_maximum_fusion.both, bf16[1728,1024]{1,0:T(8,128)(2,1)S(1)} %copy-done.1, bf16[128,1024]{1,0:T(8,128)(2,1)S(1)} %collective-permute-done.behind, bf16[128,1024]{1,0:T(8,128)(2,1)S(1)} %collective-permute-done.1.ahead), custom_call_target="tpu_custom_call" | custom-call | tf_op jit(solution)/shard_map/pallas_call | solution.py:38
  102.6 4.2 %all_to_all.61.received = f32[2,32,2432]{2,1,0:T(8,128)S(1)} all-to-all(f32[2,32,2432]{2,1,0:T(8,128)S(1)} %bitcast.14), channel_id=1, replica_groups=mesh['tok'=64,'chip'=4,'core'=2] {'core'}, dimensions={0} | all-to-all | bytes 1245184 | tf_op jit(solution)/shard_map/all_to_all | solution.py:26
  106.9 13.6 %all_to_all.62.received = bf16[4,8,2816]{2,1,0:T(8,128)(2,1)S(1)} all-to-all(bf16[4,8,2816]{2,1,0:T(8,128)(2,1)S(1)} %shard_map.65), channel_id=1, replica_groups=mesh['tok'=64,'chip'=4,'core'=2] {'chip'}, dimensions={0} | all-to-all | bytes 360448 | tf_op jit(solution)/shard_map/all_to_all | solution.py:26
  120.5 0.2 shard_map.66
  120.6 12.0 %all_to_all.63 = bf16[4,8,2816]{2,1,0:T(8,128)(2,1)S(1)} all-to-all(bf16[4,8,2816]{2,1,0:T(8,128)(2,1)S(1)} %shard_map.66), channel_id=1, replica_groups=mesh['tok'=64,'chip'=4,'core'=2] {'chip'}, dimensions={0} | all-to-all | bytes 360448 | tf_op jit(solution)/shard_map/all_to_all | solution.py:26
  132.6 2.1 %all_gather.7.found = bf16[64,2816]{1,0:T(8,128)(2,1)S(1)} all-gather(bf16[32,2816]{1,0:T(8,128)(2,1)S(1)} %bitcast.17), channel_id=1, replica_groups=mesh['tok'=64,'chip'=4,'core'=2] {'core'}, dimensions={0}, use_global_device_ids=true | all-gather | bytes 540672 | tf_op jit(solution)/shard_map/all_gather | solution.py:32
  134.7 1.5 shard_map.67
  136.1 18.8 %all_to_all.64.received = bf16[64,2,1152]{2,1,0:T(2,128)(2,1)S(1)} all-to-all(bf16[64,2,1152]{2,1,0:T(2,128)(2,1)S(1)} %shard_map.67), channel_id=1, replica_groups=mesh['tok'=64,'chip'=4,'core'=2] {'tok'}, dimensions={0} | all-to-all | bytes 589824 | tf_op jit(solution)/shard_map/all_to_all | solution.py:26
  155.0 0.4 shard_map.68
  155.3 17.9 %all_to_all.65.gathered = bf16[64,2,1152]{2,1,0:T(2,128)(2,1)S(1)} all-to-all(bf16[64,2,1152]{2,1,0:T(2,128)(2,1)S(1)} %shard_map.68), channel_id=1, replica_groups=mesh['tok'=64,'chip'=4,'core'=2] {'tok'}, dimensions={0} | all-to-all | bytes 589824 | tf_op jit(solution)/shard_map/all_to_all | solution.py:26
  173.2 2.1 %shard_map.69 = (f32[192,1024]{1,0:T(8,128)}, f32[192,192]{1,0:T(8,128)}, f32[192,192]{1,0:T(8,128)}) custom-call(bf16[64,2,1152]{2,1,0:T(2,128)(2,1)S(1)} %all_to_all.65.gathered, f32[64,1152]{1,0:T(8,128)S(1)} %bitcast.13, bf16[64,2816]{1,0:T(8,128)(2,1)S(1)} %all_gather.7.found, bf16[128,2176]{1,0:T(8,128)(2,1)S(1)} %all_gather.6.known), custom_call_target="tpu_custom_call" | custom-call | tf_op jit(solution)/shard_map/pallas_call | solution.py:38
  (3 shorter events, 0.1 us)
Async XLA Ops:
  0.6 9.1 %copy-start.2 = (f32[1024,64]{0,1:T(8,128)S(1)}, f32[1024,64]{0,1:T(8,128)}, u32[]{:S(2)}) copy-start(f32[1024,64]{0,1:T(8,128)} %param.5) | copy-start | bytes 786436
  0.6 9.1 %copy-start.3 = (f32[1024,64]{0,1:T(8,128)S(1)}, f32[1024,64]{0,1:T(8,128)}, u32[]{:S(2)}) copy-start(f32[1024,64]{0,1:T(8,128)} %param.4) | copy-start | bytes 786436
  1.8 12.0 %collective-permute-start.1 = (bf16[128,1024]{1,0:T(8,128)(2,1)S(1)}, bf16[128,1024]{1,0:T(8,128)(2,1)S(1)}, u32[]{:S(2)}, u32[]{:S(2)}) collective-permute-start(bf16[128,1024]{1,0:T(8,128)(2,1)S(1)} %get-tuple-element.9), channel_id=1, source_target_pairs={{8,0},{16,8},{24,16},{32,24},{40,32},{48,40},{56,48},{64,56},{72,6... | collective-permute-start | bytes 786440 | tf_op jit(solution)/shard_map/ppermute | solution.py:307
  4.5 10.5 %collective-permute-start = (bf16[128,1024]{1,0:T(8,128)(2,1)S(1)}, bf16[128,1024]{1,0:T(8,128)(2,1)S(1)}, u32[]{:S(2)}, u32[]{:S(2)}) collective-permute-start(bf16[128,1024]{1,0:T(8,128)(2,1)S(1)} %get-tuple-element.10), channel_id=1, source_target_pairs={{0,8},{8,16},{16,24},{24,32},{32,40},{40,48},{48,56},{56,64},{64,7... | collective-permute-start | bytes 786440 | tf_op jit(solution)/shard_map/ppermute | solution.py:306
  9.8 2.0 %copy-start = (bf16[1728,1024]{1,0:T(8,128)(2,1)S(1)}, bf16[1728,1024]{1,0:T(8,128)(2,1)}, u32[]{:S(2)}) copy-start(bf16[1728,1024]{1,0:T(8,128)(2,1)} %hidden.7) | copy-start | bytes 10616836
  20.0 38.1 %copy-start.1 = (bf16[1728,1024]{1,0:T(8,128)(2,1)S(1)}, bf16[1728,1024]{1,0:T(8,128)(2,1)}, u32[]{:S(2)}) copy-start(bf16[1728,1024]{1,0:T(8,128)(2,1)} %hidden.7) | copy-start | bytes 10616836
